TPU v7x, 32 devices: a whole 2x2x4 slice. The times are simulated.
32 devices in a mesh: row: 8 (over z, x), col: 4 (over y, core).
Axes of the slice: x: 2, y: 2, z: 4, core: 2. Of those that a mesh axis runs over, the one named last changes fastest.
Arguments:
- x_window: bfloat16 [3, 2048, 512], P(None, 'row', 'col'), may hold values from -6 to 6
- y_window: float32 [3, 2048], P(None, 'row'), may hold values from -6 to 6
- block_order: int32 [3], replicated, may hold values from 0 to 2, each once
- diag_inverse: bfloat16 [3, 2048, 2048], P(None, 'row'), may hold values from -0.5 to 1.5, as said below
- panel_window: bfloat16 [3, 2048, 2048], P(None, 'row', 'col'), may hold values from -0.078125 to 0.078125
- panel_trail: bfloat16 [1024, 3, 2048], P('row', None, 'col'), may hold values from -0.078125 to 0.078125
- x_trail: bfloat16 [1024, 512], P('row', 'col'), may hold values from -6 to 6
- y_trail: float32 [1024], P('row'), may hold values from -6 to 6
Outputs:
- whitened: bfloat16 [3, 2048, 512], P(None, 'row', 'col')
- white_resp: bfloat16 [3, 2048], P(None, 'row')
- trail_rhs: float32 [1024, 512], P('row', 'col')
- trail_resp: float32 [1024], P('row')
- normal_part: float32 [512, 512], P('row')
- right_part: float32 [512], P('row')
Inputs may be any that keep to these rules, and one draw needn't show every extreme that they name: Each diag_inverse[s] is lower triangular with a positive diagonal.
All inputs are finite; a program needn't handle non-finite values.
Results may differ from a plain program's by a relative error of at most 0.014.
Values may be sent and summed in bfloat16 or wider, within the bound.
No kernel may reach another device: no remote copies, remote signals or barrier semaphores. Data moves between devices by JAX's collectives and lax.ppermute only.
A program may use at most 64 MiB of HBM per device.

v0:
```python
import jax
import jax.numpy as jnp
from jax import lax
from jax.sharding import PartitionSpec as P


def shards(
    x_window, y_window, block_order, diag_inverse, panel_window, panel_trail, x_trail, y_trail
):
    steps = x_window.shape[0]
    own_rows = x_window.shape[1]
    own_cols = x_window.shape[2]
    width = panel_window.shape[2]
    block_rows = own_rows * lax.axis_size("row")
    full_cols = own_cols * lax.axis_size("col")
    normal_rows = full_cols // lax.axis_size("row")
    col_start = lax.axis_index("col") * width
    normal_start = lax.axis_index("row") * normal_rows
    trail_rows = x_trail.shape[0]
    solved_cols = []
    solved_resp = []
    out_tiles = []
    out_resp = []
    trail_total = jnp.zeros((trail_rows, full_cols), jnp.float32)
    trail_resp_total = jnp.zeros((trail_rows,), jnp.float32)
    gram = jnp.zeros((normal_rows, full_cols), jnp.float32)
    right = jnp.zeros((normal_rows,), jnp.float32)
    for s in range(steps):
        stored = block_order[s]
        pending = lax.dynamic_index_in_dim(x_window, stored, 0, keepdims=False).astype(jnp.float32)
        pending_resp = lax.dynamic_index_in_dim(y_window, stored, 0, keepdims=False)
        if s > 0:
            first = s * (s - 1) // 2
            factors = panel_window[first : first + s]
            earlier = jnp.stack(solved_cols)
            earlier_resp = jnp.stack(solved_resp)
            update = jnp.einsum("trw,twp->rp", factors, earlier, preferred_element_type=jnp.float32)
            update_resp = jnp.einsum(
                "trw,tw->r", factors, earlier_resp, preferred_element_type=jnp.float32
            )
            pending = pending - lax.psum_scatter(update, "col", scatter_dimension=1, tiled=True)
            pending_resp = pending_resp - lax.psum(update_resp, "col")
        residual = pending.astype(jnp.bfloat16)
        resid_resp = pending_resp.astype(jnp.bfloat16)
        whole, whole_resp = (
            lax.all_gather(residual, "row", axis=0, tiled=True),
            lax.all_gather(resid_resp, "row", axis=0, tiled=True),
        )
        inverse = diag_inverse[s]
        tile = jnp.dot(inverse, whole, preferred_element_type=jnp.float32).astype(jnp.bfloat16)
        tile_resp = jnp.dot(inverse, whole_resp, preferred_element_type=jnp.float32).astype(
            jnp.bfloat16
        )
        out_tiles.append(tile)
        out_resp.append(tile_resp)
        all_rows, all_resp = (
            lax.all_gather(tile, "row", axis=0, tiled=True),
            lax.all_gather(tile_resp, "row", axis=0, tiled=True),
        )
        mine = lax.all_to_all(all_rows, "col", split_axis=0, concat_axis=1, tiled=True)
        mine_resp = lax.dynamic_slice_in_dim(all_resp, col_start, width, 0)
        solved_cols.append(mine)
        solved_resp.append(mine_resp)
        factor_rows = panel_trail[:, s, :]
        trail_total = trail_total + jnp.dot(factor_rows, mine, preferred_element_type=jnp.float32)
        trail_resp_total = trail_resp_total + jnp.dot(
            factor_rows, mine_resp, preferred_element_type=jnp.float32
        )
        slab = lax.dynamic_slice_in_dim(mine, normal_start, normal_rows, 1)
        gram = gram + lax.dot_general(
            slab, mine, (((0,), (0,)), ((), ())), preferred_element_type=jnp.float32
        )
        right = right + lax.dot_general(
            slab, mine_resp, (((0,), (0,)), ((), ())), preferred_element_type=jnp.float32
        )
    share = lax.psum_scatter(
        trail_total.astype(jnp.bfloat16), "col", scatter_dimension=1, tiled=True
    ).astype(jnp.float32)
    trail_rhs = x_trail.astype(jnp.float32) - share
    gram, right, resp_sum = lax.psum((gram, right, trail_resp_total), "col")
    trail_resp = y_trail - resp_sum
    scale = 1.0 / (steps * block_rows)
    whitened = jnp.stack(out_tiles)
    white_resp = jnp.stack(out_resp)
    return (whitened, white_resp, trail_rhs, trail_resp, gram * scale, right * scale)


def solution(mesh):
    in_specs = (
        P(None, "row", "col"),
        P(None, "row"),
        P(),
        P(None, "row", None),
        P(None, "row", "col"),
        P("row", None, "col"),
        P("row", "col"),
        P("row"),
    )
    out_specs = (
        P(None, "row", "col"),
        P(None, "row"),
        P("row", "col"),
        P("row"),
        P("row", None),
        P("row"),
    )
    return jax.shard_map(shards, mesh=mesh, in_specs=in_specs, out_specs=out_specs, check_vma=False)
```

profile of v0, /device:TPU:0, one launch (start us, length us, event | category | flops | bytes accessed | tf_op | source)
XLA Modules:
  0.0 446.1 jit_solution(9087911912187497106)
XLA Ops:
  7.2 1.4 fusion.65
  14.4 0.9 constant_dynamic-slice_fusion.3
  15.3 33.2 %all-gather = bf16[1,2048,128]{2,1,0:T(8,128)(2,1)S(1)} all-gather(bf16[1,256,128]{2,1,0:T(8,128)(2,1)S(1)} %get-tuple-element.28), channel_id=2, replica_groups=mesh['row'=8,'col'=4] {'row'}, dimensions={1}, use_global_device_ids=true | all-gather | bytes 589824 | tf_op jit(solution)/shard_map/all_gather | solution.py:46
  48.5 1.7 convolution_convert_fusion.2
  50.2 31.2 %all_gather.37 = bf16[2048,128]{0,1:T(8,128)(2,1)S(1)} all-gather(bf16[256,128]{0,1:T(8,128)(2,1)S(1)} %bitcast.162), channel_id=1, replica_groups=mesh['row'=8,'col'=4] {'row'}, dimensions={0}, use_global_device_ids=true | all-gather | bytes 589824 | tf_op jit(solution)/shard_map/all_gather | solution.py:57
  81.4 0.8 copy.47
  82.3 3.5 all-to-all-start
  85.8 20.8 %all-gather.1 = bf16[1,2048]{1,0:T(2,128)(2,1)S(1)} all-gather(bf16[1,256]{1,0:T(2,128)(2,1)S(1)} %fusion.63), channel_id=3, replica_groups=mesh['row'=8,'col'=4] {'row'}, dimensions={1}, use_global_device_ids=true | all-gather | bytes 4608 | tf_op jit(solution)/shard_map/all_gather | solution.py:47
  106.6 1.6 fusion.15
  108.3 16.3 %all-gather.2 = bf16[8,1,256]{2,1,0:T(2,128)(2,1)S(1)} all-gather(bf16[1,1,256]{2,1,0:T(2,128)(2,1)S(1)} %reshape.44), channel_id=1, replica_groups=mesh['row'=8,'col'=4] {'row'}, dimensions={0}, use_global_device_ids=true | all-gather | bytes 4608 | tf_op jit(solution)/shard_map/all_gather | solution.py:58
  124.6 0.1 dynamic_slice.43
  124.7 0.1 fusion.28
  124.9 5.7 %psum.35 = f32[256]{0:T(256)S(1)} all-reduce(f32[256]{0:T(256)S(1)} %bitcast.177), channel_id=1, replica_groups=mesh['row'=8,'col'=4] {'col'}, use_global_device_ids=true, to_apply=%region_2.3 | all-reduce | flops 256 | bytes 2048 | tf_op jit(solution)/shard_map/psum | solution.py:42
  130.5 1.1 convolution_bitcast_fusion.1
  131.7 18.3 %all-gather.3 = bf16[8,1,256]{2,1,0:T(2,128)(2,1)S(1)} all-gather(bf16[1,1,256]{2,1,0:T(2,128)(2,1)S(1)} %reshape.46), channel_id=1, replica_groups=mesh['row'=8,'col'=4] {'row'}, dimensions={0}, use_global_device_ids=true | all-gather | bytes 4608 | tf_op jit(solution)/shard_map/all_gather | solution.py:47
  150.0 1.6 fusion.12
  151.7 16.3 %all-gather.4 = bf16[8,1,256]{2,1,0:T(2,128)(2,1)S(1)} all-gather(bf16[1,1,256]{2,1,0:T(2,128)(2,1)S(1)} %reshape.48), channel_id=1, replica_groups=mesh['row'=8,'col'=4] {'row'}, dimensions={0}, use_global_device_ids=true | all-gather | bytes 4608 | tf_op jit(solution)/shard_map/all_gather | solution.py:58
  168.0 0.1 dynamic_slice.45
  168.1 0.2 fusion.25
  168.3 5.7 %psum.36 = f32[256]{0:T(256)S(1)} all-reduce(f32[256]{0:T(256)S(1)} %bitcast.176), channel_id=1, replica_groups=mesh['row'=8,'col'=4] {'col'}, use_global_device_ids=true, to_apply=%region_3.4 | all-reduce | flops 256 | bytes 2048 | tf_op jit(solution)/shard_map/psum | solution.py:42
  174.0 0.1 copy.32
  174.1 18.3 %all-gather.5 = bf16[8,1,256]{2,1,0:T(2,128)(2,1)S(1)} all-gather(bf16[1,1,256]{2,1,0:T(2,128)(2,1)S(1)} %reshape.50), channel_id=1, replica_groups=mesh['row'=8,'col'=4] {'row'}, dimensions={0}, use_global_device_ids=true | all-gather | bytes 4608 | tf_op jit(solution)/shard_map/all_gather | solution.py:47
  192.4 0.9 fusion.34
  193.4 31.7 %all_gather.38 = bf16[2048,128]{0,1:T(8,128)(2,1)S(1)} all-gather(bf16[256,128]{0,1:T(8,128)(2,1)S(1)} %fusion.34), channel_id=1, replica_groups=mesh['row'=8,'col'=4] {'row'}, dimensions={0}, use_global_device_ids=true | all-gather | bytes 589824 | tf_op jit(solution)/shard_map/all_gather | solution.py:46
  225.1 1.7 convolution_convert_fusion.1
  226.8 31.3 %all_gather.39 = bf16[2048,128]{0,1:T(8,128)(2,1)S(1)} all-gather(bf16[256,128]{0,1:T(8,128)(2,1)S(1)} %bitcast.164), channel_id=1, replica_groups=mesh['row'=8,'col'=4] {'row'}, dimensions={0}, use_global_device_ids=true | all-gather | bytes 589824 | tf_op jit(solution)/shard_map/all_gather | solution.py:57
  258.1 0.8 copy.46
  258.9 3.6 all-to-all-start.1
  262.5 1.6 fusion.9
  264.1 16.5 %all-gather.6 = bf16[8,1,256]{2,1,0:T(2,128)(2,1)S(1)} all-gather(bf16[1,1,256]{2,1,0:T(2,128)(2,1)S(1)} %reshape.52), channel_id=1, replica_groups=mesh['row'=8,'col'=4] {'row'}, dimensions={0}, use_global_device_ids=true | all-gather | bytes 4608 | tf_op jit(solution)/shard_map/all_gather | solution.py:58
  280.6 0.1 dynamic_slice.46
  280.7 0.1 copy.27
  280.9 0.1 copy.33
  281.0 0.1 convolution_bitcast_fusion.6
  281.1 0.1 convolution_bitcast_fusion.5
  281.3 1.3 convolution_bitcast_fusion
  282.6 0.6 pad_maximum_fusion.1
  283.2 0.1 fusion.3
  283.3 0.3 fusion.53
  283.6 0.3 fusion.40
  283.9 0.3 convolution_add_fusion.3
  284.2 19.5 %reduce-scatter.6.cloned.1.call-done = f32[256,128]{0,1:T(8,128)} async-done(((f32[256,512]{0,1:T(8,128)}), f32[256,128]{0,1:T(8,128)}) %reduce-scatter.6.cloned.1.call-update) | async-done | bytes 131088 | tf_op jit(solution)/shard_map/reduce_scatter | solution.py:41
  303.7 0.9 fusion.33
  304.6 31.5 %all_gather.40 = bf16[2048,128]{0,1:T(8,128)(2,1)S(1)} all-gather(bf16[256,128]{0,1:T(8,128)(2,1)S(1)} %fusion.33), channel_id=1, replica_groups=mesh['row'=8,'col'=4] {'row'}, dimensions={0}, use_global_device_ids=true | all-gather | bytes 589824 | tf_op jit(solution)/shard_map/all_gather | solution.py:46
  336.0 1.7 convolution_convert_fusion
  337.8 31.2 %all_gather.46 = bf16[2048,128]{0,1:T(8,128)(2,1)S(1)} all-gather(bf16[256,128]{0,1:T(8,128)(2,1)S(1)} %bitcast.166), channel_id=1, replica_groups=mesh['row'=8,'col'=4] {'row'}, dimensions={0}, use_global_device_ids=true | all-gather | bytes 589824 | tf_op jit(solution)/shard_map/all_gather | solution.py:57
  368.9 0.8 copy.45
  369.8 3.5 all-to-all-start.2
  373.3 0.1 convolution_bitcast_fusion.3
  373.4 0.3 convolution_add_fusion.1
  373.8 0.8 copy.29
  374.6 7.4 %all-to-all-done.2 = bf16[4,512,128]{1,2,0:T(8,128)(2,1)S(1)} async-done(((bf16[4,512,128]{1,2,0:T(8,128)(2,1)}), bf16[4,512,128]{1,2,0:T(8,128)(2,1)S(1)}, u32[]{:S(2)}, u32[]{:S(2)}) %all-to-all-start.2) | async-done | bytes 524320 | tf_op jit(solution)/shard_map/all_to_all | solution.py:60
  382.0 0.1 convolution_bitcast_fusion.2
  382.2 0.9 fusion.1
  383.1 0.9 convolution_add_fusion.2
  384.1 0.1 fusion.5
  384.2 5.7 %all-reduce = (f32[128]{0:T(128)S(1)}, f32[64]{0:T(128)S(1)}) all-reduce(f32[128]{0:T(128)S(1)} %fusion.3, f32[64]{0:T(128)S(1)} %fusion.5), channel_id=1, replica_groups=mesh['row'=8,'col'=4] {'col'}, use_global_device_ids=true, to_apply=%region_5.6 | all-reduce | flops 192 | bytes 1536 | tf_op jit(solution)/shard_map/psum | solution.py:80
  390.0 0.5 broadcast_multiply_fusion.1
  390.5 0.5 sub.23
  391.0 25.1 %all-reduce.3.cloned.1.call-done = f32[64,512]{1,0:T(8,128)} async-done(((f32[64,512]{1,0:T(8,128)}), f32[64,512]{1,0:T(8,128)}) %all-reduce.3.cloned.1.call-update) | async-done | bytes 131088 | tf_op jit(solution)/shard_map/psum | solution.py:80
  416.1 1.6 broadcast_multiply_fusion
  417.7 20.4 %reduce-scatter.8.cloned.1.call-done = bf16[128,128]{0,1:T(8,128)(2,1)} async-done(((bf16[128,512]{0,1:T(8,128)(2,1)}), bf16[128,128]{0,1:T(8,128)(2,1)}) %reduce-scatter.8.cloned.1.call-update) | async-done | bytes 32784 | tf_op jit(solution)/shard_map/reduce_scatter | solution.py:76
  438.0 0.8 convert_subtract_fusion.2
  438.8 0.7 copy.30
  (49 shorter events, 0.5 us)
Async XLA Ops:
  7.2 78.6 %copy-start.3 = (f32[3,256]{1,0:T(4,128)S(1)}, f32[3,256]{1,0:T(4,128)}, u32[]{:S(2)}) copy-start(f32[3,256]{1,0:T(4,128)} %param.9) | copy-start | bytes 9220
  15.3 109.4 %copy-start = (bf16[3,256,512]{2,1,0:T(8,128)(2,1)S(1)}, bf16[3,256,512]{2,1,0:T(8,128)(2,1)}, u32[]{:S(2)}) copy-start(bf16[3,256,512]{2,1,0:T(8,128)(2,1)} %param.12) | copy-start | bytes 2359300
  82.3 48.3 %all-to-all-start = ((bf16[4,512,128]{1,2,0:T(8,128)(2,1)}), bf16[4,512,128]{1,2,0:T(8,128)(2,1)S(1)}, u32[]{:S(2)}, u32[]{:S(2)}) async-start(bf16[4,512,128]{1,2,0:T(8,128)(2,1)} %bitcast.146), calls=%async_computation | async-start | bytes 1048576 | tf_op jit(solution)/shard_map/all_to_all | solution.py:60
  85.7 106.7 %reduce-scatter.4.cloned.1.call-start = ((), (), s32[]{:S(2)}) async-start(), calls=%async_computation.6 | async-start | bytes 655360 | tf_op jit(solution)/shard_map/reduce_scatter | solution.py:41
  193.3 87.4 %copy-start.2 = (bf16[128,128]{1,0:T(8,128)(2,1)S(1)}, bf16[128,128]{1,0:T(8,128)(2,1)}, u32[]{:S(2)}) copy-start(bf16[128,128]{1,0:T(8,128)(2,1)} %param.14) | copy-start | bytes 98308
  193.4 87.6 %copy-start.1 = (bf16[128,3,512]{2,0,1:T(8,128)(2,1)S(1)}, bf16[128,3,512]{2,0,1:T(8,128)(2,1)}, u32[]{:S(2)}) copy-start(bf16[128,3,512]{2,0,1:T(8,128)(2,1)} %param.13) | copy-start | bytes 1179652
  258.9 22.4 %all-to-all-start.1 = ((bf16[4,512,128]{1,2,0:T(8,128)(2,1)}), bf16[4,512,128]{1,2,0:T(8,128)(2,1)S(1)}, u32[]{:S(2)}, u32[]{:S(2)}) async-start(bf16[4,512,128]{1,2,0:T(8,128)(2,1)} %bitcast.145), calls=%async_computation.2 | async-start | bytes 1048576 | tf_op jit(solution)/shard_map/all_to_all | solution.py:60
  262.5 41.2 %reduce-scatter.6.cloned.1.call-start = ((), (), s32[]{:S(2)}) async-start(), calls=%async_computation.7 | async-start | bytes 655360 | tf_op jit(solution)/shard_map/reduce_scatter | solution.py:41
  368.9 21.6 %copy-start.4 = (f32[128]{0:T(128)S(1)}, f32[128]{0:T(128)}, u32[]{:S(2)}) copy-start(f32[128]{0:T(128)} %param.15) | copy-start | bytes 1540
  369.8 12.3 %all-to-all-start.2 = ((bf16[4,512,128]{1,2,0:T(8,128)(2,1)}), bf16[4,512,128]{1,2,0:T(8,128)(2,1)S(1)}, u32[]{:S(2)}, u32[]{:S(2)}) async-start(bf16[4,512,128]{1,2,0:T(8,128)(2,1)} %bitcast.144), calls=%async_computation.4 | async-start | bytes 1048576 | tf_op jit(solution)/shard_map/all_to_all | solution.py:60
  373.3 42.8 %all-reduce.3.cloned.1.call-start = ((), (), s32[]{:S(2)}) async-start(), calls=%async_computation.9 | async-start | bytes 262144 | tf_op jit(solution)/shard_map/psum | solution.py:80
  384.1 54.0 %reduce-scatter.8.cloned.1.call-start = ((), (), s32[]{:S(2)}) async-start(), calls=%async_computation.8 | async-start | bytes 163840 | tf_op jit(solution)/shard_map/reduce_scatter | solution.py:76
Sparse Core Ops, SparseCore 0:
  131.8 20.9 reduce-scatter.3
  282.7 20.9 reduce-scatter.5
  384.2 31.8 all-reduce.2
  418.4 19.6 reduce-scatter.7
where the time goes:
time: 447 us; the launch traced here: 446 us
  blocking collectives  314 us (70%)
  waiting for transfers between devices  72.4 us (16%)
  between operations  19.8 us (4%)
  matrix products  16.5 us (4%)
  starting transfers between devices  10.6 us (2%)
  local copies, waits for them, and re-layouts  7.06 us (2%)
  other arithmetic  5.95 us (1%)
    all_gather x3, blocking collectives, shards(): lax.all_gather(residual, 'row', axis=0, tiled=True)  96.4 us
    all_gather x3, blocking collectives, shards(): lax.all_gather(tile, 'row', axis=0, tiled=True)  93.7 us
    all_gather x3, blocking collectives, shards(): lax.all_gather(resid_resp, 'row', axis=0, tiled=True)  57.4 us
    all_gather x3, blocking collectives, shards(): lax.all_gather(tile_resp, 'row', axis=0, tiled=True)  49.1 us
    psum x1, waiting for transfers between devices, shards(): gram, right, resp_sum = lax.psum((gram, right, trail_resp_total), 'col')  25.1 us
    reduce_scatter x1, waiting for transfers between devices, shards(): lax.psum_scatter(trail_total.astype(jnp.bfloat16), 'col', scatter_dimensi...  20.4 us
    reduce_scatter x2, waiting for transfers between devices, shards(): lax.psum_scatter(update, 'col', scatter_dimension=1, tiled=True)  19.5 us
    psum x2, blocking collectives, shards(): pending_resp = pending_resp - lax.psum(update_resp, 'col')  11.3 us
  transfers between devices with their start and end apart: 7, of which 4 were waited for; matrix products, arithmetic and copies ran while one was open for 3% of the time, Pallas kernels for 0%

commit v1 on v0

v1 whole, which is shorter than its diff:
```python
import functools

import jax
import jax.numpy as jnp
from jax import lax
from jax.experimental import pallas as pl
from jax.experimental.pallas import tpu as pltpu
from jax.sharding import PartitionSpec as P

BF16 = jnp.bfloat16
F32 = jnp.float32
PAD = 8
CONTRACT_LAST = (((1,), (1,)), ((), ()))


def dot_t(a, b):
    return lax.dot_general(a, b, CONTRACT_LAST, preferred_element_type=F32)


class Place:
    def __init__(self, row, col):
        self.row, self.col = row, col
        self.z, self.x, self.core = row // 2, row % 2, col % 2
        self.scalars = None


def call(kernel, name, place, operands, outs, scratch):
    arrays, layers = [], []
    for item in operands:
        array, index = item if isinstance(item, tuple) else (item, None)
        arrays.append(array)
        layers.append(index)

    def body(scalars, *refs):
        views = [r if n is None else r.at[n] for r, n in zip(refs, layers)]
        kernel(scalars, *views, *refs[len(layers) :])

    vmem = pl.BlockSpec(memory_space=pltpu.VMEM)
    return pl.pallas_call(
        body,
        in_specs=[pl.BlockSpec(memory_space=pltpu.SMEM)] + [vmem] * len(arrays),
        out_specs=[vmem] * len(outs),
        out_shape=outs,
        scratch_shapes=scratch,
        name=name,
    )(place.scalars, *arrays)


def contract_kernel(plan, counts, scalars, *refs):
    tiles_n, mats_n, has_base, me, block = counts
    place = Place(scalars[0], scalars[1])
    tiles, refs = refs[:tiles_n], refs[tiles_n:]
    mats, refs = refs[:mats_n], refs[mats_n:]
    base, refs = (refs[0], refs[1:]) if has_base else (None, refs)
    out, gathered = refs
    for k, tile in enumerate(tiles):
        at = pl.multiple_of((me(place) ^ k) * block, block)
        gathered[:, pl.ds(at, block)] = tile[...]
    for members, rows, out_at in plan:
        total = None
        for index, width, col_at in members:
            at = pl.multiple_of(col_at(place), width)
            part = dot_t(gathered[:, pl.ds(at, width)], mats[index][...])
            total = part if total is None else total + part
        at = pl.ds(pl.multiple_of(out_at(place), rows), rows)
        if base is not None:
            total = base[:, at] - total
        out[:, at] = total.astype(out.dtype)


def contract(name, place, tiles, me, groups, out_rows, base=None, dtype=BF16):
    height, block = tiles[0].shape
    mats, plan = [], []
    for members, rows, out_at in groups:
        listed = []
        for mat, width, col_at in members:
            listed.append((len(mats), width, col_at))
            mats.append(mat)
        plan.append((listed, rows, out_at))
    widths = [w for members, _, _ in plan for _, w, _ in members] + [r for _, r, _ in plan]
    if all(w % 128 == 0 for w in widths + [block]):
        counts = (len(tiles), len(mats), base is not None, me, block)
        return call(
            functools.partial(contract_kernel, plan, counts),
            name,
            place,
            list(tiles) + mats + ([base] if base is not None else []),
            [jax.ShapeDtypeStruct((height, out_rows), dtype)],
            [pltpu.VMEM((height, block * len(tiles)), BF16)],
        )[0]
    order = me(place) ^ jnp.arange(len(tiles))
    gathered = jnp.stack(tiles)[order].transpose(1, 0, 2).reshape(height, -1)
    out = jnp.zeros((height, out_rows), F32)
    for members, rows, out_at in plan:
        total = 0.0
        for index, width, col_at in members:
            mat = mats[index]
            mat = mat[0][mat[1]] if isinstance(mat, tuple) else mat
            total += dot_t(lax.dynamic_slice_in_dim(gathered, col_at(place), width, 1), mat)
        if base is not None:
            total = lax.dynamic_slice_in_dim(base, out_at(place), rows, 1) - total
        out = lax.dynamic_update_slice_in_dim(out, total, out_at(place), 1)
    return out.astype(dtype)


def partial_kernel(counts, scalars, *refs):
    planes, cols, blocks, layers, has_base = counts
    place = Place(scalars[0], scalars[1])
    tiles, refs = refs[: 2 * cols], refs[2 * cols :]
    resps, refs = refs[: len(layers)], refs[len(layers) :]
    factors, refs = refs[: len(layers)], refs[len(layers) :]
    base, refs = (refs[: 2 * planes], refs[2 * planes :]) if has_base else (None, refs)
    grams, trails, wide = refs[:planes], refs[planes : 2 * planes], refs[2 * planes]
    half = tiles[0].shape[-2]
    trail_rows = factors[0].shape[0]
    full = 2 * cols * half
    for n in range(len(layers)):
        for dx in range(2):
            for dc in range(cols):
                at = (place.col ^ dc) * (2 * half) + (place.x ^ dx) * half
                wide[n, pl.ds(pl.multiple_of(at, half), half), :] = tiles[dx * cols + dc][n]
    for k in range(planes):
        to = place.z ^ k
        gram, resp, trail, trail_resp = 0.0, 0.0, 0.0, 0.0
        for n in range(len(layers)):
            own = wide[n, pl.ds(pl.multiple_of(to * (2 * half) + place.x * half, half), half), :]
            gram += dot_t(own, wide[n])
            resp += dot_t(resps[n][...], own)
            block = wide[n, pl.ds(pl.multiple_of(to * (2 * half), 2 * half), 2 * half), :]
            trail += dot_t(factors[n][...], block)
            trail_resp += dot_t(resps[n][...], factors[n][...])
        if has_base:
            gram += base[k][:half, :]
            resp += base[k][half:, :half]
            trail += base[planes + k][:trail_rows, : 2 * half]
            trail_resp += base[planes + k][trail_rows:, :trail_rows]
        kind = grams[k].dtype
        grams[k][:half, :] = gram.astype(kind)
        grams[k][half:, :] = jnp.zeros((PAD, full), kind)
        grams[k][half:, :half] = resp.astype(kind)
        trails[k][:trail_rows, : 2 * half] = trail.astype(kind)
        trails[k][trail_rows:, :trail_rows] = trail_resp.astype(kind)


def partials(name, place, planes, cols, tiles, resps, factors, layers, base, dtype):
    half, block = tiles[0].shape[-2:]
    trail_rows = factors.shape[1]
    full = 2 * cols * half
    gram = jax.ShapeDtypeStruct((half + PAD, full), dtype)
    trail = jax.ShapeDtypeStruct((trail_rows + PAD, max(2 * half, trail_rows)), dtype)
    counts = (planes, cols, block, layers, base is not None)
    return call(
        functools.partial(partial_kernel, counts),
        name,
        place,
        list(tiles) + list(resps) + [(factors, n) for n in layers] + list(base or []),
        [gram] * planes + [trail] * planes,
        [pltpu.VMEM((len(layers), full, block), BF16)],
    )


def final_kernel(planes, scale, scalars, *refs):
    grams, trails = refs[:planes], refs[planes : 2 * planes]
    x_ref, y_ref, rhs, resp, normal, right = refs[2 * planes :]
    half = normal.shape[0]
    rows = rhs.shape[0]
    gram = sum(g[...].astype(F32) for g in grams)
    trail = sum(t[...].astype(F32) for t in trails)
    normal[...] = gram[:half] * scale
    right[...] = gram[half:] * scale
    rhs[...] = x_ref[...].astype(F32) - trail[:rows, : rhs.shape[1]]
    resp[...] = y_ref[...] - trail[rows:, :rows]


def shards(
    x_window, y_window, block_order, diag_inverse, panel_window, panel_trail, x_trail, y_trail
):
    steps, rows, own_cols = x_window.shape
    width = panel_window.shape[2]
    n_rows, n_cols = lax.axis_size("row"), lax.axis_size("col")
    planes = n_rows // 2
    place = Place(lax.axis_index("row"), lax.axis_index("col"))
    place.scalars = jnp.stack([place.row, place.col]).astype(jnp.int32)
    x, core = place.x, place.core
    half = own_cols // 2
    pair = 2 * rows
    total_rows = rows * n_rows

    def move(array, to):
        table = []
        for r in range(n_rows):
            for c in range(n_cols):
                tr, tc = to(r, c)
                table.append((r * n_cols + c, tr * n_cols + tc))
        return lax.ppermute(array, ("row", "col"), table)

    def flip(array, dr=0, dc=0):
        return move(array, lambda r, c: (r ^ dr, c ^ dc))

    def ordered(own, other, axis):
        return jnp.where(
            x == 0,
            jnp.concatenate([own, other], axis),
            jnp.concatenate([other, own], axis),
        )

    def stored(s):
        xs = lax.dynamic_index_in_dim(x_window, block_order[s], 0, keepdims=False).T
        ys = lax.dynamic_index_in_dim(y_window, block_order[s], 0, keepdims=True)
        return xs, ys

    x0, y0 = stored(0)
    first = jnp.concatenate([x0, y0.astype(BF16), jnp.zeros((PAD - 1, rows), BF16)], 0)
    first_tiles = [first] + [flip(first, dr=k) for k in range(1, n_rows)]

    def panel(array):
        pieces = {(0, 0): array}
        bit = n_cols // 2
        while bit > 1:
            pieces |= {(dx, dc ^ bit): flip(a, dc=bit) for (dx, dc), a in pieces.items()}
            bit //= 2
        pieces |= {(1, dc): flip(a, dr=1) for (dx, dc), a in pieces.items()}
        pieces |= {(dx, dc ^ 1): flip(a, dc=1) for (dx, dc), a in pieces.items()}
        return pieces

    panels = {}
    for s in range(1, steps):
        at = s * (s - 1) // 2
        got = panel(panel_window[at : at + s])
        for t in range(s):
            panels[s, t] = {key: (a, t) for key, a in got.items()}

    part = lax.dynamic_slice_in_dim(diag_inverse, core * (rows // 2), rows // 2, 1)[1:]
    part_same = flip(part, dr=1)
    part_other = flip(part_same, dc=1)

    bases = []
    sent, kept = [], []
    for s in range(1, steps):
        xs, ys = stored(s)
        high = ys.astype(BF16)
        low = (ys - high.astype(F32)).astype(BF16)
        zeros = jnp.zeros((PAD - 2, rows), BF16)
        other = lax.dynamic_slice_in_dim(xs, (1 - x) * half, half, 0)
        own = lax.dynamic_slice_in_dim(xs, x * half, half, 0)
        sent.append(jnp.concatenate([other, high, low, zeros], 0))
        kept.append(jnp.concatenate([own.astype(F32), ys, jnp.zeros((PAD - 1, rows), F32)], 0))
    got = flip(jnp.stack(sent), dr=1).astype(F32)
    for n in range(steps - 1):
        resp = got[n, half : half + 1] + got[n, half + 1 : half + 2]
        other = jnp.concatenate([got[n, :half], resp, jnp.zeros((PAD - 1, rows), F32)], 0)
        bases.append(ordered(kept[n], other, 1))

    trail_factor = move(panel_trail.transpose(1, 0, 2), lambda r, c: (2 * c + r % 2, r // 2))

    def spread(tile):
        return [tile] + [flip(tile, dr=2 * k) for k in range(1, planes)]

    def solve(s, tiles):
        n = s - 1
        groups = [
            ([((diag_inverse, s), total_rows, lambda p: 0)], rows, lambda p: p.x * rows),
            (
                [((part_same, n), total_rows, lambda p: 0)],
                rows // 2,
                lambda p: (1 - p.x) * rows + p.core * (rows // 2),
            ),
            (
                [((part_other, n), total_rows, lambda p: 0)],
                rows // 2,
                lambda p: (1 - p.x) * rows + (1 - p.core) * (rows // 2),
            ),
        ]
        return contract(f"solve{s}", place, tiles, lambda p: p.z, groups, pair)

    def update(s, t, tiles, base, dtype):
        groups = []
        for dx in range(2):
            members = [
                (panels[s, t][dx, dc], width, lambda p, dc=dc: (p.col ^ dc) * width)
                for dc in range(n_cols)
            ]
            groups.append((members, rows, lambda p, dx=dx: (p.x ^ dx) * rows))
        return contract(f"update{s}{t}", place, tiles, lambda p: p.z, groups, pair, base, dtype)

    whole0 = contract(
        "solve0",
        place,
        first_tiles,
        lambda p: p.row,
        [([((diag_inverse, 0), total_rows, lambda p: 0)], rows, lambda p: 0)],
        rows,
    )
    resp0 = whole0[own_cols:]
    give = jnp.concatenate([lax.dynamic_slice_in_dim(whole0, (1 - x) * half, half, 0), resp0], 0)
    keep = jnp.concatenate([lax.dynamic_slice_in_dim(whole0, x * half, half, 0), resp0], 0)
    solved = [ordered(keep, flip(give, dr=1), 1)]
    pending = list(bases)
    for s in range(1, steps):
        tiles = spread(solved[s - 1])
        residual = update(s, s - 1, tiles, pending[s - 1], BF16)
        for later in range(s + 1, steps):
            pending[later - 1] = update(later, s - 1, tiles, pending[later - 1], F32)
        solved.append(solve(s, spread(residual)))

    early = jnp.stack([t[:half] for t in solved[:-1]])
    pieces = {(0, 0): early}
    bit = 1
    while bit < n_cols:
        pieces |= {(dx, dc ^ bit): flip(a, dc=bit) for (dx, dc), a in pieces.items()}
        bit *= 2
    pieces |= {(1, dc): flip(a, dr=1) for (dx, dc), a in pieces.items()}
    early_tiles = [pieces[dx, dc] for dx in range(2) for dc in range(n_cols)]
    late = solved[-1][:half][None]
    late_tiles = [
        flip(late, dr=dx, dc=dc) if dx or dc else late for dx in range(2) for dc in range(n_cols)
    ]
    resps = [t[half:] for t in solved]
    early_sums = partials(
        "early", place, planes, n_cols, early_tiles, resps[:-1], trail_factor,
        tuple(range(steps - 1)), None, F32,
    )
    late_sums = partials(
        "late", place, planes, n_cols, late_tiles, resps[-1:], trail_factor,
        (steps - 1,), early_sums, BF16,
    )
    grams = [late_sums[0]] + [flip(late_sums[k], dr=2 * k) for k in range(1, planes)]
    trails = [
        move(late_sums[planes + k], lambda r, c, k=k: (2 * c + r % 2, (r // 2) ^ k))
        for k in range(planes)
    ]
    scale = 1.0 / (steps * total_rows)
    full = own_cols * n_cols
    trail_rows = x_trail.shape[0]
    trail_rhs, trail_resp, normal, right = call(
        functools.partial(final_kernel, planes, scale),
        "final",
        place,
        grams + trails + [x_trail, y_trail[None]],
        [
            jax.ShapeDtypeStruct((trail_rows, own_cols), F32),
            jax.ShapeDtypeStruct((PAD, trail_rows), F32),
            jax.ShapeDtypeStruct((half, full), F32),
            jax.ShapeDtypeStruct((PAD, full), F32),
        ],
        [],
    )

    outs = [whole0[:own_cols].T]
    resp_outs = [resp0[0]]
    for s in range(1, steps):
        other = early_tiles[n_cols][s] if s < steps - 1 else late_tiles[n_cols][0]
        both = ordered(solved[s][:half], other, 0)
        outs.append(lax.dynamic_slice_in_dim(both, x * rows, rows, 1).T)
        resp_outs.append(lax.dynamic_slice_in_dim(solved[s][half], x * rows, rows, 0))
    return (
        jnp.stack(outs),
        jnp.stack(resp_outs),
        trail_rhs,
        trail_resp[0],
        normal,
        right[0, :half],
    )


def solution(mesh):
    in_specs = (
        P(None, "row", "col"),
        P(None, "row"),
        P(),
        P(None, "row", None),
        P(None, "row", "col"),
        P("row", None, "col"),
        P("row", "col"),
        P("row"),
    )
    out_specs = (
        P(None, "row", "col"),
        P(None, "row"),
        P("row", "col"),
        P("row"),
        P("row", None),
        P("row"),
    )
    return jax.shard_map(shards, mesh=mesh, in_specs=in_specs, out_specs=out_specs, check_vma=False)
```

time: 447 us -> 189 us (0.42)
  blocking collectives: 314 us -> 0 us
  starting transfers between devices: 10.6 us -> 61.3 us
  Pallas kernels: 0 us -> 31.2 us
  waiting for transfers between devices: 72.4 us -> 49.8 us
  local copies, waits for them, and re-layouts: 7.06 us -> 28.4 us
  matrix products: 16.5 us -> 0 us
  between operations: 19.8 us -> 7.29 us
    all_gather x12 -> x0, blocking collectives: 297 us -> none  [the longest x3 96.4 us: shards(): lax.all_gather(residual, 'row', axis=0, tiled=True)]
    ppermute x0 -> x59, starting transfers between devices: none -> 61.3 us  [move(): return lax.ppermute(array, ('row', 'col'), table)]
    ppermute x0 -> x59, waiting for transfers between devices: none -> 49.8 us  [move(): return lax.ppermute(array, ('row', 'col'), table)]
    reduce_scatter x3 -> x0, waiting for transfers between devices: 39.8 us -> none  [the longest x1 20.4 us: shards(): lax.psum_scatter(trail_total.astype(jnp.bfloat16), 'col', scatter_dimensi...]
    pallas_call x0 -> x9, Pallas kernels: none -> 31.2 us  [call(): pl.pallas_call(body, in_specs=[pl.BlockSpec(memory_space=pltpu.SMEM)] + [...]
    psum x1 -> x0, waiting for transfers between devices: 25.1 us -> none  [shards(): gram, right, resp_sum = lax.psum((gram, right, trail_resp_total), 'col')]
    psum x3 -> x0, blocking collectives: 17.1 us -> none  [the longest x2 11.3 us: shards(): pending_resp = pending_resp - lax.psum(update_resp, 'col')]
    dot_general x22 -> x0, matrix products: 16.5 us -> none  [the longest x3 5.12 us: shards(): jnp.dot(inverse, whole, preferred_element_type=jnp.float32)]
  transfers between devices with their start and end apart: 7 -> 59, of which waited for: 4 -> 15; matrix products, arithmetic and copies ran while one was open for 3% -> 14% of each run, Pallas kernels for 0% -> 14%
where the time goes in v1:
time: 189 us; the launch traced here: 188 us
  starting transfers between devices  61.3 us (32%)
  waiting for transfers between devices  49.8 us (26%)
  Pallas kernels  31.2 us (17%)
  local copies, waits for them, and re-layouts  28.4 us (15%)
  other arithmetic  9.64 us (5%)
  between operations  7.29 us (4%)
    ppermute x59, starting transfers between devices, move(): return lax.ppermute(array, ('row', 'col'), table)  61.3 us
    ppermute x59, waiting for transfers between devices, move(): return lax.ppermute(array, ('row', 'col'), table)  49.8 us
    pallas_call x9, Pallas kernels, call(): pl.pallas_call(body, in_specs=[pl.BlockSpec(memory_space=pltpu.SMEM)] + [...  31.2 us
    unnamed x121, local copies, waits for them, and re-layouts  8.98 us
  transfers between devices with their start and end apart: 59, of which 15 were waited for; matrix products, arithmetic and copies ran while one was open for 14% of the time, Pallas kernels for 14%

profile of v1, /device:TPU:0, one launch (start us, length us, event | category | flops | bytes accessed | tf_op | source)
XLA Modules:
  0.0 187.6 jit_solution(7549712234126888081)
XLA Ops:
  0.6 1.4 fusion.21
  5.8 3.0 %collective-permute-start = (bf16[136,256]{1,0:T(8,128)(2,1)S(1)}, bf16[136,256]{1,0:T(8,128)(2,1)S(1)}, u32[]{:S(2)}, u32[]{:S(2)}) collective-permute-start(bf16[136,256]{1,0:T(8,128)(2,1)S(1)} %maximum_maximum_fusion.refs_0_), channel_id=1, source_target_pairs={{0,4},{1,5},{2,6},{3,7},{4,0},{5,1},{6,2},{7,3},{8,12},{9,13},{10,... | collective-permute-start | bytes 208904 | tf_op jit(solution)/shard_map/ppermute | solution.py:195
  8.8 1.6 collective-permute-start.1
  10.4 3.0 %collective-permute-start.3 = (bf16[136,256]{1,0:T(8,128)(2,1)S(1)}, bf16[136,256]{1,0:T(8,128)(2,1)S(1)}, u32[]{:S(2)}, u32[]{:S(2)}) collective-permute-start(bf16[136,256]{1,0:T(8,128)(2,1)S(1)} %maximum_maximum_fusion.refs_0_), channel_id=1, source_target_pairs={{0,16},{1,17},{2,18},{3,19},{4,20},{5,21},{6,22},{7,23},{8,24},{9,... | collective-permute-start | bytes 208904 | tf_op jit(solution)/shard_map/ppermute | solution.py:195
  13.4 1.3 constant_dynamic-slice_fusion.3
  14.7 1.6 collective-permute-start.22
  20.9 1.7 constant_dynamic-slice_fusion.2
  23.2 3.9 %collective-permute-start.5 = (bf16[136,256]{1,0:T(8,128)(2,1)S(1)}, bf16[136,256]{1,0:T(8,128)(2,1)S(1)}, u32[]{:S(2)}, u32[]{:S(2)}) collective-permute-start(bf16[136,256]{1,0:T(8,128)(2,1)S(1)} %maximum_maximum_fusion.refs_0_), channel_id=1, source_target_pairs={{0,24},{1,25},{2,26},{3,27},{4,28},{5,29},{6,30},{7,31},{8,16},{9,... | collective-permute-start | bytes 208904 | tf_op jit(solution)/shard_map/ppermute | solution.py:195
  27.1 1.2 collective-permute-start.6
  28.9 3.4 %collective-permute-done.4.refs_5_ = bf16[136,256]{1,0:T(8,128)(2,1)S(1)} collective-permute-done((bf16[136,256]{1,0:T(8,128)(2,1)S(1)}, bf16[136,256]{1,0:T(8,128)(2,1)S(1)}, u32[]{:S(2)}, u32[]{:S(2)}) %collective-permute-start.4) | collective-permute-done | bytes 69664 | tf_op jit(solution)/shard_map/ppermute | solution.py:195
  32.3 1.9 %collective-permute-done.6.refs_7_ = bf16[136,256]{1,0:T(8,128)(2,1)S(1)} collective-permute-done((bf16[136,256]{1,0:T(8,128)(2,1)S(1)}, bf16[136,256]{1,0:T(8,128)(2,1)S(1)}, u32[]{:S(2)}, u32[]{:S(2)}) %collective-permute-start.6) | collective-permute-done | bytes 69664 | tf_op jit(solution)/shard_map/ppermute | solution.py:195
  34.9 3.3 %solve0.1 = bf16[136,256]{1,0:T(8,128)(2,1)} custom-call(s32[2]{0:T(128)} %pad_add_fusion.scalars, bf16[136,256]{1,0:T(8,128)(2,1)} %copy-done.13, bf16[136,256]{1,0:T(8,128)(2,1)} %copy-done.39, bf16[136,256]{1,0:T(8,128)(2,1)} %copy-done.40, bf16[136,256]{1,0:T(8,128)(2,1)} %copy-done.41, bf16[136,256]{1,0:T(8,128)(2,1)} %copy-done.42, ...), custom_call_target="tpu_custom_call" | custom-call | tf_op jit(solution)/shard_map/solve0/pallas_call | solution.py:39
  39.7 1.6 collective-permute-start.7
  41.9 1.9 collective-permute-done.7
  43.8 1.4 collective-permute-start.8
  45.8 2.5 %collective-permute-start.10 = (bf16[72,512]{1,0:T(8,128)(2,1)S(1)}, bf16[72,512]{1,0:T(8,128)(2,1)}, u32[]{:S(2)}, u32[]{:S(2)}) collective-permute-start(bf16[72,512]{1,0:T(8,128)(2,1)S(1)} %maximum_select_fusion.refs_0_), channel_id=1, source_target_pairs={{0,24},{1,25},{2,26},{3,27},{4,28},{5,29},{6,30},{7,31},{8,16},{9,... | collective-permute-start | bytes 221192 | tf_op jit(solution)/shard_map/ppermute | solution.py:195
  48.3 1.0 slice.87.refs_4_
  49.3 1.6 collective-permute-start.12
  51.5 1.1 slice.97.refs_4_
  53.3 1.5 collective-permute-start.14
  55.4 1.4 convert_bitcast_fusion.1
  56.8 1.5 copy.21
  59.1 1.4 convert_bitcast_fusion
  61.4 1.1 collective-permute-done.14.refs_8_
  62.6 1.5 collective-permute-start.31
  64.8 3.4 %collective-permute-done.16.refs_10_ = bf16[1,256,512]{2,1,0:T(8,128)(2,1)} collective-permute-done((bf16[1,256,512]{2,1,0:T(8,128)(2,1)}, bf16[1,256,512]{2,1,0:T(8,128)(2,1)}, u32[]{:S(2)}, u32[]{:S(2)}) %collective-permute-start.16) | collective-permute-done | bytes 262176 | tf_op jit(solution)/shard_map/ppermute | solution.py:195
  70.4 1.6 fusion.1.refs_12_
  72.0 3.1 %update10.1.refs_0_ = bf16[72,512]{1,0:T(8,128)(2,1)} custom-call(s32[2]{0:T(128)} %pad_add_fusion.scalars, bf16[72,512]{1,0:T(8,128)(2,1)} %copy-done.5, bf16[72,512]{1,0:T(8,128)(2,1)} %copy-done.11, bf16[72,512]{1,0:T(8,128)(2,1)} %copy-done.12, bf16[72,512]{1,0:T(8,128)(2,1)} %collective-permute-done.10.refs_3_, bf16[1,256,512]{2,1,0:T(8,128)(2,1)} %copy-done.6, ...), custom_call_target="tpu_custom_call" | custom-call | tf_op jit(solution)/shard_map/update10/pallas_call | solution.py:39
  75.3 1.5 collective-permute-start.20
  76.8 2.6 %collective-permute-done.31.refs_8_ = bf16[2,256,512]{2,1,0:T(8,128)(2,1)} collective-permute-done((bf16[2,256,512]{2,1,0:T(8,128)(2,1)S(1)}, bf16[2,256,512]{2,1,0:T(8,128)(2,1)}, u32[]{:S(2)}, u32[]{:S(2)}) %collective-permute-start.31) | collective-permute-done | bytes 524320 | tf_op jit(solution)/shard_map/ppermute | solution.py:195
  79.4 1.4 collective-permute-start.21
  80.9 1.7 collective-permute-done.20.refs_2_
  82.6 3.2 %collective-permute-done.21.refs_3_ = bf16[72,512]{1,0:T(8,128)(2,1)S(1)} collective-permute-done((bf16[72,512]{1,0:T(8,128)(2,1)}, bf16[72,512]{1,0:T(8,128)(2,1)S(1)}, u32[]{:S(2)}, u32[]{:S(2)}) %collective-permute-start.21) | collective-permute-done | bytes 73760 | tf_op jit(solution)/shard_map/ppermute | solution.py:195
  85.8 4.5 %collective-permute-done.33.refs_10_ = bf16[2,256,512]{2,1,0:T(8,128)(2,1)} collective-permute-done((bf16[2,256,512]{2,1,0:T(8,128)(2,1)S(1)}, bf16[2,256,512]{2,1,0:T(8,128)(2,1)}, u32[]{:S(2)}, u32[]{:S(2)}) %collective-permute-start.33) | collective-permute-done | bytes 524320 | tf_op jit(solution)/shard_map/ppermute | solution.py:195
  91.1 1.0 copy-done.2
  92.1 4.0 %solve1.1.refs_0_ = bf16[72,512]{1,0:T(8,128)(2,1)} custom-call(s32[2]{0:T(128)} %pad_add_fusion.scalars, bf16[72,512]{1,0:T(8,128)(2,1)} %update10.1.refs_0_, bf16[72,512]{1,0:T(8,128)(2,1)} %copy-done.30, bf16[72,512]{1,0:T(8,128)(2,1)} %copy-done.32, bf16[72,512]{1,0:T(8,128)(2,1)} %copy-done.35, bf16[3,256,2048]{2,1,0:T(8,128)(2,1)} %refs_4_.3, ...), custom_call_target="tpu_custom_call" | custom-call | tf_op jit(solution)/shard_map/solve1/pallas_call | solution.py:39
  97.1 1.6 collective-permute-start.24
  99.6 1.3 slice.126.refs_8_
  100.9 3.7 %update20.1.refs_12_ = f32[72,512]{1,0:T(8,128)} custom-call(s32[2]{0:T(128)} %pad_add_fusion.scalars, bf16[72,512]{1,0:T(8,128)(2,1)} %copy-done.5, bf16[72,512]{1,0:T(8,128)(2,1)} %copy-done.11, bf16[72,512]{1,0:T(8,128)(2,1)} %copy-done.12, bf16[72,512]{1,0:T(8,128)(2,1)} %collective-permute-done.10.refs_3_, bf16[2,256,512]{2,1,0:T(8,128)(2,1)} %copy-done, ...), custom_call_target="tpu_custom_call" | custom-call | tf_op jit(solution)/shard_map/update20/pallas_call | solution.py:39
  104.6 1.6 collective-permute-start.26
  106.3 2.8 %collective-permute-start.27 = (bf16[72,512]{1,0:T(8,128)(2,1)S(1)}, bf16[72,512]{1,0:T(8,128)(2,1)S(1)}, u32[]{:S(2)}, u32[]{:S(2)}) collective-permute-start(bf16[72,512]{1,0:T(8,128)(2,1)S(1)} %copy-done.7), channel_id=1, source_target_pairs={{0,24},{1,25},{2,26},{3,27},{4,28},{5,29},{6,30},{7,31},{8,16},{9,... | collective-permute-start | bytes 221192 | tf_op jit(solution)/shard_map/ppermute | solution.py:195
  110.8 11.0 %collective-permute-done.26.refs_2_ = bf16[72,512]{1,0:T(8,128)(2,1)S(1)} collective-permute-done((bf16[72,512]{1,0:T(8,128)(2,1)S(1)}, bf16[72,512]{1,0:T(8,128)(2,1)S(1)}, u32[]{:S(2)}, u32[]{:S(2)}) %collective-permute-start.26) | collective-permute-done | bytes 73760 | tf_op jit(solution)/shard_map/ppermute | solution.py:195
  123.1 3.7 %update21.1.refs_0_ = bf16[72,512]{1,0:T(8,128)(2,1)} custom-call(s32[2]{0:T(128)} %pad_add_fusion.scalars, bf16[72,512]{1,0:T(8,128)(2,1)} %solve1.1.refs_0_, bf16[72,512]{1,0:T(8,128)(2,1)} %copy-done.34, bf16[72,512]{1,0:T(8,128)(2,1)} %copy-done.36, bf16[72,512]{1,0:T(8,128)(2,1)} %copy-done.37, bf16[2,256,512]{2,1,0:T(8,128)(2,1)} %copy-done, ...), custom_call_target="tpu_custom_call" | custom-call | tf_op jit(solution)/shard_map/update21/pallas_call | solution.py:39
  126.8 2.1 %collective-permute-start.35 = (bf16[72,512]{1,0:T(8,128)(2,1)}, bf16[72,512]{1,0:T(8,128)(2,1)S(1)}, u32[]{:S(2)}, u32[]{:S(2)}) collective-permute-start(bf16[72,512]{1,0:T(8,128)(2,1)} %update21.1.refs_0_), channel_id=1, source_target_pairs={{0,8},{1,9},{2,10},{3,11},{4,12},{5,13},{6,14},{7,15},{8,0},{9,1},... | collective-permute-start | bytes 221192 | tf_op jit(solution)/shard_map/ppermute | solution.py:195
  129.0 3.7 %collective-permute-start.37 = (bf16[72,512]{1,0:T(8,128)(2,1)}, bf16[72,512]{1,0:T(8,128)(2,1)S(1)}, u32[]{:S(2)}, u32[]{:S(2)}) collective-permute-start(bf16[72,512]{1,0:T(8,128)(2,1)} %update21.1.refs_0_), channel_id=1, source_target_pairs={{0,24},{1,25},{2,26},{3,27},{4,28},{5,29},{6,30},{7,31},{8,16},{9,... | collective-permute-start | bytes 221192 | tf_op jit(solution)/shard_map/ppermute | solution.py:195
  132.8 4.3 %collective-permute-done.36.refs_2_ = bf16[72,512]{1,0:T(8,128)(2,1)S(1)} collective-permute-done((bf16[72,512]{1,0:T(8,128)(2,1)}, bf16[72,512]{1,0:T(8,128)(2,1)S(1)}, u32[]{:S(2)}, u32[]{:S(2)}) %collective-permute-start.36) | collective-permute-done | bytes 73760 | tf_op jit(solution)/shard_map/ppermute | solution.py:195
  138.4 4.0 %solve2.1 = bf16[72,512]{1,0:T(8,128)(2,1)} custom-call(s32[2]{0:T(128)} %pad_add_fusion.scalars, bf16[72,512]{1,0:T(8,128)(2,1)} %update21.1.refs_0_, bf16[72,512]{1,0:T(8,128)(2,1)} %copy-done.31, bf16[72,512]{1,0:T(8,128)(2,1)} %copy-done.33, bf16[72,512]{1,0:T(8,128)(2,1)} %copy-done.38, bf16[3,256,2048]{2,1,0:T(8,128)(2,1)} %refs_4_.3, ...), custom_call_target="tpu_custom_call" | custom-call | tf_op jit(solution)/shard_map/solve2/pallas_call | solution.py:39
  142.4 1.5 collective-permute-start.51
  145.5 1.3 slice.125.refs_8_
  147.4 3.6 %collective-permute-done.38.refs_4_ = bf16[1,64,512]{2,1,0:T(8,128)(2,1)S(1)} collective-permute-done((bf16[1,64,512]{2,1,0:T(8,128)(2,1)S(1)}, bf16[1,64,512]{2,1,0:T(8,128)(2,1)S(1)}, u32[]{:S(2)}, u32[]{:S(2)}) %collective-permute-start.38) | collective-permute-done | bytes 65568 | tf_op jit(solution)/shard_map/ppermute | solution.py:195
  151.2 2.3 %collective-permute-start.42 = (bf16[1,64,512]{2,1,0:T(8,128)(2,1)S(1)}, bf16[1,64,512]{2,1,0:T(8,128)(2,1)S(1)}, u32[]{:S(2)}, u32[]{:S(2)}) collective-permute-start(bf16[1,64,512]{2,1,0:T(8,128)(2,1)S(1)} %get-tuple-element.67.refs_0_), channel_id=1, source_target_pairs={{0,5},{1,4},{2,7},{3,6},{4,1},{5,0},{6,3},{7,2},{8,13},{9,12},{10,... | collective-permute-start | bytes 196616 | tf_op jit(solution)/shard_map/ppermute | solution.py:195
  153.4 0.9 collective-permute-start.43
  154.3 1.2 collective-permute-start.44
  156.2 4.3 %early.1 = (f32[72,512]{1,0:T(8,128)}, f32[72,512]{1,0:T(8,128)}, f32[72,512]{1,0:T(8,128)}, f32[72,512]{1,0:T(8,128)}, f32[136,128]{1,0:T(8,128)}, /*index=5*/f...) custom-call(s32[2]{0:T(128)} %pad_add_fusion.scalars, bf16[2,64,512]{2,1,0:T(8,128)(2,1)} %copy-done.9, ...), custom_call_target="tpu_custom_call" | custom-call | tf_op jit(solution)/shard_map/early/pallas_call | solution.py:39
  161.2 3.2 %late.1 = (bf16[72,512]{1,0:T(8,128)(2,1)}, bf16[72,512]{1,0:T(8,128)(2,1)}, bf16[72,512]{1,0:T(8,128)(2,1)}, bf16[72,512]{1,0:T(8,128)(2,1)}, bf16[136,128]{1,0...) custom-call(s32[2]{0:T(128)} %pad_add_fusion.scalars, ...), custom_call_target="tpu_custom_call" | custom-call | tf_op jit(solution)/shard_map/late/pallas_call | solution.py:39
  164.4 1.4 collective-permute-start.55
  165.8 1.5 collective-permute-start.56
  168.2 1.7 collective-permute-start.52
  169.9 2.8 %collective-permute-start.53 = (bf16[72,512]{1,0:T(8,128)(2,1)}, bf16[72,512]{1,0:T(8,128)(2,1)S(1)}, u32[]{:S(2)}, u32[]{:S(2)}) collective-permute-start(bf16[72,512]{1,0:T(8,128)(2,1)} %get-tuple-element.36), channel_id=1, source_target_pairs={{0,16},{1,17},{2,18},{3,19},{4,20},{5,21},{6,22},{7,23},{8,24},{9,... | collective-permute-start | bytes 221192 | tf_op jit(solution)/shard_map/ppermute | solution.py:195
  173.1 2.2 %collective-permute-start.57 = (bf16[136,128]{1,0:T(8,128)(2,1)}, bf16[136,128]{1,0:T(8,128)(2,1)S(1)}, u32[]{:S(2)}, u32[]{:S(2)}) collective-permute-start(bf16[136,128]{1,0:T(8,128)(2,1)} %get-tuple-element.40), channel_id=1, source_target_pairs={{0,2},{1,10},{2,18},{3,26},{4,6},{5,14},{6,22},{7,30},{8,3},{9,11}... | collective-permute-start | bytes 104456 | tf_op jit(solution)/shard_map/ppermute | solution.py:195
  176.9 5.8 %collective-permute-done.57.refs_6_ = bf16[136,128]{1,0:T(8,128)(2,1)S(1)} collective-permute-done((bf16[136,128]{1,0:T(8,128)(2,1)}, bf16[136,128]{1,0:T(8,128)(2,1)S(1)}, u32[]{:S(2)}, u32[]{:S(2)}) %collective-permute-start.57) | collective-permute-done | bytes 34848 | tf_op jit(solution)/shard_map/ppermute | solution.py:195
  183.5 1.8 final.1
  185.2 1.2 slice_bitcast_fusion.6
  186.4 1.2 slice_bitcast_fusion.5
  (236 shorter events, 28.2 us)
Async XLA Ops:
  5.8 28.4 %copy-start.13 = (bf16[136,256]{1,0:T(8,128)(2,1)}, bf16[136,256]{1,0:T(8,128)(2,1)S(1)}, u32[]{:S(2)}) copy-start(bf16[136,256]{1,0:T(8,128)(2,1)S(1)} %maximum_maximum_fusion.refs_0_) | copy-start | bytes 208900
  5.8 17.2 %collective-permute-start = (bf16[136,256]{1,0:T(8,128)(2,1)S(1)}, bf16[136,256]{1,0:T(8,128)(2,1)S(1)}, u32[]{:S(2)}, u32[]{:S(2)}) collective-permute-start(bf16[136,256]{1,0:T(8,128)(2,1)S(1)} %maximum_maximum_fusion.refs_0_), channel_id=1, source_target_pairs={{0,4},{1,5},{2,6},{3,7},{4,0},{5,1},{6,2},{7,3},{8,12},{9,13},{10,... | collective-permute-start | bytes 208904 | tf_op jit(solution)/shard_map/ppermute | solution.py:195
  8.8 14.3 %collective-permute-start.1 = (bf16[136,256]{1,0:T(8,128)(2,1)S(1)}, bf16[136,256]{1,0:T(8,128)(2,1)S(1)}, u32[]{:S(2)}, u32[]{:S(2)}) collective-permute-start(bf16[136,256]{1,0:T(8,128)(2,1)S(1)} %maximum_maximum_fusion.refs_0_), channel_id=1, source_target_pairs={{0,8},{1,9},{2,10},{3,11},{4,12},{5,13},{6,14},{7,15},{8,0},{9,1},... | collective-permute-start | bytes 208904 | tf_op jit(solution)/shard_map/ppermute | solution.py:195
  10.4 16.7 %collective-permute-start.2 = (bf16[136,256]{1,0:T(8,128)(2,1)S(1)}, bf16[136,256]{1,0:T(8,128)(2,1)S(1)}, u32[]{:S(2)}, u32[]{:S(2)}) collective-permute-start(bf16[136,256]{1,0:T(8,128)(2,1)S(1)} %maximum_maximum_fusion.refs_0_), channel_id=1, source_target_pairs={{0,12},{1,13},{2,14},{3,15},{4,8},{5,9},{6,10},{7,11},{8,4},{9,5},... | collective-permute-start | bytes 208904 | tf_op jit(solution)/shard_map/ppermute | solution.py:195
  10.4 18.5 %collective-permute-start.3 = (bf16[136,256]{1,0:T(8,128)(2,1)S(1)}, bf16[136,256]{1,0:T(8,128)(2,1)S(1)}, u32[]{:S(2)}, u32[]{:S(2)}) collective-permute-start(bf16[136,256]{1,0:T(8,128)(2,1)S(1)} %maximum_maximum_fusion.refs_0_), channel_id=1, source_target_pairs={{0,16},{1,17},{2,18},{3,19},{4,20},{5,21},{6,22},{7,23},{8,24},{9,... | collective-permute-start | bytes 208904 | tf_op jit(solution)/shard_map/ppermute | solution.py:195
  14.7 44.4 %collective-permute-start.22 = (bf16[2,128,2048]{2,1,0:T(8,128)(2,1)S(1)}, bf16[2,128,2048]{2,1,0:T(8,128)(2,1)S(1)}, u32[]{:S(2)}, u32[]{:S(2)}) collective-permute-start(bf16[2,128,2048]{2,1,0:T(8,128)(2,1)S(1)} %constant_dynamic-slice_fusion.3), channel_id=1, source_target_pairs={{0,4},{1,5},{2,6},{3,7},{4,0},{5,1},{6,2},{7,3},{8,12},{9,13},{10,... | collective-permute-start | bytes 3145736 | tf_op jit(solution)/shard_map/ppermute | solution.py:195
  23.0 9.2 %collective-permute-start.4 = (bf16[136,256]{1,0:T(8,128)(2,1)S(1)}, bf16[136,256]{1,0:T(8,128)(2,1)S(1)}, u32[]{:S(2)}, u32[]{:S(2)}) collective-permute-start(bf16[136,256]{1,0:T(8,128)(2,1)S(1)} %maximum_maximum_fusion.refs_0_), channel_id=1, source_target_pairs={{0,20},{1,21},{2,22},{3,23},{4,16},{5,17},{6,18},{7,19},{8,28},{9,... | collective-permute-start | bytes 208904 | tf_op jit(solution)/shard_map/ppermute | solution.py:195
  23.2 9.1 %collective-permute-start.5 = (bf16[136,256]{1,0:T(8,128)(2,1)S(1)}, bf16[136,256]{1,0:T(8,128)(2,1)S(1)}, u32[]{:S(2)}, u32[]{:S(2)}) collective-permute-start(bf16[136,256]{1,0:T(8,128)(2,1)S(1)} %maximum_maximum_fusion.refs_0_), channel_id=1, source_target_pairs={{0,24},{1,25},{2,26},{3,27},{4,28},{5,29},{6,30},{7,31},{8,16},{9,... | collective-permute-start | bytes 208904 | tf_op jit(solution)/shard_map/ppermute | solution.py:195
  27.1 7.1 %collective-permute-start.6 = (bf16[136,256]{1,0:T(8,128)(2,1)S(1)}, bf16[136,256]{1,0:T(8,128)(2,1)S(1)}, u32[]{:S(2)}, u32[]{:S(2)}) collective-permute-start(bf16[136,256]{1,0:T(8,128)(2,1)S(1)} %maximum_maximum_fusion.refs_0_), channel_id=1, source_target_pairs={{0,28},{1,29},{2,30},{3,31},{4,24},{5,25},{6,26},{7,27},{8,20},{9,... | collective-permute-start | bytes 208904 | tf_op jit(solution)/shard_map/ppermute | solution.py:195
  38.2 42.6 %copy-start.8 = (bf16[136,256]{1,0:T(8,128)(2,1)S(1)}, bf16[136,256]{1,0:T(8,128)(2,1)}, u32[]{:S(2)}) copy-start(bf16[136,256]{1,0:T(8,128)(2,1)} %solve0.1) | copy-start | bytes 208900
  39.7 4.0 %collective-permute-start.7 = (bf16[72,256]{1,0:T(8,128)(2,1)S(1)}, bf16[72,256]{1,0:T(8,128)(2,1)S(1)}, u32[]{:S(2)}, u32[]{:S(2)}) collective-permute-start(bf16[72,256]{1,0:T(8,128)(2,1)S(1)} %pad_maximum_fusion.11), channel_id=1, source_target_pairs={{0,4},{1,5},{2,6},{3,7},{4,0},{5,1},{6,2},{7,3},{8,12},{9,13},{10,... | collective-permute-start | bytes 110600 | tf_op jit(solution)/shard_map/ppermute | solution.py:195
  41.3 7.9 %collective-permute-start.18 = (bf16[2,72,256]{2,1,0:T(8,128)(2,1)S(1)}, bf16[2,72,256]{2,1,0:T(8,128)(2,1)S(1)}, u32[]{:S(2)}, u32[]{:S(2)}) collective-permute-start(bf16[2,72,256]{2,1,0:T(8,128)(2,1)S(1)} %pad_maximum_fusion.10), channel_id=1, source_target_pairs={{0,4},{1,5},{2,6},{3,7},{4,0},{5,1},{6,2},{7,3},{8,12},{9,13},{10,... | collective-permute-start | bytes 221192 | tf_op jit(solution)/shard_map/ppermute | solution.py:195
  43.8 7.0 %collective-permute-start.8 = (bf16[72,512]{1,0:T(8,128)(2,1)S(1)}, bf16[72,512]{1,0:T(8,128)(2,1)S(1)}, u32[]{:S(2)}, u32[]{:S(2)}) collective-permute-start(bf16[72,512]{1,0:T(8,128)(2,1)S(1)} %maximum_select_fusion.refs_0_), channel_id=1, source_target_pairs={{0,8},{1,9},{2,10},{3,11},{4,12},{5,13},{6,14},{7,15},{8,0},{9,1},... | collective-permute-start | bytes 221192 | tf_op jit(solution)/shard_map/ppermute | solution.py:195
  45.2 8.1 %collective-permute-start.9 = (bf16[72,512]{1,0:T(8,128)(2,1)S(1)}, bf16[72,512]{1,0:T(8,128)(2,1)S(1)}, u32[]{:S(2)}, u32[]{:S(2)}) collective-permute-start(bf16[72,512]{1,0:T(8,128)(2,1)S(1)} %maximum_select_fusion.refs_0_), channel_id=1, source_target_pairs={{0,16},{1,17},{2,18},{3,19},{4,20},{5,21},{6,22},{7,23},{8,24},{9,... | collective-permute-start | bytes 221192 | tf_op jit(solution)/shard_map/ppermute | solution.py:195
  45.8 9.1 %collective-permute-start.10 = (bf16[72,512]{1,0:T(8,128)(2,1)S(1)}, bf16[72,512]{1,0:T(8,128)(2,1)}, u32[]{:S(2)}, u32[]{:S(2)}) collective-permute-start(bf16[72,512]{1,0:T(8,128)(2,1)S(1)} %maximum_select_fusion.refs_0_), channel_id=1, source_target_pairs={{0,24},{1,25},{2,26},{3,27},{4,28},{5,29},{6,30},{7,31},{8,16},{9,... | collective-permute-start | bytes 221192 | tf_op jit(solution)/shard_map/ppermute | solution.py:195
  49.3 9.1 %collective-permute-start.12 = (bf16[1,256,512]{2,1,0:T(8,128)(2,1)S(1)}, bf16[1,256,512]{2,1,0:T(8,128)(2,1)}, u32[]{:S(2)}, u32[]{:S(2)}) collective-permute-start(bf16[1,256,512]{2,1,0:T(8,128)(2,1)S(1)} %slice.87.refs_4_), channel_id=1, source_target_pairs={{0,2},{1,3},{2,0},{3,1},{4,6},{5,7},{6,4},{7,5},{8,10},{9,11},{10,... | collective-permute-start | bytes 786440 | tf_op jit(solution)/shard_map/ppermute | solution.py:195
  51.5 6.9 %collective-permute-start.11 = (bf16[1,256,512]{2,1,0:T(8,128)(2,1)S(1)}, bf16[1,256,512]{2,1,0:T(8,128)(2,1)}, u32[]{:S(2)}, u32[]{:S(2)}) collective-permute-start(bf16[1,256,512]{2,1,0:T(8,128)(2,1)S(1)} %slice.87.refs_4_), channel_id=1, source_target_pairs={{0,1},{1,0},{2,3},{3,2},{4,5},{5,4},{6,7},{7,6},{8,9},{9,8},{10,11... | collective-permute-start | bytes 786440 | tf_op jit(solution)/shard_map/ppermute | solution.py:195
  52.6 43.6 %copy-start = (bf16[2,256,512]{2,1,0:T(8,128)(2,1)}, bf16[2,256,512]{2,1,0:T(8,128)(2,1)S(1)}, u32[]{:S(2)}) copy-start(bf16[2,256,512]{2,1,0:T(8,128)(2,1)S(1)} %slice.97.refs_4_) | copy-start | bytes 1572868
  53.3 9.2 %collective-permute-start.14 = (bf16[1,256,512]{2,1,0:T(8,128)(2,1)S(1)}, bf16[1,256,512]{2,1,0:T(8,128)(2,1)}, u32[]{:S(2)}, u32[]{:S(2)}) collective-permute-start(bf16[1,256,512]{2,1,0:T(8,128)(2,1)S(1)} %slice.87.refs_4_), channel_id=1, source_target_pairs={{0,4},{1,5},{2,6},{3,7},{4,0},{5,1},{6,2},{7,3},{8,12},{9,13},{10,... | collective-permute-start | bytes 786440 | tf_op jit(solution)/shard_map/ppermute | solution.py:195
  54.8 14.1 %collective-permute-start.29 = (bf16[2,256,512]{2,1,0:T(8,128)(2,1)S(1)}, bf16[2,256,512]{2,1,0:T(8,128)(2,1)S(1)}, u32[]{:S(2)}, u32[]{:S(2)}) collective-permute-start(bf16[2,256,512]{2,1,0:T(8,128)(2,1)S(1)} %slice.97.refs_4_), channel_id=1, source_target_pairs={{0,2},{1,3},{2,0},{3,1},{4,6},{5,7},{6,4},{7,5},{8,10},{9,11},{10,... | collective-permute-start | bytes 1572872 | tf_op jit(solution)/shard_map/ppermute | solution.py:195
  58.3 6.4 %collective-permute-start.13 = (bf16[1,256,512]{2,1,0:T(8,128)(2,1)}, bf16[1,256,512]{2,1,0:T(8,128)(2,1)}, u32[]{:S(2)}, u32[]{:S(2)}) collective-permute-start(bf16[1,256,512]{2,1,0:T(8,128)(2,1)} %collective-permute-done.12.refs_6_), channel_id=1, source_target_pairs={{0,1},{1,0},{2,3},{3,2},{4,5},{5,4},{6,7},{7,6},{8,9},{9,8},{10,11... | collective-permute-start | bytes 786440 | tf_op jit(solution)/shard_map/ppermute | solution.py:195
  58.4 9.8 %collective-permute-start.16 = (bf16[1,256,512]{2,1,0:T(8,128)(2,1)}, bf16[1,256,512]{2,1,0:T(8,128)(2,1)}, u32[]{:S(2)}, u32[]{:S(2)}) collective-permute-start(bf16[1,256,512]{2,1,0:T(8,128)(2,1)} %collective-permute-done.12.refs_6_), channel_id=1, source_target_pairs={{0,4},{1,5},{2,6},{3,7},{4,0},{5,1},{6,2},{7,3},{8,12},{9,13},{10,... | collective-permute-start | bytes 786440 | tf_op jit(solution)/shard_map/ppermute | solution.py:195
  59.1 32.0 %copy-start.1 = (bf16[2,128,2048]{2,1,0:T(8,128)(2,1)}, bf16[2,128,2048]{2,1,0:T(8,128)(2,1)S(1)}, u32[]{:S(2)}) copy-start(bf16[2,128,2048]{2,1,0:T(8,128)(2,1)S(1)} %collective-permute-done.22.refs_5_) | copy-start | bytes 3145732
  59.1 32.0 %collective-permute-start.23 = (bf16[2,128,2048]{2,1,0:T(8,128)(2,1)S(1)}, bf16[2,128,2048]{2,1,0:T(8,128)(2,1)S(1)}, u32[]{:S(2)}, u32[]{:S(2)}) collective-permute-start(bf16[2,128,2048]{2,1,0:T(8,128)(2,1)S(1)} %collective-permute-done.22.refs_5_), channel_id=1, source_target_pairs={{0,1},{1,0},{2,3},{3,2},{4,5},{5,4},{6,7},{7,6},{8,9},{9,8},{10,11... | collective-permute-start | bytes 3145736 | tf_op jit(solution)/shard_map/ppermute | solution.py:195
  62.6 16.9 %collective-permute-start.31 = (bf16[2,256,512]{2,1,0:T(8,128)(2,1)S(1)}, bf16[2,256,512]{2,1,0:T(8,128)(2,1)}, u32[]{:S(2)}, u32[]{:S(2)}) collective-permute-start(bf16[2,256,512]{2,1,0:T(8,128)(2,1)S(1)} %slice.97.refs_4_), channel_id=1, source_target_pairs={{0,4},{1,5},{2,6},{3,7},{4,0},{5,1},{6,2},{7,3},{8,12},{9,13},{10,... | collective-permute-start | bytes 1572872 | tf_op jit(solution)/shard_map/ppermute | solution.py:195
  64.8 7.2 %collective-permute-start.15 = (bf16[1,256,512]{2,1,0:T(8,128)(2,1)}, bf16[1,256,512]{2,1,0:T(8,128)(2,1)}, u32[]{:S(2)}, u32[]{:S(2)}) collective-permute-start(bf16[1,256,512]{2,1,0:T(8,128)(2,1)} %collective-permute-done.14.refs_8_), channel_id=1, source_target_pairs={{0,1},{1,0},{2,3},{3,2},{4,5},{5,4},{6,7},{7,6},{8,9},{9,8},{10,11... | collective-permute-start | bytes 786440 | tf_op jit(solution)/shard_map/ppermute | solution.py:195
  68.2 3.8 %collective-permute-start.17 = (bf16[1,256,512]{2,1,0:T(8,128)(2,1)}, bf16[1,256,512]{2,1,0:T(8,128)(2,1)}, u32[]{:S(2)}, u32[]{:S(2)}) collective-permute-start(bf16[1,256,512]{2,1,0:T(8,128)(2,1)} %collective-permute-done.16.refs_10_), channel_id=1, source_target_pairs={{0,1},{1,0},{2,3},{3,2},{4,5},{5,4},{6,7},{7,6},{8,9},{9,8},{10,11... | collective-permute-start | bytes 786440 | tf_op jit(solution)/shard_map/ppermute | solution.py:195
  69.0 21.3 %collective-permute-start.33 = (bf16[2,256,512]{2,1,0:T(8,128)(2,1)S(1)}, bf16[2,256,512]{2,1,0:T(8,128)(2,1)}, u32[]{:S(2)}, u32[]{:S(2)}) collective-permute-start(bf16[2,256,512]{2,1,0:T(8,128)(2,1)S(1)} %collective-permute-done.29.refs_6_), channel_id=1, source_target_pairs={{0,4},{1,5},{2,6},{3,7},{4,0},{5,1},{6,2},{7,3},{8,12},{9,13},{10,... | collective-permute-start | bytes 1572872 | tf_op jit(solution)/shard_map/ppermute | solution.py:195
  75.1 5.7 %collective-permute-start.19 = (bf16[72,512]{1,0:T(8,128)(2,1)}, bf16[72,512]{1,0:T(8,128)(2,1)S(1)}, u32[]{:S(2)}, u32[]{:S(2)}) collective-permute-start(bf16[72,512]{1,0:T(8,128)(2,1)} %update10.1.refs_0_), channel_id=1, source_target_pairs={{0,8},{1,9},{2,10},{3,11},{4,12},{5,13},{6,14},{7,15},{8,0},{9,1},... | collective-permute-start | bytes 221192 | tf_op jit(solution)/shard_map/ppermute | solution.py:195
  75.3 7.3 %collective-permute-start.20 = (bf16[72,512]{1,0:T(8,128)(2,1)}, bf16[72,512]{1,0:T(8,128)(2,1)S(1)}, u32[]{:S(2)}, u32[]{:S(2)}) collective-permute-start(bf16[72,512]{1,0:T(8,128)(2,1)} %update10.1.refs_0_), channel_id=1, source_target_pairs={{0,16},{1,17},{2,18},{3,19},{4,20},{5,21},{6,22},{7,23},{8,24},{9,... | collective-permute-start | bytes 221192 | tf_op jit(solution)/shard_map/ppermute | solution.py:195
  79.4 6.4 %collective-permute-start.21 = (bf16[72,512]{1,0:T(8,128)(2,1)}, bf16[72,512]{1,0:T(8,128)(2,1)S(1)}, u32[]{:S(2)}, u32[]{:S(2)}) collective-permute-start(bf16[72,512]{1,0:T(8,128)(2,1)} %update10.1.refs_0_), channel_id=1, source_target_pairs={{0,24},{1,25},{2,26},{3,27},{4,28},{5,29},{6,30},{7,31},{8,16},{9,... | collective-permute-start | bytes 221192 | tf_op jit(solution)/shard_map/ppermute | solution.py:195
  80.9 17.8 %collective-permute-start.28 = (bf16[2,256,512]{2,1,0:T(8,128)(2,1)S(1)}, bf16[2,256,512]{2,1,0:T(8,128)(2,1)}, u32[]{:S(2)}, u32[]{:S(2)}) collective-permute-start(bf16[2,256,512]{2,1,0:T(8,128)(2,1)S(1)} %slice.97.refs_4_), channel_id=1, source_target_pairs={{0,1},{1,0},{2,3},{3,2},{4,5},{5,4},{6,7},{7,6},{8,9},{9,8},{10,11... | collective-permute-start | bytes 1572872 | tf_op jit(solution)/shard_map/ppermute | solution.py:195
  82.6 18.2 %collective-permute-start.30 = (bf16[2,256,512]{2,1,0:T(8,128)(2,1)S(1)}, bf16[2,256,512]{2,1,0:T(8,128)(2,1)}, u32[]{:S(2)}, u32[]{:S(2)}) collective-permute-start(bf16[2,256,512]{2,1,0:T(8,128)(2,1)S(1)} %collective-permute-done.29.refs_6_), channel_id=1, source_target_pairs={{0,1},{1,0},{2,3},{3,2},{4,5},{5,4},{6,7},{7,6},{8,9},{9,8},{10,11... | collective-permute-start | bytes 1572872 | tf_op jit(solution)/shard_map/ppermute | solution.py:195
  85.8 15.1 %collective-permute-start.32 = (bf16[2,256,512]{2,1,0:T(8,128)(2,1)}, bf16[2,256,512]{2,1,0:T(8,128)(2,1)}, u32[]{:S(2)}, u32[]{:S(2)}) collective-permute-start(bf16[2,256,512]{2,1,0:T(8,128)(2,1)} %collective-permute-done.31.refs_8_), channel_id=1, source_target_pairs={{0,1},{1,0},{2,3},{3,2},{4,5},{5,4},{6,7},{7,6},{8,9},{9,8},{10,11... | collective-permute-start | bytes 1572872 | tf_op jit(solution)/shard_map/ppermute | solution.py:195
  90.3 10.6 %collective-permute-start.34 = (bf16[2,256,512]{2,1,0:T(8,128)(2,1)}, bf16[2,256,512]{2,1,0:T(8,128)(2,1)}, u32[]{:S(2)}, u32[]{:S(2)}) collective-permute-start(bf16[2,256,512]{2,1,0:T(8,128)(2,1)} %collective-permute-done.33.refs_10_), channel_id=1, source_target_pairs={{0,1},{1,0},{2,3},{3,2},{4,5},{5,4},{6,7},{7,6},{8,9},{9,8},{10,11... | collective-permute-start | bytes 1572872 | tf_op jit(solution)/shard_map/ppermute | solution.py:195
  97.1 29.7 %copy-start.9 = (bf16[2,64,512]{2,1,0:T(8,128)(2,1)}, bf16[2,64,512]{2,1,0:T(8,128)(2,1)S(1)}, u32[]{:S(2)}) copy-start(bf16[2,64,512]{2,1,0:T(8,128)(2,1)S(1)} %pad_maximum_fusion.9.refs_0_) | copy-start | bytes 393220
  97.1 31.7 %collective-permute-start.24 = (bf16[2,64,512]{2,1,0:T(8,128)(2,1)S(1)}, bf16[2,64,512]{2,1,0:T(8,128)(2,1)S(1)}, u32[]{:S(2)}, u32[]{:S(2)}) collective-permute-start(bf16[2,64,512]{2,1,0:T(8,128)(2,1)S(1)} %pad_maximum_fusion.9.refs_0_), channel_id=1, source_target_pairs={{0,4},{1,5},{2,6},{3,7},{4,0},{5,1},{6,2},{7,3},{8,12},{9,13},{10,... | collective-permute-start | bytes 393224 | tf_op jit(solution)/shard_map/ppermute | solution.py:195
  98.7 30.2 %collective-permute-start.46 = (bf16[2,64,512]{2,1,0:T(8,128)(2,1)S(1)}, bf16[2,64,512]{2,1,0:T(8,128)(2,1)S(1)}, u32[]{:S(2)}, u32[]{:S(2)}) collective-permute-start(bf16[2,64,512]{2,1,0:T(8,128)(2,1)S(1)} %pad_maximum_fusion.9.refs_0_), channel_id=1, source_target_pairs={{0,1},{1,0},{2,3},{3,2},{4,5},{5,4},{6,7},{7,6},{8,9},{9,8},{10,11... | collective-permute-start | bytes 393224 | tf_op jit(solution)/shard_map/ppermute | solution.py:195
  104.6 5.5 %collective-permute-start.25 = (bf16[72,512]{1,0:T(8,128)(2,1)S(1)}, bf16[72,512]{1,0:T(8,128)(2,1)S(1)}, u32[]{:S(2)}, u32[]{:S(2)}) collective-permute-start(bf16[72,512]{1,0:T(8,128)(2,1)S(1)} %copy-done.7), channel_id=1, source_target_pairs={{0,8},{1,9},{2,10},{3,11},{4,12},{5,13},{6,14},{7,15},{8,0},{9,1},... | collective-permute-start | bytes 221192 | tf_op jit(solution)/shard_map/ppermute | solution.py:195
  104.6 17.2 %collective-permute-start.26 = (bf16[72,512]{1,0:T(8,128)(2,1)S(1)}, bf16[72,512]{1,0:T(8,128)(2,1)S(1)}, u32[]{:S(2)}, u32[]{:S(2)}) collective-permute-start(bf16[72,512]{1,0:T(8,128)(2,1)S(1)} %copy-done.7), channel_id=1, source_target_pairs={{0,16},{1,17},{2,18},{3,19},{4,20},{5,21},{6,22},{7,23},{8,24},{9,... | collective-permute-start | bytes 221192 | tf_op jit(solution)/shard_map/ppermute | solution.py:195
  106.3 15.6 %collective-permute-start.27 = (bf16[72,512]{1,0:T(8,128)(2,1)S(1)}, bf16[72,512]{1,0:T(8,128)(2,1)S(1)}, u32[]{:S(2)}, u32[]{:S(2)}) collective-permute-start(bf16[72,512]{1,0:T(8,128)(2,1)S(1)} %copy-done.7), channel_id=1, source_target_pairs={{0,24},{1,25},{2,26},{3,27},{4,28},{5,29},{6,30},{7,31},{8,16},{9,... | collective-permute-start | bytes 221192 | tf_op jit(solution)/shard_map/ppermute | solution.py:195
  110.1 37.2 %collective-permute-start.45 = (bf16[3,128,512]{2,1,0:T(8,128)(2,1)S(1)}, bf16[3,128,512]{2,1,0:T(8,128)(2,1)S(1)}, u32[]{:S(2)}, u32[]{:S(2)}) collective-permute-start(bf16[3,128,512]{2,1,0:T(8,128)(2,1)S(1)} %bitcast.68), channel_id=1, source_target_pairs={{0,0},{1,8},{2,16},{3,24},{4,4},{5,12},{6,20},{7,28},{8,1},{9,9},{... | collective-permute-start | bytes 1179656 | tf_op jit(solution)/shard_map/ppermute | solution.py:195
  121.8 7.1 %collective-permute-start.47 = (bf16[2,64,512]{2,1,0:T(8,128)(2,1)S(1)}, bf16[2,64,512]{2,1,0:T(8,128)(2,1)S(1)}, u32[]{:S(2)}, u32[]{:S(2)}) collective-permute-start(bf16[2,64,512]{2,1,0:T(8,128)(2,1)S(1)} %pad_maximum_fusion.9.refs_0_), channel_id=1, source_target_pairs={{0,2},{1,3},{2,0},{3,1},{4,6},{5,7},{6,4},{7,5},{8,10},{9,11},{10,... | collective-permute-start | bytes 393224 | tf_op jit(solution)/shard_map/ppermute | solution.py:195
  126.8 5.9 %collective-permute-start.35 = (bf16[72,512]{1,0:T(8,128)(2,1)}, bf16[72,512]{1,0:T(8,128)(2,1)S(1)}, u32[]{:S(2)}, u32[]{:S(2)}) collective-permute-start(bf16[72,512]{1,0:T(8,128)(2,1)} %update21.1.refs_0_), channel_id=1, source_target_pairs={{0,8},{1,9},{2,10},{3,11},{4,12},{5,13},{6,14},{7,15},{8,0},{9,1},... | collective-permute-start | bytes 221192 | tf_op jit(solution)/shard_map/ppermute | solution.py:195
  128.9 8.3 %collective-permute-start.36 = (bf16[72,512]{1,0:T(8,128)(2,1)}, bf16[72,512]{1,0:T(8,128)(2,1)S(1)}, u32[]{:S(2)}, u32[]{:S(2)}) collective-permute-start(bf16[72,512]{1,0:T(8,128)(2,1)} %update21.1.refs_0_), channel_id=1, source_target_pairs={{0,16},{1,17},{2,18},{3,19},{4,20},{5,21},{6,22},{7,23},{8,24},{9,... | collective-permute-start | bytes 221192 | tf_op jit(solution)/shard_map/ppermute | solution.py:195
  128.9 13.5 %collective-permute-start.48 = (bf16[2,64,512]{2,1,0:T(8,128)(2,1)S(1)}, bf16[2,64,512]{2,1,0:T(8,128)(2,1)S(1)}, u32[]{:S(2)}, u32[]{:S(2)}) collective-permute-start(bf16[2,64,512]{2,1,0:T(8,128)(2,1)S(1)} %collective-permute-done.46.refs_1_), channel_id=1, source_target_pairs={{0,2},{1,3},{2,0},{3,1},{4,6},{5,7},{6,4},{7,5},{8,10},{9,11},{10,... | collective-permute-start | bytes 393224 | tf_op jit(solution)/shard_map/ppermute | solution.py:195
  129.0 8.4 %collective-permute-start.37 = (bf16[72,512]{1,0:T(8,128)(2,1)}, bf16[72,512]{1,0:T(8,128)(2,1)S(1)}, u32[]{:S(2)}, u32[]{:S(2)}) collective-permute-start(bf16[72,512]{1,0:T(8,128)(2,1)} %update21.1.refs_0_), channel_id=1, source_target_pairs={{0,24},{1,25},{2,26},{3,27},{4,28},{5,29},{6,30},{7,31},{8,16},{9,... | collective-permute-start | bytes 221192 | tf_op jit(solution)/shard_map/ppermute | solution.py:195
  132.7 18.4 %collective-permute-start.49 = (bf16[2,64,512]{2,1,0:T(8,128)(2,1)S(1)}, bf16[2,64,512]{2,1,0:T(8,128)(2,1)S(1)}, u32[]{:S(2)}, u32[]{:S(2)}) collective-permute-start(bf16[2,64,512]{2,1,0:T(8,128)(2,1)S(1)} %collective-permute-done.46.refs_1_), channel_id=1, source_target_pairs={{0,4},{1,5},{2,6},{3,7},{4,0},{5,1},{6,2},{7,3},{8,12},{9,13},{10,... | collective-permute-start | bytes 393224 | tf_op jit(solution)/shard_map/ppermute | solution.py:195
  137.1 16.3 %collective-permute-start.50 = (bf16[2,64,512]{2,1,0:T(8,128)(2,1)S(1)}, bf16[2,64,512]{2,1,0:T(8,128)(2,1)S(1)}, u32[]{:S(2)}, u32[]{:S(2)}) collective-permute-start(bf16[2,64,512]{2,1,0:T(8,128)(2,1)S(1)} %collective-permute-done.47.refs_2_), channel_id=1, source_target_pairs={{0,4},{1,5},{2,6},{3,7},{4,0},{5,1},{6,2},{7,3},{8,12},{9,13},{10,... | collective-permute-start | bytes 393224 | tf_op jit(solution)/shard_map/ppermute | solution.py:195
  142.4 11.9 %collective-permute-start.51 = (bf16[2,64,512]{2,1,0:T(8,128)(2,1)S(1)}, bf16[2,64,512]{2,1,0:T(8,128)(2,1)S(1)}, u32[]{:S(2)}, u32[]{:S(2)}) collective-permute-start(bf16[2,64,512]{2,1,0:T(8,128)(2,1)S(1)} %collective-permute-done.48.refs_3_), channel_id=1, source_target_pairs={{0,4},{1,5},{2,6},{3,7},{4,0},{5,1},{6,2},{7,3},{8,12},{9,13},{10,... | collective-permute-start | bytes 393224 | tf_op jit(solution)/shard_map/ppermute | solution.py:195
  146.8 4.3 %collective-permute-start.38 = (bf16[1,64,512]{2,1,0:T(8,128)(2,1)S(1)}, bf16[1,64,512]{2,1,0:T(8,128)(2,1)S(1)}, u32[]{:S(2)}, u32[]{:S(2)}) collective-permute-start(bf16[1,64,512]{2,1,0:T(8,128)(2,1)S(1)} %get-tuple-element.67.refs_0_), channel_id=1, source_target_pairs={{0,4},{1,5},{2,6},{3,7},{4,0},{5,1},{6,2},{7,3},{8,12},{9,13},{10,... | collective-permute-start | bytes 196616 | tf_op jit(solution)/shard_map/ppermute | solution.py:195
  147.4 3.6 %collective-permute-start.39 = (bf16[1,64,512]{2,1,0:T(8,128)(2,1)S(1)}, bf16[1,64,512]{2,1,0:T(8,128)(2,1)S(1)}, u32[]{:S(2)}, u32[]{:S(2)}) collective-permute-start(bf16[1,64,512]{2,1,0:T(8,128)(2,1)S(1)} %get-tuple-element.67.refs_0_), channel_id=1, source_target_pairs={{0,1},{1,0},{2,3},{3,2},{4,5},{5,4},{6,7},{7,6},{8,9},{9,8},{10,11... | collective-permute-start | bytes 196616 | tf_op jit(solution)/shard_map/ppermute | solution.py:195
  151.0 9.4 %collective-permute-start.40 = (bf16[1,64,512]{2,1,0:T(8,128)(2,1)S(1)}, bf16[1,64,512]{2,1,0:T(8,128)(2,1)S(1)}, u32[]{:S(2)}, u32[]{:S(2)}) collective-permute-start(bf16[1,64,512]{2,1,0:T(8,128)(2,1)S(1)} %get-tuple-element.67.refs_0_), channel_id=1, source_target_pairs={{0,2},{1,3},{2,0},{3,1},{4,6},{5,7},{6,4},{7,5},{8,10},{9,11},{10,... | collective-permute-start | bytes 196616 | tf_op jit(solution)/shard_map/ppermute | solution.py:195
  151.1 9.4 %collective-permute-start.41 = (bf16[1,64,512]{2,1,0:T(8,128)(2,1)S(1)}, bf16[1,64,512]{2,1,0:T(8,128)(2,1)S(1)}, u32[]{:S(2)}, u32[]{:S(2)}) collective-permute-start(bf16[1,64,512]{2,1,0:T(8,128)(2,1)S(1)} %get-tuple-element.67.refs_0_), channel_id=1, source_target_pairs={{0,3},{1,2},{2,1},{3,0},{4,7},{5,6},{6,5},{7,4},{8,11},{9,10},{10,... | collective-permute-start | bytes 196616 | tf_op jit(solution)/shard_map/ppermute | solution.py:195
  151.2 9.3 %collective-permute-start.42 = (bf16[1,64,512]{2,1,0:T(8,128)(2,1)S(1)}, bf16[1,64,512]{2,1,0:T(8,128)(2,1)S(1)}, u32[]{:S(2)}, u32[]{:S(2)}) collective-permute-start(bf16[1,64,512]{2,1,0:T(8,128)(2,1)S(1)} %get-tuple-element.67.refs_0_), channel_id=1, source_target_pairs={{0,5},{1,4},{2,7},{3,6},{4,1},{5,0},{6,3},{7,2},{8,13},{9,12},{10,... | collective-permute-start | bytes 196616 | tf_op jit(solution)/shard_map/ppermute | solution.py:195
  153.4 7.1 %collective-permute-start.43 = (bf16[1,64,512]{2,1,0:T(8,128)(2,1)S(1)}, bf16[1,64,512]{2,1,0:T(8,128)(2,1)S(1)}, u32[]{:S(2)}, u32[]{:S(2)}) collective-permute-start(bf16[1,64,512]{2,1,0:T(8,128)(2,1)S(1)} %get-tuple-element.67.refs_0_), channel_id=1, source_target_pairs={{0,6},{1,7},{2,4},{3,5},{4,2},{5,3},{6,0},{7,1},{8,14},{9,15},{10,... | collective-permute-start | bytes 196616 | tf_op jit(solution)/shard_map/ppermute | solution.py:195
  154.3 6.2 %collective-permute-start.44 = (bf16[1,64,512]{2,1,0:T(8,128)(2,1)S(1)}, bf16[1,64,512]{2,1,0:T(8,128)(2,1)S(1)}, u32[]{:S(2)}, u32[]{:S(2)}) collective-permute-start(bf16[1,64,512]{2,1,0:T(8,128)(2,1)S(1)} %get-tuple-element.67.refs_0_), channel_id=1, source_target_pairs={{0,7},{1,6},{2,5},{3,4},{4,3},{5,2},{6,1},{7,0},{8,15},{9,14},{10,... | collective-permute-start | bytes 196616 | tf_op jit(solution)/shard_map/ppermute | solution.py:195
  164.4 8.6 %collective-permute-start.55 = (bf16[136,128]{1,0:T(8,128)(2,1)}, bf16[136,128]{1,0:T(8,128)(2,1)S(1)}, u32[]{:S(2)}, u32[]{:S(2)}) collective-permute-start(bf16[136,128]{1,0:T(8,128)(2,1)} %get-tuple-element.38), channel_id=1, source_target_pairs={{0,0},{1,8},{2,16},{3,24},{4,4},{5,12},{6,20},{7,28},{8,1},{9,9},{... | collective-permute-start | bytes 104456 | tf_op jit(solution)/shard_map/ppermute | solution.py:195
  165.8 9.4 %collective-permute-start.56 = (bf16[136,128]{1,0:T(8,128)(2,1)}, bf16[136,128]{1,0:T(8,128)(2,1)S(1)}, u32[]{:S(2)}, u32[]{:S(2)}) collective-permute-start(bf16[136,128]{1,0:T(8,128)(2,1)} %get-tuple-element.39), channel_id=1, source_target_pairs={{0,1},{1,9},{2,17},{3,25},{4,5},{5,13},{6,21},{7,29},{8,0},{9,8},{... | collective-permute-start | bytes 104456 | tf_op jit(solution)/shard_map/ppermute | solution.py:195
  168.2 14.6 %collective-permute-start.52 = (bf16[72,512]{1,0:T(8,128)(2,1)}, bf16[72,512]{1,0:T(8,128)(2,1)S(1)}, u32[]{:S(2)}, u32[]{:S(2)}) collective-permute-start(bf16[72,512]{1,0:T(8,128)(2,1)} %get-tuple-element.35), channel_id=1, source_target_pairs={{0,8},{1,9},{2,10},{3,11},{4,12},{5,13},{6,14},{7,15},{8,0},{9,1},... | collective-permute-start | bytes 221192 | tf_op jit(solution)/shard_map/ppermute | solution.py:195
  169.9 12.9 %collective-permute-start.53 = (bf16[72,512]{1,0:T(8,128)(2,1)}, bf16[72,512]{1,0:T(8,128)(2,1)S(1)}, u32[]{:S(2)}, u32[]{:S(2)}) collective-permute-start(bf16[72,512]{1,0:T(8,128)(2,1)} %get-tuple-element.36), channel_id=1, source_target_pairs={{0,16},{1,17},{2,18},{3,19},{4,20},{5,21},{6,22},{7,23},{8,24},{9,... | collective-permute-start | bytes 221192 | tf_op jit(solution)/shard_map/ppermute | solution.py:195
  172.7 10.1 %collective-permute-start.54 = (bf16[72,512]{1,0:T(8,128)(2,1)}, bf16[72,512]{1,0:T(8,128)(2,1)S(1)}, u32[]{:S(2)}, u32[]{:S(2)}) collective-permute-start(bf16[72,512]{1,0:T(8,128)(2,1)} %get-tuple-element.37), channel_id=1, source_target_pairs={{0,24},{1,25},{2,26},{3,27},{4,28},{5,29},{6,30},{7,31},{8,16},{9,... | collective-permute-start | bytes 221192 | tf_op jit(solution)/shard_map/ppermute | solution.py:195
  173.1 9.7 %collective-permute-start.57 = (bf16[136,128]{1,0:T(8,128)(2,1)}, bf16[136,128]{1,0:T(8,128)(2,1)S(1)}, u32[]{:S(2)}, u32[]{:S(2)}) collective-permute-start(bf16[136,128]{1,0:T(8,128)(2,1)} %get-tuple-element.40), channel_id=1, source_target_pairs={{0,2},{1,10},{2,18},{3,26},{4,6},{5,14},{6,22},{7,30},{8,3},{9,11}... | collective-permute-start | bytes 104456 | tf_op jit(solution)/shard_map/ppermute | solution.py:195
  175.3 7.5 %collective-permute-start.58 = (bf16[136,128]{1,0:T(8,128)(2,1)}, bf16[136,128]{1,0:T(8,128)(2,1)S(1)}, u32[]{:S(2)}, u32[]{:S(2)}) collective-permute-start(bf16[136,128]{1,0:T(8,128)(2,1)} %get-tuple-element.41), channel_id=1, source_target_pairs={{0,3},{1,11},{2,19},{3,27},{4,7},{5,15},{6,23},{7,31},{8,2},{9,10}... | collective-permute-start | bytes 104456 | tf_op jit(solution)/shard_map/ppermute | solution.py:195
  (54 other events, 462.0 us)

commit v2 on v0

v2 whole, which is shorter than its diff:
```python
import functools

import jax
import jax.numpy as jnp
from jax import lax
from jax.experimental import pallas as pl
from jax.experimental.pallas import tpu as pltpu
from jax.sharding import PartitionSpec as P

BF16 = jnp.bfloat16
F32 = jnp.float32
PAD = 8
SCRATCH_BYTES = 12 * 2**20


def dot_t(a, b):
    return lax.dot_general(a, b, (((1,), (1,)), ((), ())), preferred_element_type=F32)


def aligned_at(offset, size):
    return pl.ds(pl.multiple_of(offset, size), size)


class Place:
    def __init__(self, row, col):
        self.row, self.col = row, col
        self.z, self.x, self.core = row // 2, row % 2, col % 2


def call(kernel, name, scalars, arrays, outs):
    outs, scratch = outs
    vmem = pl.BlockSpec(memory_space=pltpu.VMEM)

    def body(place, *refs):
        kernel(Place(place[0], place[1]), place, *refs)

    return pl.pallas_call(
        body,
        in_specs=[pl.BlockSpec(memory_space=pltpu.SMEM)] + [vmem] * len(arrays),
        out_specs=[vmem] * len(outs),
        out_shape=[pltpu.VMEM(shape, dtype) for shape, dtype in outs],
        scratch_shapes=[pltpu.VMEM(shape, dtype) for shape, dtype in scratch],
        compiler_params=pltpu.CompilerParams(vmem_limit_bytes=SCRATCH_BYTES),
        name=name,
    )(scalars, *[pltpu.with_memory_space_constraint(a, pltpu.VMEM) for a in arrays])


def prep_kernel(place, scalars, x_ref, y_ref, send, keep, turned):
    steps, _, _ = x_ref.shape
    half, rows = send.shape[1] - PAD, send.shape[2]
    at = lax.broadcasted_iota(jnp.int32, (PAD, rows), 0)
    for s in range(steps):
        stored = scalars[2 + s]
        turned[...] = x_ref[stored].astype(F32).T
        y = jnp.broadcast_to(y_ref[pl.ds(stored, 1), :], (PAD, rows))
        high = y.astype(BF16).astype(F32)
        keep[s, :half, :] = turned[aligned_at(place.x * half, half), :]
        keep[s, half:, :] = jnp.where(at == 0, y, 0.0)
        send[s, :half, :] = turned[aligned_at((1 - place.x) * half, half), :].astype(BF16)
        low = jnp.where(at == 1, y - high, 0.0)
        send[s, half:, :] = jnp.where(at == 0, high, low).astype(BF16)


def merge_kernel(place, scalars, keep, got, first, *bases):
    steps, height, rows = keep.shape
    half = height - PAD
    mine = aligned_at(place.x * rows, rows)
    other = aligned_at((1 - place.x) * rows, rows)
    at = lax.broadcasted_iota(jnp.int32, (PAD, rows), 0)
    for s in range(steps):
        out = first if s == 0 else bases[s - 1]
        tail = got[s, half:, :].astype(F32)
        resp = jnp.where(at == 0, jnp.sum(tail, 0, keepdims=True), 0.0)
        out[:, mine] = keep[s].astype(out.dtype)
        out[:half, other] = got[s, :half, :].astype(out.dtype)
        out[half:, other] = resp.astype(out.dtype)


def gather_tiles(place, tiles, gathered):
    block = tiles[0].shape[1]
    for k, tile in enumerate(tiles):
        gathered[:, aligned_at((place.z ^ k) * block, block)] = tile[...]


def solve_kernel(counts, place, scalars, *refs):
    planes, layer, offsets, extra = counts
    tiles, inverse, refs = refs[:planes], refs[planes], refs[planes + 1 :]
    parts, refs = refs[: len(offsets)], refs[len(offsets) :]
    before, refs = refs[: extra - 1], refs[extra - 1 :] if extra else refs
    out, gathered, other = refs[0], refs[-2], refs[-1]
    rows = inverse.shape[1]
    gather_tiles(place, tiles, gathered)
    for part, (dc, n) in zip(parts, offsets):
        count = part.shape[1]
        other[aligned_at((place.col ^ dc) * count, count), :] = part[n]
    out[:, aligned_at(place.x * rows, rows)] = dot_t(gathered[...], inverse[layer]).astype(BF16)
    theirs = dot_t(gathered[...], other[...]).astype(BF16)
    out[:, aligned_at((1 - place.x) * rows, rows)] = theirs
    if extra:
        copies = refs[1]
        half = copies.shape[1]
        for n, tile in enumerate(before):
            copies[n] = tile[:half, :]
        for n in range(len(before), copies.shape[0]):
            copies[n] = out[:half, :]


def update_kernel(counts, place, scalars, *refs):
    planes, pieces = counts
    tiles, refs = refs[:planes], refs[planes:]
    base, out, gathered, total = refs[-4:]
    gather_tiles(place, tiles, gathered)
    total[...] = base[...]
    for index, lead, where in pieces:
        piece = refs[index]
        rows, width = piece.shape[-2:]
        dx, dc = where(place)
        columns = gathered[:, aligned_at((place.col ^ dc) * width, width)]
        at = aligned_at((place.x ^ dx) * rows, rows)
        total[:, at] = total[:, at] - dot_t(columns, piece[lead])
    out[...] = total[...].astype(out.dtype)


def partial_kernel(counts, place, scalars, *refs):
    planes, tiles, layers, n_factors, has_base, n_arrays = counts
    arrays, refs = refs[:n_arrays], refs[n_arrays:]
    resps, refs = refs[: len(layers)], refs[len(layers) :]
    factors, refs = refs[:n_factors], refs[n_factors:]
    base, refs = (refs[0], refs[1:]) if has_base else (None, refs)
    outs, wide, sums = refs[:-2], refs[-2], refs[-1]
    full, block = wide.shape[1:]
    half = arrays[0].shape[-2]
    trail_rows = factors[0].shape[1]
    own_cols = 2 * half
    height = resps[0].shape[0] - PAD
    packed = own_cols % 128 == 0
    for index, lead, where in tiles:
        x, col = where(place)
        at = aligned_at(col * own_cols + x * half, half)
        for n in range(len(layers)):
            wide[n, at, :] = arrays[index][lead(n)]
    sums[...] = base[...] if has_base else jnp.zeros(sums.shape, F32)
    for k in range(planes):
        to = place.z ^ k
        for n in range(len(layers)):
            own = wide[n, aligned_at(to * own_cols + place.x * half, half), :]
            sums[k, :half, :] += dot_t(own, wide[n])
            sums[k, half : half + PAD, :half] += dot_t(resps[n][height:, :], own)
    for dc, factor in enumerate(factors):
        k = place.z ^ place.col ^ dc
        for n, layer in enumerate(layers):
            columns = wide[n, aligned_at(place.col * own_cols, own_cols), :]
            trail = dot_t(factor[layer], columns)
            if packed:
                per = full // own_cols
                count = trail_rows // per
                for j in range(per):
                    piece = trail[j * count : (j + 1) * count]
                    lanes = slice(j * own_cols, (j + 1) * own_cols)
                    sums[k, half + PAD :, lanes] += piece
            else:
                sums[k, half + PAD :, :own_cols] += trail
            resp = dot_t(resps[n][height:, :], factor[layer])
            sums[k, half : half + PAD, 128 : 128 + trail_rows] += resp
    if len(outs) == 1:
        outs[0][...] = sums[...]
    else:
        for k, out in enumerate(outs):
            out[...] = sums[k].astype(out.dtype)


def final_kernel(scale, place, scalars, *refs):
    slots = refs[:-6]
    x_ref, y_ref, rhs, resp, normal, right = refs[-6:]
    half, full = normal.shape
    trail_rows, own_cols = rhs.shape
    total = slots[0][...].astype(F32)
    for slot in slots[1:]:
        total += slot[...].astype(F32)
    normal[...] = total[:half] * scale
    right[...] = total[half : half + 1, :half] * scale
    resp[...] = y_ref[...] - total[half : half + 1, 128 : 128 + trail_rows]
    trail = total[half + PAD :]
    if own_cols % 128 == 0:
        per = full // own_cols
        count = trail_rows // per
        for j in range(per):
            rows, lanes = slice(j * count, (j + 1) * count), slice(j * own_cols, (j + 1) * own_cols)
            rhs[rows, :] = x_ref[rows, :].astype(F32) - trail[:, lanes]
    else:
        rhs[...] = x_ref[...].astype(F32) - trail[:, :own_cols]


def white_kernel(counts, place, scalars, *refs):
    steps, last_x, first_x, cols = counts
    solved, refs = refs[:steps], refs[steps:]
    late, early, out, resp_out, turned = refs[0], refs[1:-3], refs[-3], refs[-2], refs[-1]
    half = late.shape[1]
    rows = out.shape[1]
    lanes = aligned_at(place.x * rows, rows)
    row_at = lax.broadcasted_iota(jnp.int32, (steps, rows), 0)
    resps = jnp.zeros((steps, rows), F32)
    for s in range(steps):
        if s < steps - 1:
            (a, i), (b, j) = last_x, first_x
            mine = early[a][i, s, :, lanes].astype(F32)
            theirs = early[b][j, s, :, lanes].astype(F32)
            other = jnp.where(place.core == 0, mine, theirs)
        else:
            other = late[(1 - place.x) * cols + place.col, :, lanes].astype(F32)
        turned[aligned_at(place.x * half, half), :] = solved[s][:half, lanes].astype(F32)
        turned[aligned_at((1 - place.x) * half, half), :] = other
        out[s] = turned[...].T.astype(BF16)
        resp = solved[s][half:, lanes].astype(F32)[:1]
        resps = jnp.where(row_at == s, jnp.broadcast_to(resp, (steps, rows)), resps)
    resp_out[...] = resps.astype(BF16)


def shards(
    x_window, y_window, block_order, diag_inverse, panel_window, panel_trail, x_trail, y_trail
):
    steps, rows, own_cols = x_window.shape
    width = panel_window.shape[2]
    n_rows, n_cols = lax.axis_size("row"), lax.axis_size("col")
    planes = n_rows // 2
    place = Place(lax.axis_index("row"), lax.axis_index("col"))
    x, core = place.x, place.core
    half = own_cols // 2
    height = half + PAD
    pair = 2 * rows
    total_rows = rows * n_rows
    full = own_cols * n_cols
    trail_rows = x_trail.shape[0]
    kernels = rows % 128 == 0 and half % 8 == 0
    scalars = jnp.concatenate([jnp.stack([place.row, place.col]), block_order]).astype(jnp.int32)

    def move(array, to):
        table = []
        for r in range(n_rows):
            for c in range(n_cols):
                tr, tc = to(r, c)
                table.append((r * n_cols + c, tr * n_cols + tc))
        return lax.ppermute(array, ("row", "col"), table)

    def flip(array, dr=0, dc=0):
        return move(array, lambda r, c: (r ^ dr, c ^ dc))

    def ordered(own, other, axis):
        return jnp.where(
            x == 0,
            jnp.concatenate([own, other], axis),
            jnp.concatenate([other, own], axis),
        )

    far = []
    bit = n_cols // 2
    while bit > 1:
        far.append((0, bit))
        bit //= 2
    hops = (far + [(1, 0)], [(1, 0)] + far)

    def label(index, which):
        dx = dc = 0
        for stage, (hx, hc) in enumerate(hops[which]):
            if index >> stage & 1:
                dx, dc = dx ^ hx, dc ^ hc
        return dx, dc

    def hop(array, stage):
        def to(r, c):
            hx, hc = hops[c % 2][stage]
            return r ^ hx, c ^ hc

        return move(array, to)

    def finish(start, stage):
        held = start
        for n in range(stage, len(hops[0])):
            held = held + [hop(jnp.concatenate(held, 0) if len(held) > 1 else held[0], n)]
            if n + 1 < len(hops[0]):
                held = [jnp.concatenate(held, 0)]
        return held + [flip(a, dc=1) for a in held]

    def piece_labels(arrays):
        listed = []
        own = len(arrays) // 2
        for side in range(2):
            index = 0
            for n in range(own):
                for lead in range(arrays[n].shape[0]):

                    def where(p, index=index, side=side):
                        (ax, ac), (bx, bc) = label(index, side), label(index, 1 - side)
                        dx = jnp.where(p.core == 0, ax, bx)
                        dc = jnp.where(p.core == 0, ac, bc) ^ side
                        return dx, dc

                    listed.append((side * own + n, lead, where))
                    index += 1
        return listed

    if kernels:
        send, keep = call(
            prep_kernel,
            "prep",
            scalars,
            [x_window, y_window],
            (
                [((steps, height, rows), BF16), ((steps, height, rows), F32)],
                [((own_cols, rows), F32)],
            ),
        )
    else:
        xs = x_window[block_order].transpose(0, 2, 1).astype(F32)
        ys = y_window[block_order][:, None]
        high = ys.astype(BF16).astype(F32)
        fill = jnp.zeros((steps, PAD - 1, rows), F32)
        keep = jnp.concatenate([lax.dynamic_slice_in_dim(xs, x * half, half, 1), ys, fill], 1)
        other = lax.dynamic_slice_in_dim(xs, (1 - x) * half, half, 1)
        send = jnp.concatenate([other, high, ys - high, fill[:, 1:]], 1).astype(BF16)
    got = flip(send, dr=1)
    if kernels:
        residual, *pending = call(
            merge_kernel,
            "merge",
            scalars,
            [keep, got],
            ([((height, pair), BF16)] + [((height, pair), F32)] * (steps - 1), []),
        )
    else:
        resp = got[:, half:].astype(F32).sum(1, keepdims=True)
        theirs = jnp.concatenate([got[:, :half].astype(F32), resp, fill], 1)
        both = ordered(keep, theirs, 2)
        residual, pending = both[0].astype(BF16), list(both[1:])

    part_rows = rows // n_cols

    def partner_rows(first, count):
        part = lax.dynamic_slice(
            diag_inverse, (first, place.col * part_rows, 0), (count, part_rows, total_rows)
        )
        pieces = {0: flip(part, dr=1)}
        bit = n_cols // 2
        while bit:
            pieces |= {dc ^ bit: flip(a, dc=bit) for dc, a in pieces.items()}
            bit //= 2
        return pieces

    partner = [(partner_rows(0, 1), 0)]
    panel_next = hop(panel_window, 0)
    panels = {}
    for s in range(1, steps):
        at = s * (s - 1) // 2
        both = jnp.stack([panel_window[at : at + s], panel_next[at : at + s]])
        got_panels = finish([both], 1)
        panels[s] = (got_panels, piece_labels(got_panels))
        if s == 1:
            later = partner_rows(1, steps - 1)
            partner += [(later, n) for n in range(steps - 1)]

    factor = move(panel_trail.transpose(1, 0, 2), lambda r, c: (2 * c + r % 2, r // 2))
    factors = {0: factor}
    bit = n_cols // 2
    while bit:
        factors |= {dc ^ bit: flip(a, dc=bit) for dc, a in factors.items()}
        bit //= 2
    factors = [factors[dc] for dc in range(n_cols)]

    def spread(tile):
        return [tile] + [flip(tile, dr=2 * k) for k in range(1, planes)]

    def joined(tiles):
        order = place.z ^ jnp.arange(planes)
        return jnp.stack(tiles)[order].transpose(1, 0, 2).reshape(height, -1)

    def solve(s, tiles, before=None, copies=0):
        parts, n = partner[s]
        listed = sorted(parts)
        if kernels:
            outs = [((height, pair), BF16)]
            if copies:
                outs.append(((copies, half, pair), BF16))
            counts = (planes, s, [(dc, n) for dc in listed], 1 + len(before) if copies else 0)
            return call(
                functools.partial(solve_kernel, counts),
                f"solve{s}",
                scalars,
                tiles + [diag_inverse] + [parts[dc] for dc in listed] + (before or []),
                (outs, [((height, total_rows), BF16), ((rows, total_rows), BF16)]),
            )
        order = place.col ^ jnp.arange(n_cols)
        other = jnp.stack([parts[dc][n] for dc in listed])[order].reshape(rows, total_rows)
        both = ordered(diag_inverse[s], other, 0)
        out = dot_t(joined(tiles), both).astype(BF16)
        copied = [t[:half] for t in before or []]
        copied += [out[:half]] * (copies - len(copied))
        return [out, jnp.stack(copied)] if copies else [out]

    def update(s, t, tiles, base, dtype):
        arrays, labels = panels[s]
        if kernels:
            counts = (planes, [(i, (lead, t), where) for i, lead, where in labels])
            return call(
                functools.partial(update_kernel, counts),
                f"update{s}{t}",
                scalars,
                tiles + arrays + [base],
                (
                    [((height, pair), dtype)],
                    [((height, total_rows), BF16), ((height, pair), F32)],
                ),
            )[0]
        gathered, total = joined(tiles), base
        for i, lead, where in labels:
            dx, dc = where(place)
            columns = lax.dynamic_slice_in_dim(gathered, (place.col ^ dc) * width, width, 1)
            at = (x ^ dx) * rows
            now = lax.dynamic_slice_in_dim(total, at, rows, 1)
            now = now - dot_t(columns, arrays[i][lead, t])
            total = lax.dynamic_update_slice_in_dim(total, now, at, 1)
        return total.astype(dtype)

    solved = []
    group = 2 * n_cols
    for s in range(steps):
        copied = None
        tiles = spread(residual)
        if s == steps - 1:
            tile, copied = solve(s, tiles, [], group)
        elif s == steps - 2:
            tile, copied = solve(s, tiles, list(solved), steps - 1)
        else:
            (tile,) = solve(s, tiles)
        solved.append(tile)
        if s == steps - 2:
            early = finish([copied[None]], 0)
        if s == steps - 1:
            table = [
                [r * n_cols + c for r in (2 * z, 2 * z + 1) for c in range(n_cols)]
                for z in range(planes)
            ]
            late = lax.all_to_all(
                copied, ("row", "col"), 0, 0, tiled=True, axis_index_groups=table
            )
        else:
            tiles = spread(tile)
            residual = update(s + 1, s, tiles, pending[s], BF16)
            for later in range(s + 2, steps):
                pending[later - 1] = update(later, s, tiles, pending[later - 1], F32)

    packed = own_cols % 128 == 0
    slot = half + PAD + (trail_rows * own_cols // full if packed else trail_rows)

    def partials(name, layers, arrays, tiles, resps, base, outs):
        counts = (planes, tiles, layers, n_cols, base is not None, len(arrays))
        return call(
            functools.partial(partial_kernel, counts),
            name,
            scalars,
            arrays + resps + factors + ([] if base is None else [base]),
            (outs, [((len(layers), full, pair), BF16), ((planes, slot, full), F32)]),
        )

    early_tiles = []
    for i, lead, where in piece_labels(early):

        def early_at(p, where=where):
            dx, dc = where(p)
            return p.x ^ dx, p.col ^ dc

        early_tiles.append((i, lambda n, lead=lead: (lead, n), early_at))
    late_tiles = [
        (0, lambda n, m=m: m, lambda p, m=m: (m // n_cols, m % n_cols)) for m in range(group)
    ]
    (sums,) = partials(
        "early", tuple(range(steps - 1)), early, early_tiles, solved[:-1], None,
        [((planes, slot, full), F32)],
    )
    slots = partials(
        "late", (steps - 1,), [late], late_tiles, solved[-1:], sums,
        [((slot, full), BF16)] * planes,
    )
    slots = [slots[0]] + [flip(slots[k], dr=2 * k) for k in range(1, planes)]
    scale = 1.0 / (steps * total_rows)
    trail_rhs, trail_resp, normal, right = call(
        functools.partial(final_kernel, scale),
        "final",
        scalars,
        slots + [x_trail, y_trail[None]],
        (
            [
                ((trail_rows, own_cols), F32),
                ((1, trail_rows), F32),
                ((half, full), F32),
                ((1, half), F32),
            ],
            [],
        ),
    )

    flat = [(n, i) for n in range(len(early) // 2) for i in range(early[n].shape[0])]
    last_x, first_x = flat[1 << (len(hops[0]) - 1)], flat[1]
    if kernels:
        whitened, white_resp = call(
            functools.partial(white_kernel, (steps, last_x, first_x, n_cols)),
            "white",
            scalars,
            solved + [late] + early[: len(early) // 2],
            (
                [((steps, rows, own_cols), BF16), ((steps, rows), BF16)],
                [((own_cols, rows), F32)],
            ),
        )
    else:
        outs, resps = [], []
        for s in range(steps):
            if s < steps - 1:
                (a, i), (b, j) = last_x, first_x
                other = jnp.where(core == 0, early[a][i, s], early[b][j, s])
            else:
                other = late[(1 - x) * n_cols + place.col]
            both = ordered(solved[s][:half], other, 0)
            outs.append(lax.dynamic_slice_in_dim(both, x * rows, rows, 1).T)
            resps.append(lax.dynamic_slice_in_dim(solved[s][half], x * rows, rows, 0))
        whitened, white_resp = jnp.stack(outs), jnp.stack(resps)
    return whitened, white_resp, trail_rhs, trail_resp[0], normal, right[0]


def solution(mesh):
    in_specs = (
        P(None, "row", "col"),
        P(None, "row"),
        P(),
        P(None, "row", None),
        P(None, "row", "col"),
        P("row", None, "col"),
        P("row", "col"),
        P("row"),
    )
    out_specs = (
        P(None, "row", "col"),
        P(None, "row"),
        P("row", "col"),
        P("row"),
        P("row", None),
        P("row"),
    )
    return jax.shard_map(shards, mesh=mesh, in_specs=in_specs, out_specs=out_specs, check_vma=False)
```

time: 447 us -> 145 us (0.32)
  blocking collectives: 314 us -> 0 us
  starting transfers between devices: 10.6 us -> 82.8 us
  waiting for transfers between devices: 72.4 us -> 30.7 us
  between operations: 19.8 us -> 0.89 us
  matrix products: 16.5 us -> 0 us
  Pallas kernels: 0 us -> 15.9 us
  local copies, waits for them, and re-layouts: 7.06 us -> 13.5 us
  other arithmetic: 5.95 us -> 0.91 us
    all_gather x12 -> x0, blocking collectives: 297 us -> none  [the longest x3 96.4 us: shards(): lax.all_gather(residual, 'row', axis=0, tiled=True)]
    ppermute x0 -> x42, starting transfers between devices: none -> 79.3 us  [move(): return lax.ppermute(array, ('row', 'col'), table)]
    reduce_scatter x3 -> x0, waiting for transfers between devices: 39.8 us -> none  [the longest x1 20.4 us: shards(): lax.psum_scatter(trail_total.astype(jnp.bfloat16), 'col', scatter_dimensi...]
    ppermute x0 -> x42, waiting for transfers between devices: none -> 28.7 us  [move(): return lax.ppermute(array, ('row', 'col'), table)]
    psum x1 -> x0, waiting for transfers between devices: 25.1 us -> none  [shards(): gram, right, resp_sum = lax.psum((gram, right, trail_resp_total), 'col')]
    psum x3 -> x0, blocking collectives: 17.1 us -> none  [the longest x2 11.3 us: shards(): pending_resp = pending_resp - lax.psum(update_resp, 'col')]
    dot_general x22 -> x0, matrix products: 16.5 us -> none  [the longest x3 5.12 us: shards(): jnp.dot(inverse, whole, preferred_element_type=jnp.float32)]
    pallas_call x0 -> x12, Pallas kernels: none -> 15.9 us  [call(): pl.pallas_call(body, in_specs=[pl.BlockSpec(memory_space=pltpu.SMEM)] + [...]
  transfers between devices with their start and end apart: 7 -> 43, of which waited for: 4 -> 16; matrix products, arithmetic and copies ran while one was open for 3% -> 4% of each run, Pallas kernels for 0% -> 9%
where the time goes in v2:
time: 145 us
  starting transfers between devices  82.8 us (57%)
  waiting for transfers between devices  30.7 us (21%)
  Pallas kernels  15.9 us (11%)
  local copies, waits for them, and re-layouts  13.5 us (9%)
    ppermute x42, starting transfers between devices, move(): return lax.ppermute(array, ('row', 'col'), table)  79.3 us
    ppermute x42, waiting for transfers between devices, move(): return lax.ppermute(array, ('row', 'col'), table)  28.7 us
    pallas_call x12, Pallas kernels, call(): pl.pallas_call(body, in_specs=[pl.BlockSpec(memory_space=pltpu.SMEM)] + [...  15.9 us
    unnamed x30, local copies, waits for them, and re-layouts  9.38 us
    all_to_all x1, starting transfers between devices, shards(): lax.all_to_all(copied, ('row', 'col'), 0, 0, tiled=True, axis_index_group...  3.49 us
  transfers between devices with their start and end apart: 43, of which 16 were waited for; matrix products, arithmetic and copies ran while one was open for 4% of the time, Pallas kernels for 9%

profile of v2, /device:TPU:0, one launch (start us, length us, event | category | flops | bytes accessed | tf_op | source)
XLA Modules:
  0.0 144.7 jit_solution(15887555698897147686)
XLA Ops:
  0.6 3.1 %collective-permute-start.11 = (bf16[3,256,512]{2,1,0:T(8,128)(2,1)}, bf16[3,256,512]{2,1,0:T(8,128)(2,1)S(1)}, u32[]{:S(2)}, u32[]{:S(2)}) collective-permute-start(bf16[3,256,512]{2,1,0:T(8,128)(2,1)} %param.12), channel_id=1, source_target_pairs={{0,2},{1,5},{2,0},{3,7},{4,6},{5,1},{6,4},{7,3},{8,10},{9,13},{10,... | collective-permute-start | bytes 2359304 | tf_op jit(solution)/shard_map/ppermute | solution.py:243
  3.7 0.7 pad_add_fusion.place
  4.4 0.9 copy-done.7
  5.4 0.7 copy-done.9
  6.0 0.7 prep.1
  6.8 1.6 %collective-permute-start = (bf16[3,72,256]{2,1,0:T(8,128)(2,1)S(1)}, bf16[3,72,256]{2,1,0:T(8,128)(2,1)S(1)}, u32[]{:S(2)}, u32[]{:S(2)}) collective-permute-start(bf16[3,72,256]{2,1,0:T(8,128)(2,1)S(1)} %get-tuple-element.26), channel_id=1, source_target_pairs={{0,4},{1,5},{2,6},{3,7},{4,0},{5,1},{6,2},{7,3},{8,12},{9,13},{10,... | collective-permute-start | bytes 331784 | tf_op jit(solution)/shard_map/ppermute | solution.py:243
  8.3 1.0 constant_dynamic-slice_fusion.1
  9.9 1.1 constant_dynamic-slice_fusion
  11.0 1.6 %collective-permute-start.18 = (bf16[2,64,2048]{2,1,0:T(8,128)(2,1)S(1)}, bf16[2,64,2048]{2,1,0:T(8,128)(2,1)S(1)}, u32[]{:S(2)}, u32[]{:S(2)}) collective-permute-start(bf16[2,64,2048]{2,1,0:T(8,128)(2,1)S(1)} %constant_dynamic-slice_fusion), channel_id=1, source_target_pairs={{0,4},{1,5},{2,6},{3,7},{4,0},{5,1},{6,2},{7,3},{8,12},{9,13},{10,... | collective-permute-start | bytes 1572872 | tf_op jit(solution)/shard_map/ppermute | solution.py:243
  12.5 1.1 slice_bitcast_fusion.1
  14.0 2.1 %collective-permute-start.25 = (bf16[2,2,256,512]{3,2,1,0:T(8,128)(2,1)S(1)}, bf16[2,2,256,512]{3,2,1,0:T(8,128)(2,1)S(1)}, u32[]{:S(2)}, u32[]{:S(2)}) collective-permute-start(bf16[2,2,256,512]{3,2,1,0:T(8,128)(2,1)S(1)} %pad_maximum_fusion.refs_4_), channel_id=1, source_target_pairs={{0,4},{1,3},{2,6},{3,1},{4,0},{5,7},{6,2},{7,5},{8,12},{9,11},{10,... | collective-permute-start | bytes 3145736 | tf_op jit(solution)/shard_map/ppermute | solution.py:243
  16.1 1.0 slice_bitcast_fusion.3
  17.7 1.6 %collective-permute-start.1 = (bf16[72,512]{1,0:T(8,128)(2,1)S(1)}, bf16[72,512]{1,0:T(8,128)(2,1)S(1)}, u32[]{:S(2)}, u32[]{:S(2)}) collective-permute-start(bf16[72,512]{1,0:T(8,128)(2,1)S(1)} %get-tuple-element.27.refs_0_), channel_id=1, source_target_pairs={{0,8},{1,9},{2,10},{3,11},{4,12},{5,13},{6,14},{7,15},{8,0},{9,1},... | collective-permute-start | bytes 221192 | tf_op jit(solution)/shard_map/ppermute | solution.py:243
  19.3 2.6 %collective-permute-start.2 = (bf16[72,512]{1,0:T(8,128)(2,1)S(1)}, bf16[72,512]{1,0:T(8,128)(2,1)S(1)}, u32[]{:S(2)}, u32[]{:S(2)}) collective-permute-start(bf16[72,512]{1,0:T(8,128)(2,1)S(1)} %get-tuple-element.27.refs_0_), channel_id=1, source_target_pairs={{0,16},{1,17},{2,18},{3,19},{4,20},{5,21},{6,22},{7,23},{8,24},{9,... | collective-permute-start | bytes 221192 | tf_op jit(solution)/shard_map/ppermute | solution.py:243
  21.9 1.5 %collective-permute-start.6 = (bf16[1,64,2048]{2,1,0:T(8,128)(2,1)S(1)}, bf16[1,64,2048]{2,1,0:T(8,128)(2,1)S(1)}, u32[]{:S(2)}, u32[]{:S(2)}) collective-permute-start(bf16[1,64,2048]{2,1,0:T(8,128)(2,1)S(1)} %collective-permute-done.4.refs_5_), channel_id=1, source_target_pairs={{0,2},{1,3},{2,0},{3,1},{4,6},{5,7},{6,4},{7,5},{8,10},{9,11},{10,... | collective-permute-start | bytes 786440 | tf_op jit(solution)/shard_map/ppermute | solution.py:243
  23.4 2.2 %collective-permute-start.3 = (bf16[72,512]{1,0:T(8,128)(2,1)S(1)}, bf16[72,512]{1,0:T(8,128)(2,1)S(1)}, u32[]{:S(2)}, u32[]{:S(2)}) collective-permute-start(bf16[72,512]{1,0:T(8,128)(2,1)S(1)} %get-tuple-element.27.refs_0_), channel_id=1, source_target_pairs={{0,24},{1,25},{2,26},{3,27},{4,28},{5,29},{6,30},{7,31},{8,16},{9,... | collective-permute-start | bytes 221192 | tf_op jit(solution)/shard_map/ppermute | solution.py:243
  26.3 3.3 %collective-permute-done.3.refs_3_ = bf16[72,512]{1,0:T(8,128)(2,1)S(1)} collective-permute-done((bf16[72,512]{1,0:T(8,128)(2,1)S(1)}, bf16[72,512]{1,0:T(8,128)(2,1)S(1)}, u32[]{:S(2)}, u32[]{:S(2)}) %collective-permute-start.3) | collective-permute-done | bytes 73760 | tf_op jit(solution)/shard_map/ppermute | solution.py:243
  29.7 1.8 %collective-permute-start.5 = (bf16[1,64,2048]{2,1,0:T(8,128)(2,1)S(1)}, bf16[1,64,2048]{2,1,0:T(8,128)(2,1)S(1)}, u32[]{:S(2)}, u32[]{:S(2)}) collective-permute-start(bf16[1,64,2048]{2,1,0:T(8,128)(2,1)S(1)} %collective-permute-done.4.refs_5_), channel_id=1, source_target_pairs={{0,1},{1,0},{2,3},{3,2},{4,5},{5,4},{6,7},{7,6},{8,9},{9,8},{10,11... | collective-permute-start | bytes 786440 | tf_op jit(solution)/shard_map/ppermute | solution.py:243
  31.4 5.2 %collective-permute-start.7 = (bf16[1,64,2048]{2,1,0:T(8,128)(2,1)S(1)}, bf16[1,64,2048]{2,1,0:T(8,128)(2,1)S(1)}, u32[]{:S(2)}, u32[]{:S(2)}) collective-permute-start(bf16[1,64,2048]{2,1,0:T(8,128)(2,1)S(1)} %collective-permute-done.6.refs_7_), channel_id=1, source_target_pairs={{0,1},{1,0},{2,3},{3,2},{4,5},{5,4},{6,7},{7,6},{8,9},{9,8},{10,11... | collective-permute-start | bytes 786440 | tf_op jit(solution)/shard_map/ppermute | solution.py:243
  36.6 1.2 collective-permute-done.7.refs_8_
  37.8 1.3 solve0.1.refs_0_.refs_9_.refs_4_
  39.1 1.6 %collective-permute-start.8 = (bf16[72,512]{1,0:T(8,128)(2,1)S(1)}, bf16[72,512]{1,0:T(8,128)(2,1)S(1)}, u32[]{:S(2)}, u32[]{:S(2)}) collective-permute-start(bf16[72,512]{1,0:T(8,128)(2,1)S(1)} %solve0.1.refs_0_.refs_9_.refs_4_), channel_id=1, source_target_pairs={{0,8},{1,9},{2,10},{3,11},{4,12},{5,13},{6,14},{7,15},{8,0},{9,1},... | collective-permute-start | bytes 221192 | tf_op jit(solution)/shard_map/ppermute | solution.py:243
  40.7 2.6 %collective-permute-start.9 = (bf16[72,512]{1,0:T(8,128)(2,1)S(1)}, bf16[72,512]{1,0:T(8,128)(2,1)S(1)}, u32[]{:S(2)}, u32[]{:S(2)}) collective-permute-start(bf16[72,512]{1,0:T(8,128)(2,1)S(1)} %solve0.1.refs_0_.refs_9_.refs_4_), channel_id=1, source_target_pairs={{0,16},{1,17},{2,18},{3,19},{4,20},{5,21},{6,22},{7,23},{8,24},{9,... | collective-permute-start | bytes 221192 | tf_op jit(solution)/shard_map/ppermute | solution.py:243
  43.3 1.7 %collective-permute-start.20 = (bf16[2,64,2048]{2,1,0:T(8,128)(2,1)S(1)}, bf16[2,64,2048]{2,1,0:T(8,128)(2,1)S(1)}, u32[]{:S(2)}, u32[]{:S(2)}) collective-permute-start(bf16[2,64,2048]{2,1,0:T(8,128)(2,1)S(1)} %collective-permute-done.18.refs_5_), channel_id=1, source_target_pairs={{0,2},{1,3},{2,0},{3,1},{4,6},{5,7},{6,4},{7,5},{8,10},{9,11},{10,... | collective-permute-start | bytes 1572872 | tf_op jit(solution)/shard_map/ppermute | solution.py:243
  45.1 2.5 %collective-permute-done.9.refs_2_ = bf16[72,512]{1,0:T(8,128)(2,1)S(1)} collective-permute-done((bf16[72,512]{1,0:T(8,128)(2,1)S(1)}, bf16[72,512]{1,0:T(8,128)(2,1)S(1)}, u32[]{:S(2)}, u32[]{:S(2)}) %collective-permute-start.9) | collective-permute-done | bytes 73760 | tf_op jit(solution)/shard_map/ppermute | solution.py:243
  47.5 2.5 %collective-permute-start.10 = (bf16[72,512]{1,0:T(8,128)(2,1)S(1)}, bf16[72,512]{1,0:T(8,128)(2,1)S(1)}, u32[]{:S(2)}, u32[]{:S(2)}) collective-permute-start(bf16[72,512]{1,0:T(8,128)(2,1)S(1)} %solve0.1.refs_0_.refs_9_.refs_4_), channel_id=1, source_target_pairs={{0,24},{1,25},{2,26},{3,27},{4,28},{5,29},{6,30},{7,31},{8,16},{9,... | collective-permute-start | bytes 221192 | tf_op jit(solution)/shard_map/ppermute | solution.py:243
  50.0 3.6 %collective-permute-done.10.refs_3_ = bf16[72,512]{1,0:T(8,128)(2,1)S(1)} collective-permute-done((bf16[72,512]{1,0:T(8,128)(2,1)S(1)}, bf16[72,512]{1,0:T(8,128)(2,1)S(1)}, u32[]{:S(2)}, u32[]{:S(2)}) %collective-permute-start.10) | collective-permute-done | bytes 73760 | tf_op jit(solution)/shard_map/ppermute | solution.py:243
  54.2 2.8 %collective-permute-done.20.refs_7_ = bf16[2,64,2048]{2,1,0:T(8,128)(2,1)S(1)} collective-permute-done((bf16[2,64,2048]{2,1,0:T(8,128)(2,1)S(1)}, bf16[2,64,2048]{2,1,0:T(8,128)(2,1)S(1)}, u32[]{:S(2)}, u32[]{:S(2)}) %collective-permute-start.20) | collective-permute-done | bytes 524320 | tf_op jit(solution)/shard_map/ppermute | solution.py:243
  57.5 0.7 collective-permute-start.33
  58.2 1.3 update10.1.refs_0_
  59.5 7.8 %collective-permute-start.15 = (bf16[72,512]{1,0:T(8,128)(2,1)S(1)}, bf16[72,512]{1,0:T(8,128)(2,1)S(1)}, u32[]{:S(2)}, u32[]{:S(2)}) collective-permute-start(bf16[72,512]{1,0:T(8,128)(2,1)S(1)} %update10.1.refs_0_), channel_id=1, source_target_pairs={{0,8},{1,9},{2,10},{3,11},{4,12},{5,13},{6,14},{7,15},{8,0},{9,1},... | collective-permute-start | bytes 221192 | tf_op jit(solution)/shard_map/ppermute | solution.py:243
  67.4 12.5 %collective-permute-start.16 = (bf16[72,512]{1,0:T(8,128)(2,1)S(1)}, bf16[72,512]{1,0:T(8,128)(2,1)S(1)}, u32[]{:S(2)}, u32[]{:S(2)}) collective-permute-start(bf16[72,512]{1,0:T(8,128)(2,1)S(1)} %update10.1.refs_0_), channel_id=1, source_target_pairs={{0,16},{1,17},{2,18},{3,19},{4,20},{5,21},{6,22},{7,23},{8,24},{9,... | collective-permute-start | bytes 221192 | tf_op jit(solution)/shard_map/ppermute | solution.py:243
  79.9 1.5 %collective-permute-start.17 = (bf16[72,512]{1,0:T(8,128)(2,1)S(1)}, bf16[72,512]{1,0:T(8,128)(2,1)S(1)}, u32[]{:S(2)}, u32[]{:S(2)}) collective-permute-start(bf16[72,512]{1,0:T(8,128)(2,1)S(1)} %update10.1.refs_0_), channel_id=1, source_target_pairs={{0,24},{1,25},{2,26},{3,27},{4,28},{5,29},{6,30},{7,31},{8,16},{9,... | collective-permute-start | bytes 221192 | tf_op jit(solution)/shard_map/ppermute | solution.py:243
  81.4 4.8 %collective-permute-start.35 = (bf16[3,128,512]{2,1,0:T(8,128)(2,1)S(1)}, bf16[3,128,512]{2,1,0:T(8,128)(2,1)S(1)}, u32[]{:S(2)}, u32[]{:S(2)}) collective-permute-start(bf16[3,128,512]{2,1,0:T(8,128)(2,1)S(1)} %collective-permute-done.33.refs_6_.refs_2_), channel_id=1, source_target_pairs={{0,2},{1,3},{2,0},{3,1},{4,6},{5,7},{6,4},{7,5},{8,10},{9,11},{10,... | collective-permute-start | bytes 1179656 | tf_op jit(solution)/shard_map/ppermute | solution.py:243
  86.2 0.8 collective-permute-done.17.refs_3_
  87.0 1.3 solve1.1
  88.4 2.5 %collective-permute-start.31 = (bf16[1,2,64,512]{3,2,1,0:T(8,128)(2,1)S(1)}, bf16[1,2,64,512]{3,2,1,0:T(8,128)(2,1)S(1)}, u32[]{:S(2)}, u32[]{:S(2)}) collective-permute-start(bf16[1,2,64,512]{3,2,1,0:T(8,128)(2,1)S(1)} %bitcast.17), channel_id=1, source_target_pairs={{0,2},{1,5},{2,0},{3,7},{4,6},{5,1},{6,4},{7,3},{8,10},{9,13},{10,... | collective-permute-start | bytes 393224 | tf_op jit(solution)/shard_map/ppermute | solution.py:243
  91.4 3.3 %collective-permute-start.23 = (bf16[72,512]{1,0:T(8,128)(2,1)S(1)}, bf16[72,512]{1,0:T(8,128)(2,1)S(1)}, u32[]{:S(2)}, u32[]{:S(2)}) collective-permute-start(bf16[72,512]{1,0:T(8,128)(2,1)S(1)} %get-tuple-element.29.refs_0_.refs_1_.refs_5_), channel_id=1, source_target_pairs={{0,16},{1,17},{2,18},{3,19},{4,20},{5,21},{6,22},{7,23},{8,24},{9,... | collective-permute-start | bytes 221192 | tf_op jit(solution)/shard_map/ppermute | solution.py:243
  95.3 1.3 update20.1.refs_8_
  96.6 3.3 %collective-permute-done.23.refs_2_ = bf16[72,512]{1,0:T(8,128)(2,1)S(1)} collective-permute-done((bf16[72,512]{1,0:T(8,128)(2,1)S(1)}, bf16[72,512]{1,0:T(8,128)(2,1)S(1)}, u32[]{:S(2)}, u32[]{:S(2)}) %collective-permute-start.23) | collective-permute-done | bytes 73760 | tf_op jit(solution)/shard_map/ppermute | solution.py:243
  99.9 1.0 collective-permute-done.24.refs_3_
  101.0 1.3 update21.1.refs_0_
  102.3 1.3 collective-permute-start.28
  103.6 1.0 collective-permute-start.29
  104.6 2.2 %collective-permute-start.30 = (bf16[72,512]{1,0:T(8,128)(2,1)S(1)}, bf16[72,512]{1,0:T(8,128)(2,1)S(1)}, u32[]{:S(2)}, u32[]{:S(2)}) collective-permute-start(bf16[72,512]{1,0:T(8,128)(2,1)S(1)} %update21.1.refs_0_), channel_id=1, source_target_pairs={{0,24},{1,25},{2,26},{3,27},{4,28},{5,29},{6,30},{7,31},{8,16},{9,... | collective-permute-start | bytes 221192 | tf_op jit(solution)/shard_map/ppermute | solution.py:243
  106.8 1.3 collective-permute-start.32
  108.1 3.8 %collective-permute-done.29.refs_2_ = bf16[72,512]{1,0:T(8,128)(2,1)S(1)} collective-permute-done((bf16[72,512]{1,0:T(8,128)(2,1)S(1)}, bf16[72,512]{1,0:T(8,128)(2,1)S(1)}, u32[]{:S(2)}, u32[]{:S(2)}) %collective-permute-start.29) | collective-permute-done | bytes 73760 | tf_op jit(solution)/shard_map/ppermute | solution.py:243
  111.9 2.2 %solve2.1 = (bf16[72,512]{1,0:T(8,128)(2,1)S(1)}, bf16[8,64,512]{2,1,0:T(8,128)(2,1)}) custom-call(s32[5]{0:T(128)S(1)} %pad_add_fusion.place, bf16[72,512]{1,0:T(8,128)(2,1)S(1)} %update21.1.refs_0_, bf16[72,512]{1,0:T(8,128)(2,1)S(1)} %collective-permute-done.28.refs_1_, bf16[72,512]{1,0:T(8,128)(2,1)S(1)} %collective-permute-done.29.refs_2_, ...), custom_call_target="tpu_custom_call" | custom-call | tf_op jit(solution)/shard_map/solve2/pallas_call | solution.py:37
  114.7 3.5 %all-to-all-start = ((bf16[8,64,512]{2,1,0:T(8,128)(2,1)}), bf16[8,64,512]{2,1,0:T(8,128)(2,1)S(1)}, u32[]{:S(2)}, u32[]{:S(2)}) async-start(bf16[8,64,512]{2,1,0:T(8,128)(2,1)} %get-tuple-element.32), calls=%async_computation | async-start | bytes 1048576 | tf_op jit(solution)/shard_map/all_to_all | solution.py:442
  119.3 0.8 collective-permute-done.34.refs_7_.refs_3_
  121.4 0.9 copy-done.2
  122.3 2.7 %early.1.refs_6_ = f32[4,104,512]{2,1,0:T(8,128)S(1)} custom-call(s32[5]{0:T(128)S(1)} %pad_add_fusion.place, bf16[2,2,64,512]{3,2,1,0:T(8,128)(2,1)S(1)} %pad_maximum_fusion.2.refs_4_.refs_0_, bf16[2,2,64,512]{3,2,1,0:T(8,128)(2,1)S(1)} %collective-permute-done.32.refs_5_.refs_1_, bf16[2,2,64,512]{3,2,1,0:T(8,128)(2,1)S(1)} %collective-permute-done.37.refs_2_, ...), custom_call_target="tpu_custom_call" | custom-call | tf_op jit(solution)/shard_map/early/pallas_call | solution.py:37
  125.0 2.0 %all-to-all-done.refs_3_.refs_0_ = bf16[8,64,512]{2,1,0:T(8,128)(2,1)S(1)} async-done(((bf16[8,64,512]{2,1,0:T(8,128)(2,1)}), bf16[8,64,512]{2,1,0:T(8,128)(2,1)S(1)}, u32[]{:S(2)}, u32[]{:S(2)}) %all-to-all-start) | async-done | bytes 524320 | tf_op jit(solution)/shard_map/all_to_all | solution.py:442
  127.0 0.9 copy-done.5
  127.9 1.8 %late.1 = (bf16[104,512]{1,0:T(8,128)(2,1)S(1)}, bf16[104,512]{1,0:T(8,128)(2,1)S(1)}, bf16[104,512]{1,0:T(8,128)(2,1)S(1)}, bf16[104,512]{1,0:T(8,128)(2,1)S(1)}) custom-call(s32[5]{0:T(128)S(1)} %pad_add_fusion.place, bf16[8,64,512]{2,1,0:T(8,128)(2,1)S(1)} %all-to-all-done.refs_3_.refs_0_, bf16[72,512]{1,0:T(8,128)(2,1)S(1)} %copy-done.5, ...), custom_call_target="tpu_custom_call" | custom-call | tf_op jit(solution)/shard_map/late/pallas_call | solution.py:37
  129.6 1.4 collective-permute-start.39
  131.1 1.4 collective-permute-start.40
  132.4 1.6 %collective-permute-start.41 = (bf16[104,512]{1,0:T(8,128)(2,1)S(1)}, bf16[104,512]{1,0:T(8,128)(2,1)S(1)}, u32[]{:S(2)}, u32[]{:S(2)}) collective-permute-start(bf16[104,512]{1,0:T(8,128)(2,1)S(1)} %get-tuple-element.39), channel_id=1, source_target_pairs={{0,24},{1,25},{2,26},{3,27},{4,28},{5,29},{6,30},{7,31},{8,16},{9,... | collective-permute-start | bytes 319496 | tf_op jit(solution)/shard_map/ppermute | solution.py:243
  134.1 0.9 copy-done.3
  135.0 0.9 copy-done.6
  135.9 0.7 white.1
  136.6 0.7 copy.14
  137.9 3.9 %collective-permute-done.40.refs_2_ = bf16[104,512]{1,0:T(8,128)(2,1)S(1)} collective-permute-done((bf16[104,512]{1,0:T(8,128)(2,1)S(1)}, bf16[104,512]{1,0:T(8,128)(2,1)S(1)}, u32[]{:S(2)}, u32[]{:S(2)}) %collective-permute-start.40) | collective-permute-done | bytes 106528 | tf_op jit(solution)/shard_map/ppermute | solution.py:243
  143.5 0.7 copy.18
  (74 shorter events, 10.3 us)
Async XLA Ops:
  0.6 13.2 %collective-permute-start.11 = (bf16[3,256,512]{2,1,0:T(8,128)(2,1)}, bf16[3,256,512]{2,1,0:T(8,128)(2,1)S(1)}, u32[]{:S(2)}, u32[]{:S(2)}) collective-permute-start(bf16[3,256,512]{2,1,0:T(8,128)(2,1)} %param.12), channel_id=1, source_target_pairs={{0,2},{1,5},{2,0},{3,7},{4,6},{5,1},{6,4},{7,3},{8,10},{9,13},{10,... | collective-permute-start | bytes 2359304 | tf_op jit(solution)/shard_map/ppermute | solution.py:243
  4.4 0.9 copy-start.7
  5.4 0.7 copy-start.9
  6.8 10.3 %collective-permute-start = (bf16[3,72,256]{2,1,0:T(8,128)(2,1)S(1)}, bf16[3,72,256]{2,1,0:T(8,128)(2,1)S(1)}, u32[]{:S(2)}, u32[]{:S(2)}) collective-permute-start(bf16[3,72,256]{2,1,0:T(8,128)(2,1)S(1)} %get-tuple-element.26), channel_id=1, source_target_pairs={{0,4},{1,5},{2,6},{3,7},{4,0},{5,1},{6,2},{7,3},{8,12},{9,13},{10,... | collective-permute-start | bytes 331784 | tf_op jit(solution)/shard_map/ppermute | solution.py:243
  9.3 12.6 %collective-permute-start.4 = (bf16[1,64,2048]{2,1,0:T(8,128)(2,1)S(1)}, bf16[1,64,2048]{2,1,0:T(8,128)(2,1)S(1)}, u32[]{:S(2)}, u32[]{:S(2)}) collective-permute-start(bf16[1,64,2048]{2,1,0:T(8,128)(2,1)S(1)} %constant_dynamic-slice_fusion.1), channel_id=1, source_target_pairs={{0,4},{1,5},{2,6},{3,7},{4,0},{5,1},{6,2},{7,3},{8,12},{9,13},{10,... | collective-permute-start | bytes 786440 | tf_op jit(solution)/shard_map/ppermute | solution.py:243
  11.0 26.8 %copy-start = (bf16[3,256,2048]{2,1,0:T(8,128)(2,1)S(1)}, bf16[3,256,2048]{2,1,0:T(8,128)(2,1)}, u32[]{:S(2)}) copy-start(bf16[3,256,2048]{2,1,0:T(8,128)(2,1)} %refs_4_.6) | copy-start | bytes 9437188
  11.0 32.3 %collective-permute-start.18 = (bf16[2,64,2048]{2,1,0:T(8,128)(2,1)S(1)}, bf16[2,64,2048]{2,1,0:T(8,128)(2,1)S(1)}, u32[]{:S(2)}, u32[]{:S(2)}) collective-permute-start(bf16[2,64,2048]{2,1,0:T(8,128)(2,1)S(1)} %constant_dynamic-slice_fusion), channel_id=1, source_target_pairs={{0,4},{1,5},{2,6},{3,7},{4,0},{5,1},{6,2},{7,3},{8,12},{9,13},{10,... | collective-permute-start | bytes 1572872 | tf_op jit(solution)/shard_map/ppermute | solution.py:243
  14.0 39.7 %collective-permute-start.25 = (bf16[2,2,256,512]{3,2,1,0:T(8,128)(2,1)S(1)}, bf16[2,2,256,512]{3,2,1,0:T(8,128)(2,1)S(1)}, u32[]{:S(2)}, u32[]{:S(2)}) collective-permute-start(bf16[2,2,256,512]{3,2,1,0:T(8,128)(2,1)S(1)} %pad_maximum_fusion.refs_4_), channel_id=1, source_target_pairs={{0,4},{1,3},{2,6},{3,1},{4,0},{5,7},{6,2},{7,5},{8,12},{9,11},{10,... | collective-permute-start | bytes 3145736 | tf_op jit(solution)/shard_map/ppermute | solution.py:243
  17.6 39.8 %copy-start.11 = (bf16[128,3,512]{2,0,1:T(8,128)(2,1)S(1)}, bf16[128,3,512]{2,0,1:T(8,128)(2,1)}, u32[]{:S(2)}) copy-start(bf16[128,3,512]{2,0,1:T(8,128)(2,1)} %param.13) | copy-start | bytes 1179652
  17.7 5.8 %collective-permute-start.1 = (bf16[72,512]{1,0:T(8,128)(2,1)S(1)}, bf16[72,512]{1,0:T(8,128)(2,1)S(1)}, u32[]{:S(2)}, u32[]{:S(2)}) collective-permute-start(bf16[72,512]{1,0:T(8,128)(2,1)S(1)} %get-tuple-element.27.refs_0_), channel_id=1, source_target_pairs={{0,8},{1,9},{2,10},{3,11},{4,12},{5,13},{6,14},{7,15},{8,0},{9,1},... | collective-permute-start | bytes 221192 | tf_op jit(solution)/shard_map/ppermute | solution.py:243
  19.3 6.4 %collective-permute-start.2 = (bf16[72,512]{1,0:T(8,128)(2,1)S(1)}, bf16[72,512]{1,0:T(8,128)(2,1)S(1)}, u32[]{:S(2)}, u32[]{:S(2)}) collective-permute-start(bf16[72,512]{1,0:T(8,128)(2,1)S(1)} %get-tuple-element.27.refs_0_), channel_id=1, source_target_pairs={{0,16},{1,17},{2,18},{3,19},{4,20},{5,21},{6,22},{7,23},{8,24},{9,... | collective-permute-start | bytes 221192 | tf_op jit(solution)/shard_map/ppermute | solution.py:243
  21.9 9.6 %collective-permute-start.6 = (bf16[1,64,2048]{2,1,0:T(8,128)(2,1)S(1)}, bf16[1,64,2048]{2,1,0:T(8,128)(2,1)S(1)}, u32[]{:S(2)}, u32[]{:S(2)}) collective-permute-start(bf16[1,64,2048]{2,1,0:T(8,128)(2,1)S(1)} %collective-permute-done.4.refs_5_), channel_id=1, source_target_pairs={{0,2},{1,3},{2,0},{3,1},{4,6},{5,7},{6,4},{7,5},{8,10},{9,11},{10,... | collective-permute-start | bytes 786440 | tf_op jit(solution)/shard_map/ppermute | solution.py:243
  23.4 6.2 %collective-permute-start.3 = (bf16[72,512]{1,0:T(8,128)(2,1)S(1)}, bf16[72,512]{1,0:T(8,128)(2,1)S(1)}, u32[]{:S(2)}, u32[]{:S(2)}) collective-permute-start(bf16[72,512]{1,0:T(8,128)(2,1)S(1)} %get-tuple-element.27.refs_0_), channel_id=1, source_target_pairs={{0,24},{1,25},{2,26},{3,27},{4,28},{5,29},{6,30},{7,31},{8,16},{9,... | collective-permute-start | bytes 221192 | tf_op jit(solution)/shard_map/ppermute | solution.py:243
  25.7 24.3 %collective-permute-start.12 = (bf16[2,1,256,512]{3,2,1,0:T(8,128)(2,1)S(1)}, bf16[2,1,256,512]{3,2,1,0:T(8,128)(2,1)S(1)}, u32[]{:S(2)}, u32[]{:S(2)}) collective-permute-start(bf16[2,1,256,512]{3,2,1,0:T(8,128)(2,1)S(1)} %pad_maximum_fusion.1.refs_4_), channel_id=1, source_target_pairs={{0,4},{1,3},{2,6},{3,1},{4,0},{5,7},{6,2},{7,5},{8,12},{9,11},{10,... | collective-permute-start | bytes 1572872 | tf_op jit(solution)/shard_map/ppermute | solution.py:243
  29.7 6.9 %collective-permute-start.5 = (bf16[1,64,2048]{2,1,0:T(8,128)(2,1)S(1)}, bf16[1,64,2048]{2,1,0:T(8,128)(2,1)S(1)}, u32[]{:S(2)}, u32[]{:S(2)}) collective-permute-start(bf16[1,64,2048]{2,1,0:T(8,128)(2,1)S(1)} %collective-permute-done.4.refs_5_), channel_id=1, source_target_pairs={{0,1},{1,0},{2,3},{3,2},{4,5},{5,4},{6,7},{7,6},{8,9},{9,8},{10,11... | collective-permute-start | bytes 786440 | tf_op jit(solution)/shard_map/ppermute | solution.py:243
  31.4 6.3 %collective-permute-start.7 = (bf16[1,64,2048]{2,1,0:T(8,128)(2,1)S(1)}, bf16[1,64,2048]{2,1,0:T(8,128)(2,1)S(1)}, u32[]{:S(2)}, u32[]{:S(2)}) collective-permute-start(bf16[1,64,2048]{2,1,0:T(8,128)(2,1)S(1)} %collective-permute-done.6.refs_7_), channel_id=1, source_target_pairs={{0,1},{1,0},{2,3},{3,2},{4,5},{5,4},{6,7},{7,6},{8,9},{9,8},{10,11... | collective-permute-start | bytes 786440 | tf_op jit(solution)/shard_map/ppermute | solution.py:243
  39.1 6.0 %collective-permute-start.8 = (bf16[72,512]{1,0:T(8,128)(2,1)S(1)}, bf16[72,512]{1,0:T(8,128)(2,1)S(1)}, u32[]{:S(2)}, u32[]{:S(2)}) collective-permute-start(bf16[72,512]{1,0:T(8,128)(2,1)S(1)} %solve0.1.refs_0_.refs_9_.refs_4_), channel_id=1, source_target_pairs={{0,8},{1,9},{2,10},{3,11},{4,12},{5,13},{6,14},{7,15},{8,0},{9,1},... | collective-permute-start | bytes 221192 | tf_op jit(solution)/shard_map/ppermute | solution.py:243
  40.7 6.8 %collective-permute-start.9 = (bf16[72,512]{1,0:T(8,128)(2,1)S(1)}, bf16[72,512]{1,0:T(8,128)(2,1)S(1)}, u32[]{:S(2)}, u32[]{:S(2)}) collective-permute-start(bf16[72,512]{1,0:T(8,128)(2,1)S(1)} %solve0.1.refs_0_.refs_9_.refs_4_), channel_id=1, source_target_pairs={{0,16},{1,17},{2,18},{3,19},{4,20},{5,21},{6,22},{7,23},{8,24},{9,... | collective-permute-start | bytes 221192 | tf_op jit(solution)/shard_map/ppermute | solution.py:243
  43.3 13.6 %collective-permute-start.20 = (bf16[2,64,2048]{2,1,0:T(8,128)(2,1)S(1)}, bf16[2,64,2048]{2,1,0:T(8,128)(2,1)S(1)}, u32[]{:S(2)}, u32[]{:S(2)}) collective-permute-start(bf16[2,64,2048]{2,1,0:T(8,128)(2,1)S(1)} %collective-permute-done.18.refs_5_), channel_id=1, source_target_pairs={{0,2},{1,3},{2,0},{3,1},{4,6},{5,7},{6,4},{7,5},{8,10},{9,11},{10,... | collective-permute-start | bytes 1572872 | tf_op jit(solution)/shard_map/ppermute | solution.py:243
  45.1 11.9 %collective-permute-start.13 = (bf16[2,1,256,512]{3,2,1,0:T(8,128)(2,1)S(1)}, bf16[2,1,256,512]{3,2,1,0:T(8,128)(2,1)S(1)}, u32[]{:S(2)}, u32[]{:S(2)}) collective-permute-start(bf16[2,1,256,512]{3,2,1,0:T(8,128)(2,1)S(1)} %pad_maximum_fusion.1.refs_4_), channel_id=1, source_target_pairs={{0,1},{1,0},{2,3},{3,2},{4,5},{5,4},{6,7},{7,6},{8,9},{9,8},{10,11... | collective-permute-start | bytes 1572872 | tf_op jit(solution)/shard_map/ppermute | solution.py:243
  47.5 6.2 %collective-permute-start.10 = (bf16[72,512]{1,0:T(8,128)(2,1)S(1)}, bf16[72,512]{1,0:T(8,128)(2,1)S(1)}, u32[]{:S(2)}, u32[]{:S(2)}) collective-permute-start(bf16[72,512]{1,0:T(8,128)(2,1)S(1)} %solve0.1.refs_0_.refs_9_.refs_4_), channel_id=1, source_target_pairs={{0,24},{1,25},{2,26},{3,27},{4,28},{5,29},{6,30},{7,31},{8,16},{9,... | collective-permute-start | bytes 221192 | tf_op jit(solution)/shard_map/ppermute | solution.py:243
  50.0 7.4 %collective-permute-start.14 = (bf16[2,1,256,512]{3,2,1,0:T(8,128)(2,1)S(1)}, bf16[2,1,256,512]{3,2,1,0:T(8,128)(2,1)S(1)}, u32[]{:S(2)}, u32[]{:S(2)}) collective-permute-start(bf16[2,1,256,512]{3,2,1,0:T(8,128)(2,1)S(1)} %collective-permute-done.12.refs_5_), channel_id=1, source_target_pairs={{0,1},{1,0},{2,3},{3,2},{4,5},{5,4},{6,7},{7,6},{8,9},{9,8},{10,11... | collective-permute-start | bytes 1572872 | tf_op jit(solution)/shard_map/ppermute | solution.py:243
  53.7 37.7 %collective-permute-start.26 = (bf16[2,2,256,512]{3,2,1,0:T(8,128)(2,1)S(1)}, bf16[2,2,256,512]{3,2,1,0:T(8,128)(2,1)S(1)}, u32[]{:S(2)}, u32[]{:S(2)}) collective-permute-start(bf16[2,2,256,512]{3,2,1,0:T(8,128)(2,1)S(1)} %pad_maximum_fusion.refs_4_), channel_id=1, source_target_pairs={{0,1},{1,0},{2,3},{3,2},{4,5},{5,4},{6,7},{7,6},{8,9},{9,8},{10,11... | collective-permute-start | bytes 3145736 | tf_op jit(solution)/shard_map/ppermute | solution.py:243
  53.7 41.0 %collective-permute-start.27 = (bf16[2,2,256,512]{3,2,1,0:T(8,128)(2,1)S(1)}, bf16[2,2,256,512]{3,2,1,0:T(8,128)(2,1)S(1)}, u32[]{:S(2)}, u32[]{:S(2)}) collective-permute-start(bf16[2,2,256,512]{3,2,1,0:T(8,128)(2,1)S(1)} %collective-permute-done.25.refs_5_), channel_id=1, source_target_pairs={{0,1},{1,0},{2,3},{3,2},{4,5},{5,4},{6,7},{7,6},{8,9},{9,8},{10,11... | collective-permute-start | bytes 3145736 | tf_op jit(solution)/shard_map/ppermute | solution.py:243
  57.0 10.4 %collective-permute-start.19 = (bf16[2,64,2048]{2,1,0:T(8,128)(2,1)S(1)}, bf16[2,64,2048]{2,1,0:T(8,128)(2,1)S(1)}, u32[]{:S(2)}, u32[]{:S(2)}) collective-permute-start(bf16[2,64,2048]{2,1,0:T(8,128)(2,1)S(1)} %collective-permute-done.18.refs_5_), channel_id=1, source_target_pairs={{0,1},{1,0},{2,3},{3,2},{4,5},{5,4},{6,7},{7,6},{8,9},{9,8},{10,11... | collective-permute-start | bytes 1572872 | tf_op jit(solution)/shard_map/ppermute | solution.py:243
  57.0 22.9 %collective-permute-start.21 = (bf16[2,64,2048]{2,1,0:T(8,128)(2,1)S(1)}, bf16[2,64,2048]{2,1,0:T(8,128)(2,1)S(1)}, u32[]{:S(2)}, u32[]{:S(2)}) collective-permute-start(bf16[2,64,2048]{2,1,0:T(8,128)(2,1)S(1)} %collective-permute-done.20.refs_7_), channel_id=1, source_target_pairs={{0,1},{1,0},{2,3},{3,2},{4,5},{5,4},{6,7},{7,6},{8,9},{9,8},{10,11... | collective-permute-start | bytes 1572872 | tf_op jit(solution)/shard_map/ppermute | solution.py:243
  57.5 2.0 %collective-permute-start.33 = (bf16[3,128,512]{2,1,0:T(8,128)(2,1)S(1)}, bf16[3,128,512]{2,1,0:T(8,128)(2,1)S(1)}, u32[]{:S(2)}, u32[]{:S(2)}) collective-permute-start(bf16[3,128,512]{2,1,0:T(8,128)(2,1)S(1)} %bitcast.20), channel_id=1, source_target_pairs={{0,0},{1,8},{2,16},{3,24},{4,4},{5,12},{6,20},{7,28},{8,1},{9,9},{... | collective-permute-start | bytes 1179656 | tf_op jit(solution)/shard_map/ppermute | solution.py:243
  59.5 21.9 %collective-permute-start.15 = (bf16[72,512]{1,0:T(8,128)(2,1)S(1)}, bf16[72,512]{1,0:T(8,128)(2,1)S(1)}, u32[]{:S(2)}, u32[]{:S(2)}) collective-permute-start(bf16[72,512]{1,0:T(8,128)(2,1)S(1)} %update10.1.refs_0_), channel_id=1, source_target_pairs={{0,8},{1,9},{2,10},{3,11},{4,12},{5,13},{6,14},{7,15},{8,0},{9,1},... | collective-permute-start | bytes 221192 | tf_op jit(solution)/shard_map/ppermute | solution.py:243
  67.4 18.8 %collective-permute-start.16 = (bf16[72,512]{1,0:T(8,128)(2,1)S(1)}, bf16[72,512]{1,0:T(8,128)(2,1)S(1)}, u32[]{:S(2)}, u32[]{:S(2)}) collective-permute-start(bf16[72,512]{1,0:T(8,128)(2,1)S(1)} %update10.1.refs_0_), channel_id=1, source_target_pairs={{0,16},{1,17},{2,18},{3,19},{4,20},{5,21},{6,22},{7,23},{8,24},{9,... | collective-permute-start | bytes 221192 | tf_op jit(solution)/shard_map/ppermute | solution.py:243
  79.9 7.2 %collective-permute-start.17 = (bf16[72,512]{1,0:T(8,128)(2,1)S(1)}, bf16[72,512]{1,0:T(8,128)(2,1)S(1)}, u32[]{:S(2)}, u32[]{:S(2)}) collective-permute-start(bf16[72,512]{1,0:T(8,128)(2,1)S(1)} %update10.1.refs_0_), channel_id=1, source_target_pairs={{0,24},{1,25},{2,26},{3,27},{4,28},{5,29},{6,30},{7,31},{8,16},{9,... | collective-permute-start | bytes 221192 | tf_op jit(solution)/shard_map/ppermute | solution.py:243
  81.4 37.2 %collective-permute-start.35 = (bf16[3,128,512]{2,1,0:T(8,128)(2,1)S(1)}, bf16[3,128,512]{2,1,0:T(8,128)(2,1)S(1)}, u32[]{:S(2)}, u32[]{:S(2)}) collective-permute-start(bf16[3,128,512]{2,1,0:T(8,128)(2,1)S(1)} %collective-permute-done.33.refs_6_.refs_2_), channel_id=1, source_target_pairs={{0,2},{1,3},{2,0},{3,1},{4,6},{5,7},{6,4},{7,5},{8,10},{9,11},{10,... | collective-permute-start | bytes 1179656 | tf_op jit(solution)/shard_map/ppermute | solution.py:243
  88.4 13.9 %copy-start.1 = (bf16[72,512]{1,0:T(8,128)(2,1)}, bf16[72,512]{1,0:T(8,128)(2,1)S(1)}, u32[]{:S(2)}) copy-start(bf16[72,512]{1,0:T(8,128)(2,1)S(1)} %get-tuple-element.29.refs_0_.refs_1_.refs_5_) | copy-start | bytes 221188
  88.4 18.4 %collective-permute-start.31 = (bf16[1,2,64,512]{3,2,1,0:T(8,128)(2,1)S(1)}, bf16[1,2,64,512]{3,2,1,0:T(8,128)(2,1)S(1)}, u32[]{:S(2)}, u32[]{:S(2)}) collective-permute-start(bf16[1,2,64,512]{3,2,1,0:T(8,128)(2,1)S(1)} %bitcast.17), channel_id=1, source_target_pairs={{0,2},{1,5},{2,0},{3,7},{4,6},{5,1},{6,4},{7,3},{8,10},{9,13},{10,... | collective-permute-start | bytes 393224 | tf_op jit(solution)/shard_map/ppermute | solution.py:243
  90.9 5.7 %collective-permute-start.22 = (bf16[72,512]{1,0:T(8,128)(2,1)S(1)}, bf16[72,512]{1,0:T(8,128)(2,1)S(1)}, u32[]{:S(2)}, u32[]{:S(2)}) collective-permute-start(bf16[72,512]{1,0:T(8,128)(2,1)S(1)} %get-tuple-element.29.refs_0_.refs_1_.refs_5_), channel_id=1, source_target_pairs={{0,8},{1,9},{2,10},{3,11},{4,12},{5,13},{6,14},{7,15},{8,0},{9,1},... | collective-permute-start | bytes 221192 | tf_op jit(solution)/shard_map/ppermute | solution.py:243
  91.4 8.5 %collective-permute-start.23 = (bf16[72,512]{1,0:T(8,128)(2,1)S(1)}, bf16[72,512]{1,0:T(8,128)(2,1)S(1)}, u32[]{:S(2)}, u32[]{:S(2)}) collective-permute-start(bf16[72,512]{1,0:T(8,128)(2,1)S(1)} %get-tuple-element.29.refs_0_.refs_1_.refs_5_), channel_id=1, source_target_pairs={{0,16},{1,17},{2,18},{3,19},{4,20},{5,21},{6,22},{7,23},{8,24},{9,... | collective-permute-start | bytes 221192 | tf_op jit(solution)/shard_map/ppermute | solution.py:243
  94.7 6.3 %collective-permute-start.24 = (bf16[72,512]{1,0:T(8,128)(2,1)S(1)}, bf16[72,512]{1,0:T(8,128)(2,1)S(1)}, u32[]{:S(2)}, u32[]{:S(2)}) collective-permute-start(bf16[72,512]{1,0:T(8,128)(2,1)S(1)} %get-tuple-element.29.refs_0_.refs_1_.refs_5_), channel_id=1, source_target_pairs={{0,24},{1,25},{2,26},{3,27},{4,28},{5,29},{6,30},{7,31},{8,16},{9,... | collective-permute-start | bytes 221192 | tf_op jit(solution)/shard_map/ppermute | solution.py:243
  102.3 5.8 %collective-permute-start.28 = (bf16[72,512]{1,0:T(8,128)(2,1)S(1)}, bf16[72,512]{1,0:T(8,128)(2,1)S(1)}, u32[]{:S(2)}, u32[]{:S(2)}) collective-permute-start(bf16[72,512]{1,0:T(8,128)(2,1)S(1)} %update21.1.refs_0_), channel_id=1, source_target_pairs={{0,8},{1,9},{2,10},{3,11},{4,12},{5,13},{6,14},{7,15},{8,0},{9,1},... | collective-permute-start | bytes 221192 | tf_op jit(solution)/shard_map/ppermute | solution.py:243
  103.6 8.3 %collective-permute-start.29 = (bf16[72,512]{1,0:T(8,128)(2,1)S(1)}, bf16[72,512]{1,0:T(8,128)(2,1)S(1)}, u32[]{:S(2)}, u32[]{:S(2)}) collective-permute-start(bf16[72,512]{1,0:T(8,128)(2,1)S(1)} %update21.1.refs_0_), channel_id=1, source_target_pairs={{0,16},{1,17},{2,18},{3,19},{4,20},{5,21},{6,22},{7,23},{8,24},{9,... | collective-permute-start | bytes 221192 | tf_op jit(solution)/shard_map/ppermute | solution.py:243
  104.6 7.3 %collective-permute-start.30 = (bf16[72,512]{1,0:T(8,128)(2,1)S(1)}, bf16[72,512]{1,0:T(8,128)(2,1)S(1)}, u32[]{:S(2)}, u32[]{:S(2)}) collective-permute-start(bf16[72,512]{1,0:T(8,128)(2,1)S(1)} %update21.1.refs_0_), channel_id=1, source_target_pairs={{0,24},{1,25},{2,26},{3,27},{4,28},{5,29},{6,30},{7,31},{8,16},{9,... | collective-permute-start | bytes 221192 | tf_op jit(solution)/shard_map/ppermute | solution.py:243
  106.8 12.3 %collective-permute-start.32 = (bf16[2,2,64,512]{3,2,1,0:T(8,128)(2,1)S(1)}, bf16[2,2,64,512]{3,2,1,0:T(8,128)(2,1)S(1)}, u32[]{:S(2)}, u32[]{:S(2)}) collective-permute-start(bf16[2,2,64,512]{3,2,1,0:T(8,128)(2,1)S(1)} %pad_maximum_fusion.2.refs_4_.refs_0_), channel_id=1, source_target_pairs={{0,4},{1,3},{2,6},{3,1},{4,0},{5,7},{6,2},{7,5},{8,12},{9,11},{10,... | collective-permute-start | bytes 786440 | tf_op jit(solution)/shard_map/ppermute | solution.py:243
  114.1 0.6 copy-start.4
  114.7 12.3 %all-to-all-start = ((bf16[8,64,512]{2,1,0:T(8,128)(2,1)}), bf16[8,64,512]{2,1,0:T(8,128)(2,1)S(1)}, u32[]{:S(2)}, u32[]{:S(2)}) async-start(bf16[8,64,512]{2,1,0:T(8,128)(2,1)} %get-tuple-element.32), calls=%async_computation | async-start | bytes 1048576 | tf_op jit(solution)/shard_map/all_to_all | solution.py:442
  118.2 1.9 %collective-permute-start.34 = (bf16[3,128,512]{2,1,0:T(8,128)(2,1)S(1)}, bf16[3,128,512]{2,1,0:T(8,128)(2,1)S(1)}, u32[]{:S(2)}, u32[]{:S(2)}) collective-permute-start(bf16[3,128,512]{2,1,0:T(8,128)(2,1)S(1)} %collective-permute-done.33.refs_6_.refs_2_), channel_id=1, source_target_pairs={{0,1},{1,0},{2,3},{3,2},{4,5},{5,4},{6,7},{7,6},{8,9},{9,8},{10,11... | collective-permute-start | bytes 1179656 | tf_op jit(solution)/shard_map/ppermute | solution.py:243
  118.6 2.1 %collective-permute-start.36 = (bf16[3,128,512]{2,1,0:T(8,128)(2,1)S(1)}, bf16[3,128,512]{2,1,0:T(8,128)(2,1)S(1)}, u32[]{:S(2)}, u32[]{:S(2)}) collective-permute-start(bf16[3,128,512]{2,1,0:T(8,128)(2,1)S(1)} %collective-permute-done.35.refs_8_.refs_4_), channel_id=1, source_target_pairs={{0,1},{1,0},{2,3},{3,2},{4,5},{5,4},{6,7},{7,6},{8,9},{9,8},{10,11... | collective-permute-start | bytes 1179656 | tf_op jit(solution)/shard_map/ppermute | solution.py:243
  118.8 2.3 %collective-permute-start.37 = (bf16[2,2,64,512]{3,2,1,0:T(8,128)(2,1)S(1)}, bf16[2,2,64,512]{3,2,1,0:T(8,128)(2,1)S(1)}, u32[]{:S(2)}, u32[]{:S(2)}) collective-permute-start(bf16[2,2,64,512]{3,2,1,0:T(8,128)(2,1)S(1)} %pad_maximum_fusion.2.refs_4_.refs_0_), channel_id=1, source_target_pairs={{0,1},{1,0},{2,3},{3,2},{4,5},{5,4},{6,7},{7,6},{8,9},{9,8},{10,11... | collective-permute-start | bytes 786440 | tf_op jit(solution)/shard_map/ppermute | solution.py:243
  119.1 2.3 %collective-permute-start.38 = (bf16[2,2,64,512]{3,2,1,0:T(8,128)(2,1)S(1)}, bf16[2,2,64,512]{3,2,1,0:T(8,128)(2,1)S(1)}, u32[]{:S(2)}, u32[]{:S(2)}) collective-permute-start(bf16[2,2,64,512]{3,2,1,0:T(8,128)(2,1)S(1)} %collective-permute-done.32.refs_5_.refs_1_), channel_id=1, source_target_pairs={{0,1},{1,0},{2,3},{3,2},{4,5},{5,4},{6,7},{7,6},{8,9},{9,8},{10,11... | collective-permute-start | bytes 786440 | tf_op jit(solution)/shard_map/ppermute | solution.py:243
  121.4 0.9 copy-start.2
  125.0 16.8 %copy-start.10 = (f32[128]{0:T(128)S(1)}, f32[128]{0:T(128)}, u32[]{:S(2)}) copy-start(f32[128]{0:T(128)} %param.15) | copy-start | bytes 1540
  127.0 0.9 copy-start.5
  127.9 13.9 %copy-start.8 = (bf16[128,128]{1,0:T(8,128)(2,1)S(1)}, bf16[128,128]{1,0:T(8,128)(2,1)}, u32[]{:S(2)}) copy-start(bf16[128,128]{1,0:T(8,128)(2,1)} %refs_4_.7) | copy-start | bytes 98308
  129.6 8.2 %collective-permute-start.39 = (bf16[104,512]{1,0:T(8,128)(2,1)S(1)}, bf16[104,512]{1,0:T(8,128)(2,1)S(1)}, u32[]{:S(2)}, u32[]{:S(2)}) collective-permute-start(bf16[104,512]{1,0:T(8,128)(2,1)S(1)} %get-tuple-element.37), channel_id=1, source_target_pairs={{0,8},{1,9},{2,10},{3,11},{4,12},{5,13},{6,14},{7,15},{8,0},{9,1},... | collective-permute-start | bytes 319496 | tf_op jit(solution)/shard_map/ppermute | solution.py:243
  131.1 10.7 %collective-permute-start.40 = (bf16[104,512]{1,0:T(8,128)(2,1)S(1)}, bf16[104,512]{1,0:T(8,128)(2,1)S(1)}, u32[]{:S(2)}, u32[]{:S(2)}) collective-permute-start(bf16[104,512]{1,0:T(8,128)(2,1)S(1)} %get-tuple-element.38), channel_id=1, source_target_pairs={{0,16},{1,17},{2,18},{3,19},{4,20},{5,21},{6,22},{7,23},{8,24},{9,... | collective-permute-start | bytes 319496 | tf_op jit(solution)/shard_map/ppermute | solution.py:243
  132.4 9.3 %collective-permute-start.41 = (bf16[104,512]{1,0:T(8,128)(2,1)S(1)}, bf16[104,512]{1,0:T(8,128)(2,1)S(1)}, u32[]{:S(2)}, u32[]{:S(2)}) collective-permute-start(bf16[104,512]{1,0:T(8,128)(2,1)S(1)} %get-tuple-element.39), channel_id=1, source_target_pairs={{0,24},{1,25},{2,26},{3,27},{4,28},{5,29},{6,30},{7,31},{8,16},{9,... | collective-permute-start | bytes 319496 | tf_op jit(solution)/shard_map/ppermute | solution.py:243
  134.1 0.9 copy-start.3
  135.0 0.9 copy-start.6

commit v3 on v0

v3 whole, which is shorter than its diff:
```python
import functools

import jax
import jax.numpy as jnp
from jax import lax
from jax.experimental import pallas as pl
from jax.experimental.pallas import tpu as pltpu
from jax.sharding import PartitionSpec as P


BF16 = jnp.bfloat16
F32 = jnp.float32
PAD = 8
SCRATCH_BYTES = 12 * 2**20


def dot_t(a, b):
    return lax.dot_general(a, b, (((1,), (1,)), ((), ())), preferred_element_type=F32)


def aligned_at(offset, size):
    return pl.ds(pl.multiple_of(offset, size), size)


class Place:
    def __init__(self, row, col):
        self.row, self.col = row, col
        self.z, self.x, self.core = row // 2, row % 2, col % 2


def here():
    return Place(lax.axis_index("row"), lax.axis_index("col"))


def call(kernel, arrays, outs, scratch=(), plain=(), hbm=(), more=(), to_hbm=False):
    vmem = pl.BlockSpec(memory_space=pltpu.VMEM)
    specs, given = [], []
    for n, array in enumerate(arrays):
        if n in hbm:
            specs.append(pl.BlockSpec(memory_space=pltpu.HBM))
            array = pltpu.with_memory_space_constraint(array, pltpu.HBM)
        elif n in plain:
            specs.append(vmem)
        else:
            specs.append(vmem)
            array = pltpu.with_memory_space_constraint(array, pltpu.VMEM)
        given.append(array)
    kind = jax.ShapeDtypeStruct if to_hbm else pltpu.VMEM
    return pl.pallas_call(
        lambda *refs: kernel(here(), *refs),
        in_specs=specs,
        out_specs=[vmem] * len(outs),
        out_shape=[kind(shape, dtype) for shape, dtype in outs],
        scratch_shapes=[pltpu.VMEM(shape, dtype) for shape, dtype in scratch]
        + list(more),
        compiler_params=pltpu.CompilerParams(vmem_limit_bytes=SCRATCH_BYTES),
    )(*given)


def parts_kernel(inverse, *refs):
    outs, sems = refs[:-1], refs[-1]
    place = here()
    block = inverse.shape[1]
    half, depth = outs[0].shape
    pieces = []
    for k in range(depth // block):
        columns = aligned_at((2 * k + 1 - place.x) * block, block)
        source = inverse.at[0, aligned_at(place.core * half, half), columns]
        pieces.append((source, outs[0].at[:, pl.ds(k * block, block)]))
    for n, out in enumerate(outs[1:]):
        rows = out.shape[1]
        source = inverse.at[n + 1, aligned_at(place.col * rows, rows), :]
        pieces.append((source, out.at[0]))
    copies = [
        pltpu.make_async_copy(source, target, sems.at[n])
        for n, (source, target) in enumerate(pieces)
    ]
    for copy in copies:
        copy.start()
    for copy in copies:
        copy.wait()


def pack_kernel(place, own, got, *outs):
    at = 0
    for out in outs:
        count = out.shape[1]
        out[0] = own[at : at + count]
        out[1] = got[at : at + count]
        at += count


def prep_kernel(place, order_hbm, x_hbm, y_hbm, first, send, keep, turned, *held):
    half, rows = send.shape[1] - PAD, send.shape[2]
    x_ref, y_ref, order, sems = held
    pairs = [(order_hbm, order), (x_hbm, x_ref), (y_hbm, y_ref)]
    copies = [pltpu.make_async_copy(a, b, sems.at[n]) for n, (a, b) in enumerate(pairs)]
    for copy in copies:
        copy.start()
    for copy in copies:
        copy.wait()
    at = lax.broadcasted_iota(jnp.int32, (PAD, rows), 0)
    for s in range(x_ref.shape[0]):
        stored = order[s]
        turned[...] = x_ref[stored].astype(F32).T
        y = jnp.broadcast_to(y_ref[pl.ds(stored, 1), :], (PAD, rows))
        high = y.astype(BF16).astype(F32)
        if s == 0:
            first[: 2 * half, :] = turned[...].astype(BF16)
            first[2 * half :, :] = jnp.where(at == 0, y, 0.0).astype(BF16)
            continue
        n = s - 1
        keep[n, :half, :] = turned[aligned_at(place.x * half, half), :]
        keep[n, half:, :] = jnp.where(at == 0, y, 0.0)
        send[n, :half, :] = turned[aligned_at((1 - place.x) * half, half), :].astype(BF16)
        low = jnp.where(at == 1, y - high, 0.0)
        send[n, half:, :] = jnp.where(at == 0, high, low).astype(BF16)


def merge_kernel(place, keep, got, *bases):
    _, height, rows = keep.shape
    half = height - PAD
    mine = aligned_at(place.x * rows, rows)
    other = aligned_at((1 - place.x) * rows, rows)
    at = lax.broadcasted_iota(jnp.int32, (PAD, rows), 0)
    for n, out in enumerate(bases):
        tail = got[n, half:, :].astype(F32)
        resp = jnp.where(at == 0, jnp.sum(tail, 0, keepdims=True), 0.0)
        out[:, mine] = keep[n]
        out[:half, other] = got[n, :half, :].astype(F32)
        out[half:, other] = resp


def join_kernel(place, keep, got, out):
    out[...] = (keep[...] + got[...].astype(F32)).astype(out.dtype)


def first_kernel(place, *refs):
    tiles, (inverse, mine, theirs, keep, send, gathered, total) = refs[:-7], refs[-7:]
    block = tiles[0].shape[1]
    half = keep.shape[0] - PAD
    rows = mine.shape[0]
    gather_tiles(place, tiles, gathered)
    own = None
    for k in range(len(tiles)):
        columns = aligned_at((2 * k + place.x) * block, block)
        part = dot_t(gathered[:, k * block : (k + 1) * block], inverse[0, :, columns])
        own = part if own is None else own + part
    total[:, aligned_at(place.x * block, block)] = own
    at = (1 - place.x) * block
    total[:, aligned_at(at + place.core * rows, rows)] = dot_t(gathered[...], mine[...])
    total[:, aligned_at(at + (1 - place.core) * rows, rows)] = dot_t(gathered[...], theirs[...])
    keep[:half, :] = total[aligned_at(place.x * half, half), :]
    keep[half:, :] = total[2 * half :, :]
    send[:half, :] = total[aligned_at((1 - place.x) * half, half), :].astype(BF16)
    send[half:, :] = total[2 * half :, :].astype(BF16)


def gather_tiles(place, tiles, gathered):
    block = tiles[0].shape[1]
    for k, tile in enumerate(tiles):
        gathered[:, aligned_at((place.z ^ k) * block, block)] = tile[...]


def solve_kernel(counts, place, *refs):
    planes, layer, offsets, befores = counts
    tiles, inverse, refs = refs[:planes], refs[planes], refs[planes + 1 :]
    parts, refs = refs[: len(offsets)], refs[len(offsets) :]
    before, outs, gathered, other = refs[:befores], refs[befores:-2], refs[-2], refs[-1]
    rows = inverse.shape[1]
    gather_tiles(place, tiles, gathered)
    for part, dc in zip(parts, offsets):
        count = part.shape[1]
        other[aligned_at((place.col ^ dc) * count, count), :] = part[0]
    own = dot_t(gathered[...], inverse[layer]).astype(BF16)
    theirs = dot_t(gathered[...], other[...]).astype(BF16)
    mine, yours = aligned_at(place.x * rows, rows), aligned_at((1 - place.x) * rows, rows)
    for out in outs:
        if out.ndim == 2:
            height = out.shape[0]
            first = own.shape[0] - height
            out[:, mine] = own[first:]
            out[:, yours] = theirs[first:]
        else:
            height = out.shape[1]
            for m, tile in enumerate(before):
                out[m] = tile[...]
            out[len(before), :, mine] = own[:height]
            out[len(before), :, yours] = theirs[:height]


def update_kernel(counts, place, *refs):
    planes, pieces, arrays, has_base, split = counts
    tiles, refs = refs[:planes], refs[planes:]
    given, refs = refs[:arrays], refs[arrays:]
    base, refs = (refs[0], refs[1:]) if has_base else (None, refs)
    outs, gathered, total = refs[:-2], refs[-2], refs[-1]
    gather_tiles(place, tiles, gathered)
    total[...] = base[...] if has_base else jnp.zeros(total.shape, F32)
    for index, lead, where in pieces:
        piece = given[index]
        rows, width = piece.shape[-2:]
        dx, dc = where(place)
        columns = gathered[:, aligned_at((place.col ^ dc) * width, width)]
        at = aligned_at((place.x ^ dx) * rows, rows)
        total[:, at] = total[:, at] - dot_t(columns, piece[lead])
    if split:
        rows = outs[0].shape[1]
        outs[0][...] = total[:, aligned_at(place.x * rows, rows)]
        outs[1][...] = total[:, aligned_at((1 - place.x) * rows, rows)]
    else:
        outs[0][...] = total[...].astype(outs[0].dtype)


def partial_kernel(counts, place, *refs):
    planes, tiles, layers, has_base, n_arrays, apart, half = counts
    arrays, refs = refs[:n_arrays], refs[n_arrays:]
    resps, refs = (refs[0], refs[1:]) if apart else (arrays[0], refs)
    base, refs = (refs[0], refs[1:]) if has_base else (None, refs)
    outs, wide, sums = refs[:-2], refs[-2], refs[-1]
    own_cols = 2 * half
    resps = [resps[...] if apart else resps[0, n][half:, :] for n in range(layers)]
    for index, lead, where in tiles:
        x, col = where(place)
        at = aligned_at(col * own_cols + x * half, half)
        for n in range(layers):
            wide[n, at, :] = arrays[index][lead(n)][:half, :]
    sums[...] = base[...] if has_base else jnp.zeros(sums.shape, F32)
    for k in range(planes):
        to = place.z ^ k
        for n in range(layers):
            own = wide[n, aligned_at(to * own_cols + place.x * half, half), :]
            sums[k, :half, :] += dot_t(own, wide[n])
            sums[k, half:, :half] += dot_t(resps[n], own)
    if len(outs) == 1:
        outs[0][...] = sums[...]
    else:
        for k, out in enumerate(outs):
            out[...] = sums[k].astype(out.dtype)


def final_kernel(scale, place, *refs):
    slots = refs[:-8]
    mine, theirs, x_ref, y_ref, rhs, resp, normal, right = refs[-8:]
    half = normal.shape[0]
    total = slots[0][...].astype(F32)
    for slot in slots[1:]:
        total += slot[...].astype(F32)
    normal[...] = total[:half] * scale
    right[...] = total[half, :half] * scale
    resp[...] = y_ref[...] + mine[half, :]
    own, other = mine[:half, :].T, theirs[:half, :].T
    swapped = place.x == 1
    left, after = jnp.where(swapped, other, own), jnp.where(swapped, own, other)
    rhs[...] = x_ref[...].astype(F32) + jnp.concatenate([left, after], 1)


def white_kernel(counts, place, *refs):
    steps, last_x, first_x, n_early = counts
    early, late, (resp_ref, out, resp_out, turned) = refs[:n_early], refs[n_early:-4], refs[-4:]
    half = late[0].shape[-2]
    rows = out.shape[1]
    lanes = aligned_at(place.x * rows, rows)
    row_at = lax.broadcasted_iota(jnp.int32, (steps, rows), 0)
    resps = jnp.zeros((steps, rows), F32)
    (a, i), (b, j) = last_x, first_x
    for s in range(steps):
        arrays = early if s < steps - 1 else late
        n = s if s < steps - 1 else 0
        own = arrays[0][0, n, :, lanes]
        one = arrays[a][i, n, :half, lanes].astype(F32)
        two = arrays[b][j, n, :half, lanes].astype(F32)
        resp = own[half:] if s < steps - 1 else resp_ref[:, lanes]
        turned[aligned_at(place.x * half, half), :] = own[:half].astype(F32)
        other = jnp.where(place.core == 0, one, two)
        turned[aligned_at((1 - place.x) * half, half), :] = other
        out[s] = turned[...].T.astype(BF16)
        spread = jnp.broadcast_to(resp.astype(F32)[:1], (steps, rows))
        resps = jnp.where(row_at == s, spread, resps)
    resp_out[...] = resps.astype(BF16)


def shards(
    x_window, y_window, block_order, diag_inverse, panel_window, panel_trail, x_trail, y_trail
):
    steps, rows, own_cols = x_window.shape
    n_rows, n_cols = lax.axis_size("row"), lax.axis_size("col")
    planes = n_rows // 2
    place = here()
    x, core = place.x, place.core
    half = own_cols // 2
    height = half + PAD
    pair = 2 * rows
    total_rows = rows * n_rows
    full = own_cols * n_cols
    trail_rows = x_trail.shape[0]
    kernels = rows % 128 == 0 and half % 8 == 0

    def move(array, to):
        table = []
        for r in range(n_rows):
            for c in range(n_cols):
                tr, tc = to(r, c)
                table.append((r * n_cols + c, tr * n_cols + tc))
        return lax.ppermute(array, ("row", "col"), table)

    def flip(array, dr=0, dc=0):
        return move(array, lambda r, c: (r ^ dr, c ^ dc))

    def ordered(own, other, axis):
        return jnp.where(
            x == 0,
            jnp.concatenate([own, other], axis),
            jnp.concatenate([other, own], axis),
        )

    far = []
    bit = n_cols // 2
    while bit > 1:
        far.append((0, bit))
        bit //= 2
    hops = (far + [(1, 0)], [(1, 0)] + far)

    def label(index, which):
        dx = dc = 0
        for stage, (hx, hc) in enumerate(hops[which]):
            if index >> stage & 1:
                dx, dc = dx ^ hx, dc ^ hc
        return dx, dc

    def hop(array, stage):
        def to(r, c):
            hx, hc = hops[c % 2][stage]
            return r ^ hx, c ^ hc

        return move(array, to)

    def finish(start, stage):
        held = [start]
        for n in range(stage, len(hops[0])):
            held = held + [hop(held[0], n)]
            if n + 1 < len(hops[0]):
                held = [jnp.concatenate(held, 0)]
        return held + [flip(a, dc=1) for a in held]

    def piece_labels(arrays):
        listed = []
        own = len(arrays) // 2
        for side in range(2):
            index = 0
            for n in range(own):
                for lead in range(arrays[n].shape[0]):

                    def where(p, index=index, side=side):
                        (ax, ac), (bx, bc) = label(index, side), label(index, 1 - side)
                        dx = jnp.where(p.core == 0, ax, bx)
                        dc = jnp.where(p.core == 0, ac, bc) ^ side
                        return dx, dc

                    listed.append((side * own + n, lead, where))
                    index += 1
        return listed

    part_rows = rows // n_cols
    if kernels:
        sent_first, *sent_rows = pl.pallas_call(
            parts_kernel,
            in_specs=[pl.BlockSpec(memory_space=pltpu.HBM)],
            out_specs=[pl.BlockSpec(memory_space=pltpu.VMEM)] * steps,
            out_shape=[pltpu.VMEM((rows // 2, total_rows // 2), BF16)]
            + [pltpu.VMEM((1, part_rows, total_rows), BF16)] * (steps - 1),
            scratch_shapes=[pltpu.SemaphoreType.DMA((planes + steps - 1,))],
            compiler_params=pltpu.CompilerParams(vmem_limit_bytes=SCRATCH_BYTES),
            name="parts",
        )(pltpu.with_memory_space_constraint(diag_inverse, pltpu.HBM))
    else:
        cut = lax.dynamic_slice_in_dim(diag_inverse, place.col * part_rows, part_rows, 1)
        sent_rows = [cut[s : s + 1] for s in range(1, steps)]
        by_x = diag_inverse[0].reshape(rows, planes, 2, rows)
        sent_first = lax.dynamic_index_in_dim(by_x, 1 - x, 2, keepdims=False)
        sent_first = sent_first.reshape(rows, total_rows // 2)
        sent_first = lax.dynamic_slice_in_dim(sent_first, core * (rows // 2), rows // 2, 0)
    first_mine = flip(sent_first, dr=1)
    first_theirs = flip(first_mine, dc=1)

    def partner_rows(s):
        pieces = {0: flip(sent_rows[s - 1], dr=1)}
        bit = n_cols // 2
        while bit:
            for dc, a in list(pieces.items()):
                pieces[dc ^ bit] = flip(a, dc=bit)
            bit //= 2
        return pieces

    partner = {s: partner_rows(s) for s in range(1, steps)}

    if kernels:
        first, send, keep = call(
            prep_kernel,
            [block_order, x_window, y_window],
            [
                ((own_cols + PAD, rows), BF16),
                ((steps - 1, height, rows), BF16),
                ((steps - 1, height, rows), F32),
            ],
            [((own_cols, rows), F32), (x_window.shape, BF16), (y_window.shape, F32)],
            hbm=(0, 1, 2),
            more=[pltpu.SMEM(block_order.shape, jnp.int32), pltpu.SemaphoreType.DMA((3,))],
        )
    else:
        xs = x_window[block_order].transpose(0, 2, 1).astype(F32)
        ys = y_window[block_order][:, None]
        high = ys.astype(BF16).astype(F32)
        fill = jnp.zeros((steps, PAD - 1, rows), F32)
        first = jnp.concatenate([xs[0], ys[0], fill[0]], 0).astype(BF16)
        keep = jnp.concatenate([lax.dynamic_slice_in_dim(xs, x * half, half, 1), ys, fill], 1)
        other = lax.dynamic_slice_in_dim(xs, (1 - x) * half, half, 1)
        send = jnp.concatenate([other, high, ys - high, fill[:, 1:]], 1).astype(BF16)
        keep, send = keep[1:], send[1:]
    first_tiles = [first] + [flip(first, dr=2 * k) for k in range(1, planes)]
    got = flip(send, dr=1)
    if kernels:
        pending = list(call(merge_kernel, [keep, got], [((height, pair), F32)] * (steps - 1)))
    else:
        resp = got[:, half:].astype(F32).sum(1, keepdims=True)
        theirs = jnp.concatenate([got[:, :half].astype(F32), resp, fill[1:]], 1)
        pending = list(ordered(keep, theirs, 2))

    panel_next = hop(panel_window, 0)
    if kernels:
        packed_panels = call(
            pack_kernel,
            [panel_window, panel_next],
            [((2, s) + panel_window.shape[1:], BF16) for s in range(1, steps)],
        )
    else:
        packed_panels = []
        for s in range(1, steps):
            at = s * (s - 1) // 2
            packed_panels.append(jnp.stack([panel_window[at : at + s], panel_next[at : at + s]]))
    panels = {}
    for s in range(1, steps):
        got_panels = finish(packed_panels[s - 1], 1)
        panels[s] = (got_panels, piece_labels(got_panels))

    factors = finish(panel_trail.transpose(1, 0, 2)[None], 0)
    factor_labels = piece_labels(factors)

    def spread(tile):
        return [tile] + [flip(tile, dr=2 * k) for k in range(1, planes)]

    def joined(tiles):
        order = place.z ^ jnp.arange(planes)
        return jnp.stack(tiles)[order].transpose(1, 0, 2).reshape(tiles[0].shape[0], -1)

    def solve(s, tiles, before, outs):
        parts = partner[s]
        listed = sorted(parts)
        if kernels:
            return call(
                functools.partial(solve_kernel, (planes, s, listed, len(before))),
                tiles + [diag_inverse] + [parts[dc] for dc in listed] + before,
                [(shape, BF16) for shape in outs],
                [((height, total_rows), BF16), ((rows, total_rows), BF16)],
            )
        order = place.col ^ jnp.arange(n_cols)
        other = jnp.stack([parts[dc][0] for dc in listed])[order].reshape(rows, total_rows)
        both = ordered(diag_inverse[s], other, 0)
        out = dot_t(joined(tiles), both).astype(BF16)
        return [
            out[height - shape[0] :] if len(shape) == 2
            else jnp.stack(before + [out[: shape[1]]])
            for shape in outs
        ]

    def update(gathered_pieces, t, tiles, base, dtype, split=False):
        arrays, labels = gathered_pieces
        count, width = arrays[0].shape[-2:]
        if kernels:
            pieces = [(i, (lead, t), where) for i, lead, where in labels]
            counts = (planes, pieces, len(arrays), base is not None, split)
            shapes = [(height, count)] * 2 if split else [(height, 2 * count)]
            return call(
                functools.partial(update_kernel, counts),
                tiles + arrays + ([] if base is None else [base]),
                [(shape, dtype) for shape in shapes],
                [((height, total_rows), BF16), ((height, 2 * count), F32)],
            )
        gathered = joined(tiles)
        total = jnp.zeros((height, 2 * count), F32) if base is None else base
        for i, lead, where in labels:
            dx, dc = where(place)
            columns = lax.dynamic_slice_in_dim(gathered, (place.col ^ dc) * width, width, 1)
            at = (x ^ dx) * count
            now = lax.dynamic_slice_in_dim(total, at, count, 1)
            now = now - dot_t(columns, arrays[i][lead, t])
            total = lax.dynamic_update_slice_in_dim(total, now, at, 1)
        if split:
            return [
                lax.dynamic_slice_in_dim(total, side * count, count, 1) for side in (x, 1 - x)
            ]
        return [total.astype(dtype)]

    if kernels:
        keep0, send0 = call(
            first_kernel,
            first_tiles + [diag_inverse, first_mine, first_theirs],
            [((height, pair), F32), ((height, pair), BF16)],
            [((own_cols + PAD, total_rows // 2), BF16), ((own_cols + PAD, pair), F32)],
        )
        got0 = flip(send0, dr=1)
        (tile,) = call(join_kernel, [keep0, got0], [((height, pair), BF16)])
    else:
        own = lax.dynamic_index_in_dim(by_x, x, 2, keepdims=False).reshape(rows, -1)
        theirs = jnp.where(
            core == 0,
            jnp.concatenate([first_mine, first_theirs], 0),
            jnp.concatenate([first_theirs, first_mine], 0),
        )
        out = dot_t(joined(first_tiles), ordered(own, theirs, 0))
        resp = out[own_cols:]
        mine = lax.dynamic_slice_in_dim(out, x * half, half, 0)
        yours = lax.dynamic_slice_in_dim(out, (1 - x) * half, half, 0)
        got0 = flip(jnp.concatenate([yours, resp], 0).astype(BF16), dr=1)
        tile = (jnp.concatenate([mine, resp], 0) + got0.astype(F32)).astype(BF16)
    solved = []
    trail = None
    for s in range(steps):
        if s > 0:
            tiles = spread(residual)
        tile_shape = (height, pair)
        if s == steps - 1:
            shapes = [tile_shape, (1, half, pair), (PAD, pair)]
            tile, copied, late_resp = solve(s, tiles, [], shapes)
            late = finish(copied[None], 0)
        elif s == steps - 2:
            tile, copied = solve(s, tiles, solved, [tile_shape, (steps - 1, height, pair)])
            early = finish(copied[None], 0)
        elif s > 0:
            (tile,) = solve(s, tiles, [], [tile_shape])
        solved.append(tile)
        tiles = spread(tile)
        if s < steps - 1:
            (residual,) = update(panels[s + 1], s, tiles, pending[s], BF16)
        for later in range(s + 2, steps):
            (pending[later - 1],) = update(panels[later], s, tiles, pending[later - 1], F32)
        last = s == steps - 1
        trail = update((factors, factor_labels), s, tiles, trail, F32, last)
        trail = trail if last else trail[0]
    trail_mine, trail_sent = trail
    trail_got = flip(trail_sent, dr=1)

    def partials(layers, arrays, resp, base, outs):
        tiles = []
        for i, lead, where in piece_labels(arrays):

            def at(p, where=where):
                dx, dc = where(p)
                return p.x ^ dx, p.col ^ dc

            tiles.append((i, lambda n, lead=lead: (lead, n), at))
        has_base, apart = base is not None, resp is not None
        counts = (planes, tiles, layers, has_base, len(arrays), apart, half)
        more = ([resp] if apart else []) + ([base] if has_base else [])
        return call(
            functools.partial(partial_kernel, counts),
            arrays + more,
            outs,
            [((layers, full, pair), BF16), ((planes, height, full), F32)],
        )

    (sums,) = partials(steps - 1, early, None, None, [((planes, height, full), F32)])
    slots = partials(1, late, late_resp, sums, [((height, full), BF16)] * planes)
    slots = [slots[0]] + [flip(slots[k], dr=2 * k) for k in range(1, planes)]
    scale = 1.0 / (steps * total_rows)
    trail_rhs, trail_resp, normal, right = call(
        functools.partial(final_kernel, scale),
        slots + [trail_mine, trail_got, x_trail, y_trail],
        [
            ((trail_rows, own_cols), F32),
            ((trail_rows,), F32),
            ((half, full), F32),
            ((half,), F32),
        ],
        plain=(planes + 2, planes + 3),
        to_hbm=True,
    )

    own = len(early) // 2
    flat = [(n, i) for n in range(own) for i in range(early[n].shape[0])]
    last_x, first_x = flat[1 << (len(hops[0]) - 1)], flat[1]
    if kernels:
        whitened, white_resp = call(
            functools.partial(white_kernel, (steps, last_x, first_x, own)),
            early[:own] + late[:own] + [late_resp],
            [((steps, rows, own_cols), BF16), ((steps, rows), BF16)],
            [((own_cols, rows), F32)],
            to_hbm=True,
        )
    else:
        outs, resps = [], []
        (a, i), (b, j) = last_x, first_x
        for s in range(steps):
            arrays, n = (early, s) if s < steps - 1 else (late, 0)
            other = jnp.where(core == 0, arrays[a][i, n, :half], arrays[b][j, n, :half])
            both = ordered(arrays[0][0, n, :half], other, 0)
            resp = early[0][0, n, half] if s < steps - 1 else late_resp[0]
            outs.append(lax.dynamic_slice_in_dim(both, x * rows, rows, 1).T)
            resps.append(lax.dynamic_slice_in_dim(resp, x * rows, rows, 0))
        whitened, white_resp = jnp.stack(outs), jnp.stack(resps)
    return whitened, white_resp, trail_rhs, trail_resp, normal, right


def solution(mesh):
    in_specs = (
        P(None, "row", "col"),
        P(None, "row"),
        P(),
        P(None, "row", None),
        P(None, "row", "col"),
        P("row", None, "col"),
        P("row", "col"),
        P("row"),
    )
    out_specs = (
        P(None, "row", "col"),
        P(None, "row"),
        P("row", "col"),
        P("row"),
        P("row", None),
        P("row"),
    )

    return jax.shard_map(shards, mesh=mesh, in_specs=in_specs, out_specs=out_specs, check_vma=False)
```

time: 447 us -> 153 us (0.34)
  blocking collectives: 314 us -> 0 us
  starting transfers between devices: 10.6 us -> 60.6 us
  between operations: 19.8 us -> 0.96 us
  matrix products: 16.5 us -> 0 us
  Pallas kernels: 0 us -> 12.6 us
  local copies, waits for them, and re-layouts: 7.06 us -> 1.16 us
  other arithmetic: 5.95 us -> 0.12 us
  waiting for transfers between devices: 72.4 us -> 77.5 us
    all_gather x12 -> x0, blocking collectives: 297 us -> none  [the longest x3 96.4 us: shards(): lax.all_gather(residual, 'row', axis=0, tiled=True)]
    ppermute x0 -> x53, waiting for transfers between devices: none -> 77.5 us  [move(): return lax.ppermute(array, ('row', 'col'), table)]
    ppermute x0 -> x53, starting transfers between devices: none -> 60.6 us  [move(): return lax.ppermute(array, ('row', 'col'), table)]
    reduce_scatter x3 -> x0, waiting for transfers between devices: 39.8 us -> none  [the longest x1 20.4 us: shards(): lax.psum_scatter(trail_total.astype(jnp.bfloat16), 'col', scatter_dimensi...]
    psum x1 -> x0, waiting for transfers between devices: 25.1 us -> none  [shards(): gram, right, resp_sum = lax.psum((gram, right, trail_resp_total), 'col')]
    psum x3 -> x0, blocking collectives: 17.1 us -> none  [the longest x2 11.3 us: shards(): pending_resp = pending_resp - lax.psum(update_resp, 'col')]
    dot_general x22 -> x0, matrix products: 16.5 us -> none  [the longest x3 5.12 us: shards(): jnp.dot(inverse, whole, preferred_element_type=jnp.float32)]
    pallas_call x0 -> x18, Pallas kernels: none -> 12.6 us  [the longest x17 11.4 us: call(): pl.pallas_call(lambda *refs: kernel(here(), *refs), in_specs=specs, out_s...]
  transfers between devices with their start and end apart: 7 -> 53, of which waited for: 4 -> 23; matrix products, arithmetic and copies ran while one was open for 3% -> 0% of each run, Pallas kernels for 0% -> 8%
where the time goes in v3:
time: 153 us
  waiting for transfers between devices  77.5 us (51%)
  starting transfers between devices  60.6 us (40%)
  Pallas kernels  12.6 us (8%)
    ppermute x53, waiting for transfers between devices, move(): return lax.ppermute(array, ('row', 'col'), table)  77.5 us
    ppermute x53, starting transfers between devices, move(): return lax.ppermute(array, ('row', 'col'), table)  60.6 us
    pallas_call x17, Pallas kernels, call(): pl.pallas_call(lambda *refs: kernel(here(), *refs), in_specs=specs, out_s...  11.4 us
  transfers between devices with their start and end apart: 53, of which 23 were waited for; matrix products, arithmetic and copies ran while one was open for 0% of the time, Pallas kernels for 8%

profile of v3, /device:TPU:0, one launch (start us, length us, event | category | flops | bytes accessed | tf_op | source)
XLA Modules:
  0.0 152.9 jit_solution(16337283822085758725)
XLA Ops:
  0.6 3.1 %collective-permute-start.9 = (bf16[3,256,512]{2,1,0:T(8,128)(2,1)}, bf16[3,256,512]{2,1,0:T(8,128)(2,1)S(1)}, u32[]{:S(2)}, u32[]{:S(2)}) collective-permute-start(bf16[3,256,512]{2,1,0:T(8,128)(2,1)} %refs_0_.3), channel_id=1, source_target_pairs={{0,2},{1,5},{2,0},{3,7},{4,6},{5,1},{6,4},{7,3},{8,10},{9,13},{10,... | collective-permute-start | bytes 2359304 | tf_op jit(solution)/shard_map/ppermute | solution.py:305
  3.7 10.2 %collective-permute-done.9.refs_1_ = bf16[3,256,512]{2,1,0:T(8,128)(2,1)S(1)} collective-permute-done((bf16[3,256,512]{2,1,0:T(8,128)(2,1)}, bf16[3,256,512]{2,1,0:T(8,128)(2,1)S(1)}, u32[]{:S(2)}, u32[]{:S(2)}) %collective-permute-start.9) | collective-permute-done | bytes 786464 | tf_op jit(solution)/shard_map/ppermute | solution.py:305
  13.9 1.1 copy-done.1
  15.1 2.1 %collective-permute-start.26 = (bf16[2,2,256,512]{3,2,1,0:T(8,128)(2,1)S(1)}, bf16[2,2,256,512]{3,2,1,0:T(8,128)(2,1)S(1)}, u32[]{:S(2)}, u32[]{:S(2)}) collective-permute-start(bf16[2,2,256,512]{3,2,1,0:T(8,128)(2,1)S(1)} %get-tuple-element.46.refs_4_), channel_id=1, source_target_pairs={{0,4},{1,3},{2,6},{3,1},{4,0},{5,7},{6,2},{7,5},{8,12},{9,11},{10,... | collective-permute-start | bytes 3145736 | tf_op jit(solution)/shard_map/ppermute | solution.py:305
  17.2 1.2 parts.1
  18.5 1.1 shard_map.127
  19.6 2.1 %collective-permute-start = (bf16[136,256]{1,0:T(8,128)(2,1)S(1)}, bf16[136,256]{1,0:T(8,128)(2,1)S(1)}, u32[]{:S(2)}, u32[]{:S(2)}) collective-permute-start(bf16[136,256]{1,0:T(8,128)(2,1)S(1)} %get-tuple-element.35.refs_0_), channel_id=1, source_target_pairs={{0,8},{1,9},{2,10},{3,11},{4,12},{5,13},{6,14},{7,15},{8,0},{9,1},... | collective-permute-start | bytes 208904 | tf_op jit(solution)/shard_map/ppermute | solution.py:305
  21.8 1.5 collective-permute-start.17
  23.3 2.6 %collective-permute-start.1 = (bf16[136,256]{1,0:T(8,128)(2,1)S(1)}, bf16[136,256]{1,0:T(8,128)(2,1)S(1)}, u32[]{:S(2)}, u32[]{:S(2)}) collective-permute-start(bf16[136,256]{1,0:T(8,128)(2,1)S(1)} %get-tuple-element.35.refs_0_), channel_id=1, source_target_pairs={{0,16},{1,17},{2,18},{3,19},{4,20},{5,21},{6,22},{7,23},{8,24},{9,... | collective-permute-start | bytes 208904 | tf_op jit(solution)/shard_map/ppermute | solution.py:305
  25.9 2.8 %collective-permute-start.2 = (bf16[136,256]{1,0:T(8,128)(2,1)S(1)}, bf16[136,256]{1,0:T(8,128)(2,1)S(1)}, u32[]{:S(2)}, u32[]{:S(2)}) collective-permute-start(bf16[136,256]{1,0:T(8,128)(2,1)S(1)} %get-tuple-element.35.refs_0_), channel_id=1, source_target_pairs={{0,24},{1,25},{2,26},{3,27},{4,28},{5,29},{6,30},{7,31},{8,16},{9,... | collective-permute-start | bytes 208904 | tf_op jit(solution)/shard_map/ppermute | solution.py:305
  28.6 1.2 collective-permute-done.1.refs_2_
  29.9 0.6 collective-permute-start.13
  30.5 1.5 collective-permute-done.2.refs_3_
  32.0 0.5 collective-permute-start.32
  32.5 9.5 %collective-permute-done.3.refs_5_ = bf16[128,1024]{1,0:T(8,128)(2,1)S(1)} collective-permute-done((bf16[128,1024]{1,0:T(8,128)(2,1)S(1)}, bf16[128,1024]{1,0:T(8,128)(2,1)S(1)}, u32[]{:S(2)}, u32[]{:S(2)}) %collective-permute-start.3) | collective-permute-done | bytes 262176 | tf_op jit(solution)/shard_map/ppermute | solution.py:305
  42.0 3.8 %collective-permute-done.13.refs_1_ = bf16[2,72,256]{2,1,0:T(8,128)(2,1)S(1)} collective-permute-done((bf16[2,72,256]{2,1,0:T(8,128)(2,1)S(1)}, bf16[2,72,256]{2,1,0:T(8,128)(2,1)S(1)}, u32[]{:S(2)}, u32[]{:S(2)}) %collective-permute-start.13) | collective-permute-done | bytes 73760 | tf_op jit(solution)/shard_map/ppermute | solution.py:305
  45.9 1.6 %collective-permute-start.48 = (bf16[1,3,128,512]{3,2,1,0:T(8,128)(2,1)S(1)}, bf16[1,3,128,512]{3,2,1,0:T(8,128)(2,1)S(1)}, u32[]{:S(2)}, u32[]{:S(2)}) collective-permute-start(bf16[1,3,128,512]{3,2,1,0:T(8,128)(2,1)S(1)} %bitcast.9), channel_id=1, source_target_pairs={{0,2},{1,5},{2,0},{3,7},{4,6},{5,1},{6,4},{7,3},{8,10},{9,13},{10,... | collective-permute-start | bytes 1179656 | tf_op jit(solution)/shard_map/ppermute | solution.py:305
  47.5 1.7 %collective-permute-start.10 = (bf16[2,1,256,512]{3,2,1,0:T(8,128)(2,1)S(1)}, bf16[2,1,256,512]{3,2,1,0:T(8,128)(2,1)S(1)}, u32[]{:S(2)}, u32[]{:S(2)}) collective-permute-start(bf16[2,1,256,512]{3,2,1,0:T(8,128)(2,1)S(1)} %get-tuple-element.39.refs_4_), channel_id=1, source_target_pairs={{0,4},{1,3},{2,6},{3,1},{4,0},{5,7},{6,2},{7,5},{8,12},{9,11},{10,... | collective-permute-start | bytes 1572872 | tf_op jit(solution)/shard_map/ppermute | solution.py:305
  49.2 2.3 %collective-permute-done.32.refs_5_ = bf16[1,64,2048]{2,1,0:T(8,128)(2,1)S(1)} collective-permute-done((bf16[1,64,2048]{2,1,0:T(8,128)(2,1)S(1)}, bf16[1,64,2048]{2,1,0:T(8,128)(2,1)S(1)}, u32[]{:S(2)}, u32[]{:S(2)}) %collective-permute-start.32) | collective-permute-done | bytes 262176 | tf_op jit(solution)/shard_map/ppermute | solution.py:305
  51.5 1.6 %collective-permute-start.19 = (bf16[1,64,2048]{2,1,0:T(8,128)(2,1)S(1)}, bf16[1,64,2048]{2,1,0:T(8,128)(2,1)S(1)}, u32[]{:S(2)}, u32[]{:S(2)}) collective-permute-start(bf16[1,64,2048]{2,1,0:T(8,128)(2,1)S(1)} %collective-permute-done.17.refs_5_), channel_id=1, source_target_pairs={{0,2},{1,3},{2,0},{3,1},{4,6},{5,7},{6,4},{7,5},{8,10},{9,11},{10,... | collective-permute-start | bytes 786440 | tf_op jit(solution)/shard_map/ppermute | solution.py:305
  53.6 4.2 %collective-permute-done.48 = bf16[1,3,128,512]{3,2,1,0:T(8,128)(2,1)S(1)} collective-permute-done((bf16[1,3,128,512]{3,2,1,0:T(8,128)(2,1)S(1)}, bf16[1,3,128,512]{3,2,1,0:T(8,128)(2,1)S(1)}, u32[]{:S(2)}, u32[]{:S(2)}) %collective-permute-start.48) | collective-permute-done | bytes 393248 | tf_op jit(solution)/shard_map/ppermute | solution.py:305
  57.8 4.3 %collective-permute-done.5.refs_1_ = bf16[72,512]{1,0:T(8,128)(2,1)S(1)} collective-permute-done((bf16[72,512]{1,0:T(8,128)(2,1)S(1)}, bf16[72,512]{1,0:T(8,128)(2,1)S(1)}, u32[]{:S(2)}, u32[]{:S(2)}) %collective-permute-start.5) | collective-permute-done | bytes 73760 | tf_op jit(solution)/shard_map/ppermute | solution.py:305
  62.2 1.8 %collective-permute-start.6 = (bf16[72,512]{1,0:T(8,128)(2,1)S(1)}, bf16[72,512]{1,0:T(8,128)(2,1)S(1)}, u32[]{:S(2)}, u32[]{:S(2)}) collective-permute-start(bf16[72,512]{1,0:T(8,128)(2,1)S(1)} %shard_map.129.refs_0_.refs_9_), channel_id=1, source_target_pairs={{0,8},{1,9},{2,10},{3,11},{4,12},{5,13},{6,14},{7,15},{8,0},{9,1},... | collective-permute-start | bytes 221192 | tf_op jit(solution)/shard_map/ppermute | solution.py:305
  64.3 2.7 %collective-permute-done.6.refs_1_ = bf16[72,512]{1,0:T(8,128)(2,1)S(1)} collective-permute-done((bf16[72,512]{1,0:T(8,128)(2,1)S(1)}, bf16[72,512]{1,0:T(8,128)(2,1)S(1)}, u32[]{:S(2)}, u32[]{:S(2)}) %collective-permute-start.6) | collective-permute-done | bytes 73760 | tf_op jit(solution)/shard_map/ppermute | solution.py:305
  67.0 2.8 %collective-permute-start.7 = (bf16[72,512]{1,0:T(8,128)(2,1)S(1)}, bf16[72,512]{1,0:T(8,128)(2,1)S(1)}, u32[]{:S(2)}, u32[]{:S(2)}) collective-permute-start(bf16[72,512]{1,0:T(8,128)(2,1)S(1)} %shard_map.129.refs_0_.refs_9_), channel_id=1, source_target_pairs={{0,16},{1,17},{2,18},{3,19},{4,20},{5,21},{6,22},{7,23},{8,24},{9,... | collective-permute-start | bytes 221192 | tf_op jit(solution)/shard_map/ppermute | solution.py:305
  69.8 3.9 %collective-permute-done.7.refs_2_ = bf16[72,512]{1,0:T(8,128)(2,1)S(1)} collective-permute-done((bf16[72,512]{1,0:T(8,128)(2,1)S(1)}, bf16[72,512]{1,0:T(8,128)(2,1)S(1)}, u32[]{:S(2)}, u32[]{:S(2)}) %collective-permute-start.7) | collective-permute-done | bytes 73760 | tf_op jit(solution)/shard_map/ppermute | solution.py:305
  73.7 3.3 %collective-permute-start.8 = (bf16[72,512]{1,0:T(8,128)(2,1)S(1)}, bf16[72,512]{1,0:T(8,128)(2,1)S(1)}, u32[]{:S(2)}, u32[]{:S(2)}) collective-permute-start(bf16[72,512]{1,0:T(8,128)(2,1)S(1)} %shard_map.129.refs_0_.refs_9_), channel_id=1, source_target_pairs={{0,24},{1,25},{2,26},{3,27},{4,28},{5,29},{6,30},{7,31},{8,16},{9,... | collective-permute-start | bytes 221192 | tf_op jit(solution)/shard_map/ppermute | solution.py:305
  77.5 2.3 %collective-permute-done.8.refs_3_ = bf16[72,512]{1,0:T(8,128)(2,1)S(1)} collective-permute-done((bf16[72,512]{1,0:T(8,128)(2,1)S(1)}, bf16[72,512]{1,0:T(8,128)(2,1)S(1)}, u32[]{:S(2)}, u32[]{:S(2)}) %collective-permute-start.8) | collective-permute-done | bytes 73760 | tf_op jit(solution)/shard_map/ppermute | solution.py:305
  79.9 1.1 collective-permute-start.34
  81.0 0.8 shard_map.132.refs_0_
  81.9 4.3 %collective-permute-done.14.refs_1_ = bf16[72,512]{1,0:T(8,128)(2,1)S(1)} collective-permute-done((bf16[72,512]{1,0:T(8,128)(2,1)S(1)}, bf16[72,512]{1,0:T(8,128)(2,1)S(1)}, u32[]{:S(2)}, u32[]{:S(2)}) %collective-permute-start.14) | collective-permute-done | bytes 73760 | tf_op jit(solution)/shard_map/ppermute | solution.py:305
  86.2 2.1 %collective-permute-start.15 = (bf16[72,512]{1,0:T(8,128)(2,1)S(1)}, bf16[72,512]{1,0:T(8,128)(2,1)S(1)}, u32[]{:S(2)}, u32[]{:S(2)}) collective-permute-start(bf16[72,512]{1,0:T(8,128)(2,1)S(1)} %shard_map.132.refs_0_), channel_id=1, source_target_pairs={{0,16},{1,17},{2,18},{3,19},{4,20},{5,21},{6,22},{7,23},{8,24},{9,... | collective-permute-start | bytes 221192 | tf_op jit(solution)/shard_map/ppermute | solution.py:305
  88.3 4.0 %collective-permute-done.15.refs_2_ = bf16[72,512]{1,0:T(8,128)(2,1)S(1)} collective-permute-done((bf16[72,512]{1,0:T(8,128)(2,1)S(1)}, bf16[72,512]{1,0:T(8,128)(2,1)S(1)}, u32[]{:S(2)}, u32[]{:S(2)}) %collective-permute-start.15) | collective-permute-done | bytes 73760 | tf_op jit(solution)/shard_map/ppermute | solution.py:305
  92.3 3.1 %collective-permute-start.16 = (bf16[72,512]{1,0:T(8,128)(2,1)S(1)}, bf16[72,512]{1,0:T(8,128)(2,1)S(1)}, u32[]{:S(2)}, u32[]{:S(2)}) collective-permute-start(bf16[72,512]{1,0:T(8,128)(2,1)S(1)} %shard_map.132.refs_0_), channel_id=1, source_target_pairs={{0,24},{1,25},{2,26},{3,27},{4,28},{5,29},{6,30},{7,31},{8,16},{9,... | collective-permute-start | bytes 221192 | tf_op jit(solution)/shard_map/ppermute | solution.py:305
  95.4 3.0 %collective-permute-done.16.refs_3_ = bf16[72,512]{1,0:T(8,128)(2,1)S(1)} collective-permute-done((bf16[72,512]{1,0:T(8,128)(2,1)S(1)}, bf16[72,512]{1,0:T(8,128)(2,1)S(1)}, u32[]{:S(2)}, u32[]{:S(2)}) %collective-permute-start.16) | collective-permute-done | bytes 73760 | tf_op jit(solution)/shard_map/ppermute | solution.py:305
  98.4 0.8 shard_map.133
  99.2 1.0 collective-permute-start.21
  100.3 3.7 %collective-permute-start.24 = (bf16[72,512]{1,0:T(8,128)(2,1)S(1)}, bf16[72,512]{1,0:T(8,128)(2,1)S(1)}, u32[]{:S(2)}, u32[]{:S(2)}) collective-permute-start(bf16[72,512]{1,0:T(8,128)(2,1)S(1)} %get-tuple-element.45.refs_0_), channel_id=1, source_target_pairs={{0,16},{1,17},{2,18},{3,19},{4,20},{5,21},{6,22},{7,23},{8,24},{9,... | collective-permute-start | bytes 221192 | tf_op jit(solution)/shard_map/ppermute | solution.py:305
  104.0 0.7 collective-permute-start.25
  105.0 3.3 %collective-permute-done.24.refs_2_ = bf16[72,512]{1,0:T(8,128)(2,1)S(1)} collective-permute-done((bf16[72,512]{1,0:T(8,128)(2,1)S(1)}, bf16[72,512]{1,0:T(8,128)(2,1)S(1)}, u32[]{:S(2)}, u32[]{:S(2)}) %collective-permute-start.24) | collective-permute-done | bytes 73760 | tf_op jit(solution)/shard_map/ppermute | solution.py:305
  108.3 1.8 %collective-permute-done.25.refs_3_ = bf16[72,512]{1,0:T(8,128)(2,1)S(1)} collective-permute-done((bf16[72,512]{1,0:T(8,128)(2,1)S(1)}, bf16[72,512]{1,0:T(8,128)(2,1)S(1)}, u32[]{:S(2)}, u32[]{:S(2)}) %collective-permute-start.25) | collective-permute-done | bytes 73760 | tf_op jit(solution)/shard_map/ppermute | solution.py:305
  110.7 2.1 %collective-permute-start.22 = (bf16[2,2,72,512]{3,2,1,0:T(8,128)(2,1)S(1)}, bf16[2,2,72,512]{3,2,1,0:T(8,128)(2,1)S(1)}, u32[]{:S(2)}, u32[]{:S(2)}) collective-permute-start(bf16[2,2,72,512]{3,2,1,0:T(8,128)(2,1)S(1)} %pad_maximum_fusion.1.refs_0_), channel_id=1, source_target_pairs={{0,4},{1,3},{2,6},{3,1},{4,0},{5,7},{6,2},{7,5},{8,12},{9,11},{10,... | collective-permute-start | bytes 884744 | tf_op jit(solution)/shard_map/ppermute | solution.py:305
  112.8 0.8 shard_map.134.refs_8_
  113.6 0.8 shard_map.135.refs_0_
  114.5 1.4 collective-permute-start.30
  115.9 2.9 %collective-permute-done.29.refs_1_ = bf16[72,512]{1,0:T(8,128)(2,1)S(1)} collective-permute-done((bf16[72,512]{1,0:T(8,128)(2,1)S(1)}, bf16[72,512]{1,0:T(8,128)(2,1)S(1)}, u32[]{:S(2)}, u32[]{:S(2)}) %collective-permute-start.29) | collective-permute-done | bytes 73760 | tf_op jit(solution)/shard_map/ppermute | solution.py:305
  118.8 1.7 %collective-permute-start.31 = (bf16[72,512]{1,0:T(8,128)(2,1)S(1)}, bf16[72,512]{1,0:T(8,128)(2,1)S(1)}, u32[]{:S(2)}, u32[]{:S(2)}) collective-permute-start(bf16[72,512]{1,0:T(8,128)(2,1)S(1)} %shard_map.135.refs_0_), channel_id=1, source_target_pairs={{0,24},{1,25},{2,26},{3,27},{4,28},{5,29},{6,30},{7,31},{8,16},{9,... | collective-permute-start | bytes 221192 | tf_op jit(solution)/shard_map/ppermute | solution.py:305
  120.5 1.8 %collective-permute-done.30.refs_2_ = bf16[72,512]{1,0:T(8,128)(2,1)S(1)} collective-permute-done((bf16[72,512]{1,0:T(8,128)(2,1)S(1)}, bf16[72,512]{1,0:T(8,128)(2,1)S(1)}, u32[]{:S(2)}, u32[]{:S(2)}) %collective-permute-start.30) | collective-permute-done | bytes 73760 | tf_op jit(solution)/shard_map/ppermute | solution.py:305
  122.2 2.7 %collective-permute-done.31.refs_3_ = bf16[72,512]{1,0:T(8,128)(2,1)S(1)} collective-permute-done((bf16[72,512]{1,0:T(8,128)(2,1)S(1)}, bf16[72,512]{1,0:T(8,128)(2,1)S(1)}, u32[]{:S(2)}, u32[]{:S(2)}) %collective-permute-start.31) | collective-permute-done | bytes 73760 | tf_op jit(solution)/shard_map/ppermute | solution.py:305
  124.9 0.8 shard_map.136
  125.7 1.1 collective-permute-start.36
  127.3 2.7 %collective-permute-done.36 = bf16[1,1,64,512]{3,2,1,0:T(8,128)(2,1)S(1)} collective-permute-done((bf16[1,1,64,512]{3,2,1,0:T(8,128)(2,1)S(1)}, bf16[1,1,64,512]{3,2,1,0:T(8,128)(2,1)S(1)}, u32[]{:S(2)}, u32[]{:S(2)}) %collective-permute-start.36) | collective-permute-done | bytes 65568 | tf_op jit(solution)/shard_map/ppermute | solution.py:305
  130.1 1.8 %collective-permute-start.37 = (bf16[2,1,64,512]{3,2,1,0:T(8,128)(2,1)S(1)}, bf16[2,1,64,512]{3,2,1,0:T(8,128)(2,1)S(1)}, u32[]{:S(2)}, u32[]{:S(2)}) collective-permute-start(bf16[2,1,64,512]{3,2,1,0:T(8,128)(2,1)S(1)} %pad_maximum_fusion.2.refs_2_.refs_0_), channel_id=1, source_target_pairs={{0,4},{1,3},{2,6},{3,1},{4,0},{5,7},{6,2},{7,5},{8,12},{9,11},{10,... | collective-permute-start | bytes 393224 | tf_op jit(solution)/shard_map/ppermute | solution.py:305
  131.9 3.2 %collective-permute-done.37.refs_3_.refs_1_ = bf16[2,1,64,512]{3,2,1,0:T(8,128)(2,1)S(1)} collective-permute-done((bf16[2,1,64,512]{3,2,1,0:T(8,128)(2,1)S(1)}, bf16[2,1,64,512]{3,2,1,0:T(8,128)(2,1)S(1)}, u32[]{:S(2)}, u32[]{:S(2)}) %collective-permute-start.37) | collective-permute-done | bytes 131104 | tf_op jit(solution)/shard_map/ppermute | solution.py:305
  135.1 2.3 %collective-permute-start.46 = (bf16[72,512]{1,0:T(8,128)(2,1)S(1)}, bf16[72,512]{1,0:T(8,128)(2,1)S(1)}, u32[]{:S(2)}, u32[]{:S(2)}) collective-permute-start(bf16[72,512]{1,0:T(8,128)(2,1)S(1)} %get-tuple-element.57.refs_0_), channel_id=1, source_target_pairs={{0,16},{1,17},{2,18},{3,19},{4,20},{5,21},{6,22},{7,23},{8,24},{9,... | collective-permute-start | bytes 221192 | tf_op jit(solution)/shard_map/ppermute | solution.py:305
  137.4 2.1 %collective-permute-start.47 = (bf16[72,512]{1,0:T(8,128)(2,1)S(1)}, bf16[72,512]{1,0:T(8,128)(2,1)S(1)}, u32[]{:S(2)}, u32[]{:S(2)}) collective-permute-start(bf16[72,512]{1,0:T(8,128)(2,1)S(1)} %get-tuple-element.57.refs_0_), channel_id=1, source_target_pairs={{0,24},{1,25},{2,26},{3,27},{4,28},{5,29},{6,30},{7,31},{8,16},{9,... | collective-permute-start | bytes 221192 | tf_op jit(solution)/shard_map/ppermute | solution.py:305
  139.5 1.6 %shard_map.138.refs_5_ = f32[4,72,512]{2,1,0:T(8,128)S(1)} custom-call(bf16[2,2,72,512]{3,2,1,0:T(8,128)(2,1)S(1)} %pad_maximum_fusion.1.refs_0_, bf16[2,2,72,512]{3,2,1,0:T(8,128)(2,1)S(1)} %collective-permute-done.22.refs_1_, bf16[2,2,72,512]{3,2,1,0:T(8,128)(2,1)S(1)} %collective-permute-done.40.refs_2_, ...), custom_call_target="tpu_custom_call" | custom-call | tf_op jit(solution)/shard_map/pallas_call | solution.py:49
  141.1 0.9 shard_map.139
  142.1 2.2 %collective-permute-start.43 = (bf16[72,512]{1,0:T(8,128)(2,1)S(1)}, bf16[72,512]{1,0:T(8,128)(2,1)S(1)}, u32[]{:S(2)}, u32[]{:S(2)}) collective-permute-start(bf16[72,512]{1,0:T(8,128)(2,1)S(1)} %get-tuple-element.55), channel_id=1, source_target_pairs={{0,16},{1,17},{2,18},{3,19},{4,20},{5,21},{6,22},{7,23},{8,24},{9,... | collective-permute-start | bytes 221192 | tf_op jit(solution)/shard_map/ppermute | solution.py:305
  144.3 2.1 %collective-permute-start.44 = (bf16[72,512]{1,0:T(8,128)(2,1)S(1)}, bf16[72,512]{1,0:T(8,128)(2,1)S(1)}, u32[]{:S(2)}, u32[]{:S(2)}) collective-permute-start(bf16[72,512]{1,0:T(8,128)(2,1)S(1)} %get-tuple-element.56), channel_id=1, source_target_pairs={{0,24},{1,25},{2,26},{3,27},{4,28},{5,29},{6,30},{7,31},{8,16},{9,... | collective-permute-start | bytes 221192 | tf_op jit(solution)/shard_map/ppermute | solution.py:305
  148.0 1.8 %collective-permute-start.52 = (f32[72,128]{1,0:T(8,128)S(1)}, f32[72,128]{1,0:T(8,128)S(1)}, u32[]{:S(2)}, u32[]{:S(2)}) collective-permute-start(f32[72,128]{1,0:T(8,128)S(1)} %get-tuple-element.59), channel_id=1, source_target_pairs={{0,4},{1,5},{2,6},{3,7},{4,0},{5,1},{6,2},{7,3},{8,12},{9,13},{10,... | collective-permute-start | bytes 110600 | tf_op jit(solution)/shard_map/ppermute | solution.py:305
  149.8 0.9 shard_map.137
  150.7 1.3 collective-permute-done.52.refs_5_
  152.1 0.8 shard_map.143
  (73 shorter events, 4.8 us)
Async XLA Ops:
  0.6 52.5 %copy-start = (bf16[3,256,2048]{2,1,0:T(8,128)(2,1)S(1)}, bf16[3,256,2048]{2,1,0:T(8,128)(2,1)}, u32[]{:S(2)}) copy-start(bf16[3,256,2048]{2,1,0:T(8,128)(2,1)} %refs_4_.5) | copy-start | bytes 9437188
  0.6 13.2 %collective-permute-start.9 = (bf16[3,256,512]{2,1,0:T(8,128)(2,1)}, bf16[3,256,512]{2,1,0:T(8,128)(2,1)S(1)}, u32[]{:S(2)}, u32[]{:S(2)}) collective-permute-start(bf16[3,256,512]{2,1,0:T(8,128)(2,1)} %refs_0_.3), channel_id=1, source_target_pairs={{0,2},{1,5},{2,0},{3,7},{4,6},{5,1},{6,4},{7,3},{8,10},{9,13},{10,... | collective-permute-start | bytes 2359304 | tf_op jit(solution)/shard_map/ppermute | solution.py:305
  13.9 1.1 copy-start.1
  15.0 30.8 %copy-start.4 = (bf16[128,3,512]{2,0,1:T(8,128)(2,1)S(1)}, bf16[128,3,512]{2,0,1:T(8,128)(2,1)}, u32[]{:S(2)}) copy-start(bf16[128,3,512]{2,0,1:T(8,128)(2,1)} %param.13) | copy-start | bytes 1179652
  15.1 61.8 %collective-permute-start.26 = (bf16[2,2,256,512]{3,2,1,0:T(8,128)(2,1)S(1)}, bf16[2,2,256,512]{3,2,1,0:T(8,128)(2,1)S(1)}, u32[]{:S(2)}, u32[]{:S(2)}) collective-permute-start(bf16[2,2,256,512]{3,2,1,0:T(8,128)(2,1)S(1)} %get-tuple-element.46.refs_4_), channel_id=1, source_target_pairs={{0,4},{1,3},{2,6},{3,1},{4,0},{5,7},{6,2},{7,5},{8,12},{9,11},{10,... | collective-permute-start | bytes 3145736 | tf_op jit(solution)/shard_map/ppermute | solution.py:305
  18.4 23.6 %collective-permute-start.3 = (bf16[128,1024]{1,0:T(8,128)(2,1)S(1)}, bf16[128,1024]{1,0:T(8,128)(2,1)S(1)}, u32[]{:S(2)}, u32[]{:S(2)}) collective-permute-start(bf16[128,1024]{1,0:T(8,128)(2,1)S(1)} %get-tuple-element.36), channel_id=1, source_target_pairs={{0,4},{1,5},{2,6},{3,7},{4,0},{5,1},{6,2},{7,3},{8,12},{9,13},{10,... | collective-permute-start | bytes 786440 | tf_op jit(solution)/shard_map/ppermute | solution.py:305
  19.6 6.2 %collective-permute-start = (bf16[136,256]{1,0:T(8,128)(2,1)S(1)}, bf16[136,256]{1,0:T(8,128)(2,1)S(1)}, u32[]{:S(2)}, u32[]{:S(2)}) collective-permute-start(bf16[136,256]{1,0:T(8,128)(2,1)S(1)} %get-tuple-element.35.refs_0_), channel_id=1, source_target_pairs={{0,8},{1,9},{2,10},{3,11},{4,12},{5,13},{6,14},{7,15},{8,0},{9,1},... | collective-permute-start | bytes 208904 | tf_op jit(solution)/shard_map/ppermute | solution.py:305
  21.8 25.7 %collective-permute-start.17 = (bf16[1,64,2048]{2,1,0:T(8,128)(2,1)S(1)}, bf16[1,64,2048]{2,1,0:T(8,128)(2,1)S(1)}, u32[]{:S(2)}, u32[]{:S(2)}) collective-permute-start(bf16[1,64,2048]{2,1,0:T(8,128)(2,1)S(1)} %get-tuple-element.43), channel_id=1, source_target_pairs={{0,4},{1,5},{2,6},{3,7},{4,0},{5,1},{6,2},{7,3},{8,12},{9,13},{10,... | collective-permute-start | bytes 786440 | tf_op jit(solution)/shard_map/ppermute | solution.py:305
  23.3 6.6 %collective-permute-start.1 = (bf16[136,256]{1,0:T(8,128)(2,1)S(1)}, bf16[136,256]{1,0:T(8,128)(2,1)S(1)}, u32[]{:S(2)}, u32[]{:S(2)}) collective-permute-start(bf16[136,256]{1,0:T(8,128)(2,1)S(1)} %get-tuple-element.35.refs_0_), channel_id=1, source_target_pairs={{0,16},{1,17},{2,18},{3,19},{4,20},{5,21},{6,22},{7,23},{8,24},{9,... | collective-permute-start | bytes 208904 | tf_op jit(solution)/shard_map/ppermute | solution.py:305
  25.9 6.1 %collective-permute-start.2 = (bf16[136,256]{1,0:T(8,128)(2,1)S(1)}, bf16[136,256]{1,0:T(8,128)(2,1)S(1)}, u32[]{:S(2)}, u32[]{:S(2)}) collective-permute-start(bf16[136,256]{1,0:T(8,128)(2,1)S(1)} %get-tuple-element.35.refs_0_), channel_id=1, source_target_pairs={{0,24},{1,25},{2,26},{3,27},{4,28},{5,29},{6,30},{7,31},{8,16},{9,... | collective-permute-start | bytes 208904 | tf_op jit(solution)/shard_map/ppermute | solution.py:305
  29.9 16.0 %collective-permute-start.13 = (bf16[2,72,256]{2,1,0:T(8,128)(2,1)S(1)}, bf16[2,72,256]{2,1,0:T(8,128)(2,1)S(1)}, u32[]{:S(2)}, u32[]{:S(2)}) collective-permute-start(bf16[2,72,256]{2,1,0:T(8,128)(2,1)S(1)} %get-tuple-element.41), channel_id=1, source_target_pairs={{0,4},{1,5},{2,6},{3,7},{4,0},{5,1},{6,2},{7,3},{8,12},{9,13},{10,... | collective-permute-start | bytes 221192 | tf_op jit(solution)/shard_map/ppermute | solution.py:305
  32.0 19.5 %collective-permute-start.32 = (bf16[1,64,2048]{2,1,0:T(8,128)(2,1)S(1)}, bf16[1,64,2048]{2,1,0:T(8,128)(2,1)S(1)}, u32[]{:S(2)}, u32[]{:S(2)}) collective-permute-start(bf16[1,64,2048]{2,1,0:T(8,128)(2,1)S(1)} %get-tuple-element.48), channel_id=1, source_target_pairs={{0,4},{1,5},{2,6},{3,7},{4,0},{5,1},{6,2},{7,3},{8,12},{9,13},{10,... | collective-permute-start | bytes 786440 | tf_op jit(solution)/shard_map/ppermute | solution.py:305
  42.0 9.5 %collective-permute-start.4 = (bf16[128,1024]{1,0:T(8,128)(2,1)S(1)}, bf16[128,1024]{1,0:T(8,128)(2,1)S(1)}, u32[]{:S(2)}, u32[]{:S(2)}) collective-permute-start(bf16[128,1024]{1,0:T(8,128)(2,1)S(1)} %collective-permute-done.3.refs_5_), channel_id=1, source_target_pairs={{0,1},{1,0},{2,3},{3,2},{4,5},{5,4},{6,7},{7,6},{8,9},{9,8},{10,11... | collective-permute-start | bytes 786440 | tf_op jit(solution)/shard_map/ppermute | solution.py:305
  45.9 12.0 %collective-permute-start.48 = (bf16[1,3,128,512]{3,2,1,0:T(8,128)(2,1)S(1)}, bf16[1,3,128,512]{3,2,1,0:T(8,128)(2,1)S(1)}, u32[]{:S(2)}, u32[]{:S(2)}) collective-permute-start(bf16[1,3,128,512]{3,2,1,0:T(8,128)(2,1)S(1)} %bitcast.9), channel_id=1, source_target_pairs={{0,2},{1,5},{2,0},{3,7},{4,6},{5,1},{6,4},{7,3},{8,10},{9,13},{10,... | collective-permute-start | bytes 1179656 | tf_op jit(solution)/shard_map/ppermute | solution.py:305
  47.5 29.5 %collective-permute-start.10 = (bf16[2,1,256,512]{3,2,1,0:T(8,128)(2,1)S(1)}, bf16[2,1,256,512]{3,2,1,0:T(8,128)(2,1)S(1)}, u32[]{:S(2)}, u32[]{:S(2)}) collective-permute-start(bf16[2,1,256,512]{3,2,1,0:T(8,128)(2,1)S(1)} %get-tuple-element.39.refs_4_), channel_id=1, source_target_pairs={{0,4},{1,3},{2,6},{3,1},{4,0},{5,7},{6,2},{7,5},{8,12},{9,11},{10,... | collective-permute-start | bytes 1572872 | tf_op jit(solution)/shard_map/ppermute | solution.py:305
  51.5 10.8 %collective-permute-start.18 = (bf16[1,64,2048]{2,1,0:T(8,128)(2,1)S(1)}, bf16[1,64,2048]{2,1,0:T(8,128)(2,1)S(1)}, u32[]{:S(2)}, u32[]{:S(2)}) collective-permute-start(bf16[1,64,2048]{2,1,0:T(8,128)(2,1)S(1)} %collective-permute-done.17.refs_5_), channel_id=1, source_target_pairs={{0,1},{1,0},{2,3},{3,2},{4,5},{5,4},{6,7},{7,6},{8,9},{9,8},{10,11... | collective-permute-start | bytes 786440 | tf_op jit(solution)/shard_map/ppermute | solution.py:305
  51.5 12.6 %collective-permute-start.19 = (bf16[1,64,2048]{2,1,0:T(8,128)(2,1)S(1)}, bf16[1,64,2048]{2,1,0:T(8,128)(2,1)S(1)}, u32[]{:S(2)}, u32[]{:S(2)}) collective-permute-start(bf16[1,64,2048]{2,1,0:T(8,128)(2,1)S(1)} %collective-permute-done.17.refs_5_), channel_id=1, source_target_pairs={{0,2},{1,3},{2,0},{3,1},{4,6},{5,7},{6,4},{7,5},{8,10},{9,11},{10,... | collective-permute-start | bytes 786440 | tf_op jit(solution)/shard_map/ppermute | solution.py:305
  57.8 4.4 %collective-permute-start.5 = (bf16[72,512]{1,0:T(8,128)(2,1)S(1)}, bf16[72,512]{1,0:T(8,128)(2,1)S(1)}, u32[]{:S(2)}, u32[]{:S(2)}) collective-permute-start(bf16[72,512]{1,0:T(8,128)(2,1)S(1)} %get-tuple-element.38), channel_id=1, source_target_pairs={{0,4},{1,5},{2,6},{3,7},{4,0},{5,1},{6,2},{7,3},{8,12},{9,13},{10,... | collective-permute-start | bytes 221192 | tf_op jit(solution)/shard_map/ppermute | solution.py:305
  62.2 17.6 %collective-permute-start.11 = (bf16[2,1,256,512]{3,2,1,0:T(8,128)(2,1)S(1)}, bf16[2,1,256,512]{3,2,1,0:T(8,128)(2,1)S(1)}, u32[]{:S(2)}, u32[]{:S(2)}) collective-permute-start(bf16[2,1,256,512]{3,2,1,0:T(8,128)(2,1)S(1)} %get-tuple-element.39.refs_4_), channel_id=1, source_target_pairs={{0,1},{1,0},{2,3},{3,2},{4,5},{5,4},{6,7},{7,6},{8,9},{9,8},{10,11... | collective-permute-start | bytes 1572872 | tf_op jit(solution)/shard_map/ppermute | solution.py:305
  62.2 4.8 %collective-permute-start.6 = (bf16[72,512]{1,0:T(8,128)(2,1)S(1)}, bf16[72,512]{1,0:T(8,128)(2,1)S(1)}, u32[]{:S(2)}, u32[]{:S(2)}) collective-permute-start(bf16[72,512]{1,0:T(8,128)(2,1)S(1)} %shard_map.129.refs_0_.refs_9_), channel_id=1, source_target_pairs={{0,8},{1,9},{2,10},{3,11},{4,12},{5,13},{6,14},{7,15},{8,0},{9,1},... | collective-permute-start | bytes 221192 | tf_op jit(solution)/shard_map/ppermute | solution.py:305
  64.1 39.9 %collective-permute-start.27 = (bf16[2,2,256,512]{3,2,1,0:T(8,128)(2,1)S(1)}, bf16[2,2,256,512]{3,2,1,0:T(8,128)(2,1)S(1)}, u32[]{:S(2)}, u32[]{:S(2)}) collective-permute-start(bf16[2,2,256,512]{3,2,1,0:T(8,128)(2,1)S(1)} %get-tuple-element.46.refs_4_), channel_id=1, source_target_pairs={{0,1},{1,0},{2,3},{3,2},{4,5},{5,4},{6,7},{7,6},{8,9},{9,8},{10,11... | collective-permute-start | bytes 3145736 | tf_op jit(solution)/shard_map/ppermute | solution.py:305
  67.0 6.7 %collective-permute-start.7 = (bf16[72,512]{1,0:T(8,128)(2,1)S(1)}, bf16[72,512]{1,0:T(8,128)(2,1)S(1)}, u32[]{:S(2)}, u32[]{:S(2)}) collective-permute-start(bf16[72,512]{1,0:T(8,128)(2,1)S(1)} %shard_map.129.refs_0_.refs_9_), channel_id=1, source_target_pairs={{0,16},{1,17},{2,18},{3,19},{4,20},{5,21},{6,22},{7,23},{8,24},{9,... | collective-permute-start | bytes 221192 | tf_op jit(solution)/shard_map/ppermute | solution.py:305
  73.7 6.2 %collective-permute-start.8 = (bf16[72,512]{1,0:T(8,128)(2,1)S(1)}, bf16[72,512]{1,0:T(8,128)(2,1)S(1)}, u32[]{:S(2)}, u32[]{:S(2)}) collective-permute-start(bf16[72,512]{1,0:T(8,128)(2,1)S(1)} %shard_map.129.refs_0_.refs_9_), channel_id=1, source_target_pairs={{0,24},{1,25},{2,26},{3,27},{4,28},{5,29},{6,30},{7,31},{8,16},{9,... | collective-permute-start | bytes 221192 | tf_op jit(solution)/shard_map/ppermute | solution.py:305
  77.0 2.9 %collective-permute-start.12 = (bf16[2,1,256,512]{3,2,1,0:T(8,128)(2,1)S(1)}, bf16[2,1,256,512]{3,2,1,0:T(8,128)(2,1)S(1)}, u32[]{:S(2)}, u32[]{:S(2)}) collective-permute-start(bf16[2,1,256,512]{3,2,1,0:T(8,128)(2,1)S(1)} %collective-permute-done.10.refs_5_), channel_id=1, source_target_pairs={{0,1},{1,0},{2,3},{3,2},{4,5},{5,4},{6,7},{7,6},{8,9},{9,8},{10,11... | collective-permute-start | bytes 1572872 | tf_op jit(solution)/shard_map/ppermute | solution.py:305
  77.0 33.7 %collective-permute-start.28 = (bf16[2,2,256,512]{3,2,1,0:T(8,128)(2,1)S(1)}, bf16[2,2,256,512]{3,2,1,0:T(8,128)(2,1)S(1)}, u32[]{:S(2)}, u32[]{:S(2)}) collective-permute-start(bf16[2,2,256,512]{3,2,1,0:T(8,128)(2,1)S(1)} %collective-permute-done.26.refs_5_), channel_id=1, source_target_pairs={{0,1},{1,0},{2,3},{3,2},{4,5},{5,4},{6,7},{7,6},{8,9},{9,8},{10,11... | collective-permute-start | bytes 3145736 | tf_op jit(solution)/shard_map/ppermute | solution.py:305
  79.8 20.4 %collective-permute-start.49 = (bf16[2,3,128,512]{3,2,1,0:T(8,128)(2,1)S(1)}, bf16[2,3,128,512]{3,2,1,0:T(8,128)(2,1)S(1)}, u32[]{:S(2)}, u32[]{:S(2)}) collective-permute-start(bf16[2,3,128,512]{3,2,1,0:T(8,128)(2,1)S(1)} %pad_maximum_fusion.refs_4_), channel_id=1, source_target_pairs={{0,4},{1,3},{2,6},{3,1},{4,0},{5,7},{6,2},{7,5},{8,12},{9,11},{10,... | collective-permute-start | bytes 2359304 | tf_op jit(solution)/shard_map/ppermute | solution.py:305
  79.8 2.0 %collective-permute-start.20 = (bf16[1,64,2048]{2,1,0:T(8,128)(2,1)S(1)}, bf16[1,64,2048]{2,1,0:T(8,128)(2,1)S(1)}, u32[]{:S(2)}, u32[]{:S(2)}) collective-permute-start(bf16[1,64,2048]{2,1,0:T(8,128)(2,1)S(1)} %collective-permute-done.19.refs_7_), channel_id=1, source_target_pairs={{0,1},{1,0},{2,3},{3,2},{4,5},{5,4},{6,7},{7,6},{8,9},{9,8},{10,11... | collective-permute-start | bytes 786440 | tf_op jit(solution)/shard_map/ppermute | solution.py:305
  79.9 20.4 %collective-permute-start.34 = (bf16[1,64,2048]{2,1,0:T(8,128)(2,1)S(1)}, bf16[1,64,2048]{2,1,0:T(8,128)(2,1)S(1)}, u32[]{:S(2)}, u32[]{:S(2)}) collective-permute-start(bf16[1,64,2048]{2,1,0:T(8,128)(2,1)S(1)} %collective-permute-done.32.refs_5_), channel_id=1, source_target_pairs={{0,2},{1,3},{2,0},{3,1},{4,6},{5,7},{6,4},{7,5},{8,10},{9,11},{10,... | collective-permute-start | bytes 786440 | tf_op jit(solution)/shard_map/ppermute | solution.py:305
  81.8 4.4 %collective-permute-start.14 = (bf16[72,512]{1,0:T(8,128)(2,1)S(1)}, bf16[72,512]{1,0:T(8,128)(2,1)S(1)}, u32[]{:S(2)}, u32[]{:S(2)}) collective-permute-start(bf16[72,512]{1,0:T(8,128)(2,1)S(1)} %shard_map.132.refs_0_), channel_id=1, source_target_pairs={{0,8},{1,9},{2,10},{3,11},{4,12},{5,13},{6,14},{7,15},{8,0},{9,1},... | collective-permute-start | bytes 221192 | tf_op jit(solution)/shard_map/ppermute | solution.py:305
  86.2 6.0 %collective-permute-start.15 = (bf16[72,512]{1,0:T(8,128)(2,1)S(1)}, bf16[72,512]{1,0:T(8,128)(2,1)S(1)}, u32[]{:S(2)}, u32[]{:S(2)}) collective-permute-start(bf16[72,512]{1,0:T(8,128)(2,1)S(1)} %shard_map.132.refs_0_), channel_id=1, source_target_pairs={{0,16},{1,17},{2,18},{3,19},{4,20},{5,21},{6,22},{7,23},{8,24},{9,... | collective-permute-start | bytes 221192 | tf_op jit(solution)/shard_map/ppermute | solution.py:305
  92.3 6.2 %collective-permute-start.16 = (bf16[72,512]{1,0:T(8,128)(2,1)S(1)}, bf16[72,512]{1,0:T(8,128)(2,1)S(1)}, u32[]{:S(2)}, u32[]{:S(2)}) collective-permute-start(bf16[72,512]{1,0:T(8,128)(2,1)S(1)} %shard_map.132.refs_0_), channel_id=1, source_target_pairs={{0,24},{1,25},{2,26},{3,27},{4,28},{5,29},{6,30},{7,31},{8,16},{9,... | collective-permute-start | bytes 221192 | tf_op jit(solution)/shard_map/ppermute | solution.py:305
  99.2 10.9 %collective-permute-start.21 = (bf16[1,2,72,512]{3,2,1,0:T(8,128)(2,1)S(1)}, bf16[1,2,72,512]{3,2,1,0:T(8,128)(2,1)S(1)}, u32[]{:S(2)}, u32[]{:S(2)}) collective-permute-start(bf16[1,2,72,512]{3,2,1,0:T(8,128)(2,1)S(1)} %bitcast.5), channel_id=1, source_target_pairs={{0,2},{1,5},{2,0},{3,7},{4,6},{5,1},{6,4},{7,3},{8,10},{9,13},{10,... | collective-permute-start | bytes 442376 | tf_op jit(solution)/shard_map/ppermute | solution.py:305
  100.3 4.7 %collective-permute-start.23 = (bf16[72,512]{1,0:T(8,128)(2,1)S(1)}, bf16[72,512]{1,0:T(8,128)(2,1)S(1)}, u32[]{:S(2)}, u32[]{:S(2)}) collective-permute-start(bf16[72,512]{1,0:T(8,128)(2,1)S(1)} %get-tuple-element.45.refs_0_), channel_id=1, source_target_pairs={{0,8},{1,9},{2,10},{3,11},{4,12},{5,13},{6,14},{7,15},{8,0},{9,1},... | collective-permute-start | bytes 221192 | tf_op jit(solution)/shard_map/ppermute | solution.py:305
  100.3 8.1 %collective-permute-start.24 = (bf16[72,512]{1,0:T(8,128)(2,1)S(1)}, bf16[72,512]{1,0:T(8,128)(2,1)S(1)}, u32[]{:S(2)}, u32[]{:S(2)}) collective-permute-start(bf16[72,512]{1,0:T(8,128)(2,1)S(1)} %get-tuple-element.45.refs_0_), channel_id=1, source_target_pairs={{0,16},{1,17},{2,18},{3,19},{4,20},{5,21},{6,22},{7,23},{8,24},{9,... | collective-permute-start | bytes 221192 | tf_op jit(solution)/shard_map/ppermute | solution.py:305
  104.0 6.2 %collective-permute-start.25 = (bf16[72,512]{1,0:T(8,128)(2,1)S(1)}, bf16[72,512]{1,0:T(8,128)(2,1)S(1)}, u32[]{:S(2)}, u32[]{:S(2)}) collective-permute-start(bf16[72,512]{1,0:T(8,128)(2,1)S(1)} %get-tuple-element.45.refs_0_), channel_id=1, source_target_pairs={{0,24},{1,25},{2,26},{3,27},{4,28},{5,29},{6,30},{7,31},{8,16},{9,... | collective-permute-start | bytes 221192 | tf_op jit(solution)/shard_map/ppermute | solution.py:305
  105.0 9.4 %collective-permute-start.33 = (bf16[1,64,2048]{2,1,0:T(8,128)(2,1)S(1)}, bf16[1,64,2048]{2,1,0:T(8,128)(2,1)S(1)}, u32[]{:S(2)}, u32[]{:S(2)}) collective-permute-start(bf16[1,64,2048]{2,1,0:T(8,128)(2,1)S(1)} %collective-permute-done.32.refs_5_), channel_id=1, source_target_pairs={{0,1},{1,0},{2,3},{3,2},{4,5},{5,4},{6,7},{7,6},{8,9},{9,8},{10,11... | collective-permute-start | bytes 786440 | tf_op jit(solution)/shard_map/ppermute | solution.py:305
  108.3 33.7 %collective-permute-start.50 = (bf16[2,3,128,512]{3,2,1,0:T(8,128)(2,1)S(1)}, bf16[2,3,128,512]{3,2,1,0:T(8,128)(2,1)S(1)}, u32[]{:S(2)}, u32[]{:S(2)}) collective-permute-start(bf16[2,3,128,512]{3,2,1,0:T(8,128)(2,1)S(1)} %pad_maximum_fusion.refs_4_), channel_id=1, source_target_pairs={{0,1},{1,0},{2,3},{3,2},{4,5},{5,4},{6,7},{7,6},{8,9},{9,8},{10,11... | collective-permute-start | bytes 2359304 | tf_op jit(solution)/shard_map/ppermute | solution.py:305
  110.1 4.3 %collective-permute-start.35 = (bf16[1,64,2048]{2,1,0:T(8,128)(2,1)S(1)}, bf16[1,64,2048]{2,1,0:T(8,128)(2,1)S(1)}, u32[]{:S(2)}, u32[]{:S(2)}) collective-permute-start(bf16[1,64,2048]{2,1,0:T(8,128)(2,1)S(1)} %collective-permute-done.34.refs_7_), channel_id=1, source_target_pairs={{0,1},{1,0},{2,3},{3,2},{4,5},{5,4},{6,7},{7,6},{8,9},{9,8},{10,11... | collective-permute-start | bytes 786440 | tf_op jit(solution)/shard_map/ppermute | solution.py:305
  110.1 31.9 %collective-permute-start.51 = (bf16[2,3,128,512]{3,2,1,0:T(8,128)(2,1)S(1)}, bf16[2,3,128,512]{3,2,1,0:T(8,128)(2,1)S(1)}, u32[]{:S(2)}, u32[]{:S(2)}) collective-permute-start(bf16[2,3,128,512]{3,2,1,0:T(8,128)(2,1)S(1)} %collective-permute-done.49.refs_5_), channel_id=1, source_target_pairs={{0,1},{1,0},{2,3},{3,2},{4,5},{5,4},{6,7},{7,6},{8,9},{9,8},{10,11... | collective-permute-start | bytes 2359304 | tf_op jit(solution)/shard_map/ppermute | solution.py:305
  110.7 16.2 %collective-permute-start.22 = (bf16[2,2,72,512]{3,2,1,0:T(8,128)(2,1)S(1)}, bf16[2,2,72,512]{3,2,1,0:T(8,128)(2,1)S(1)}, u32[]{:S(2)}, u32[]{:S(2)}) collective-permute-start(bf16[2,2,72,512]{3,2,1,0:T(8,128)(2,1)S(1)} %pad_maximum_fusion.1.refs_0_), channel_id=1, source_target_pairs={{0,4},{1,3},{2,6},{3,1},{4,0},{5,7},{6,2},{7,5},{8,12},{9,11},{10,... | collective-permute-start | bytes 884744 | tf_op jit(solution)/shard_map/ppermute | solution.py:305
  114.4 4.4 %collective-permute-start.29 = (bf16[72,512]{1,0:T(8,128)(2,1)S(1)}, bf16[72,512]{1,0:T(8,128)(2,1)S(1)}, u32[]{:S(2)}, u32[]{:S(2)}) collective-permute-start(bf16[72,512]{1,0:T(8,128)(2,1)S(1)} %shard_map.135.refs_0_), channel_id=1, source_target_pairs={{0,8},{1,9},{2,10},{3,11},{4,12},{5,13},{6,14},{7,15},{8,0},{9,1},... | collective-permute-start | bytes 221192 | tf_op jit(solution)/shard_map/ppermute | solution.py:305
  114.5 7.8 %collective-permute-start.30 = (bf16[72,512]{1,0:T(8,128)(2,1)S(1)}, bf16[72,512]{1,0:T(8,128)(2,1)S(1)}, u32[]{:S(2)}, u32[]{:S(2)}) collective-permute-start(bf16[72,512]{1,0:T(8,128)(2,1)S(1)} %shard_map.135.refs_0_), channel_id=1, source_target_pairs={{0,16},{1,17},{2,18},{3,19},{4,20},{5,21},{6,22},{7,23},{8,24},{9,... | collective-permute-start | bytes 221192 | tf_op jit(solution)/shard_map/ppermute | solution.py:305
  118.8 6.2 %collective-permute-start.31 = (bf16[72,512]{1,0:T(8,128)(2,1)S(1)}, bf16[72,512]{1,0:T(8,128)(2,1)S(1)}, u32[]{:S(2)}, u32[]{:S(2)}) collective-permute-start(bf16[72,512]{1,0:T(8,128)(2,1)S(1)} %shard_map.135.refs_0_), channel_id=1, source_target_pairs={{0,24},{1,25},{2,26},{3,27},{4,28},{5,29},{6,30},{7,31},{8,16},{9,... | collective-permute-start | bytes 221192 | tf_op jit(solution)/shard_map/ppermute | solution.py:305
  125.7 4.3 %collective-permute-start.36 = (bf16[1,1,64,512]{3,2,1,0:T(8,128)(2,1)S(1)}, bf16[1,1,64,512]{3,2,1,0:T(8,128)(2,1)S(1)}, u32[]{:S(2)}, u32[]{:S(2)}) collective-permute-start(bf16[1,1,64,512]{3,2,1,0:T(8,128)(2,1)S(1)} %bitcast.7), channel_id=1, source_target_pairs={{0,2},{1,5},{2,0},{3,7},{4,6},{5,1},{6,4},{7,3},{8,10},{9,13},{10,... | collective-permute-start | bytes 196616 | tf_op jit(solution)/shard_map/ppermute | solution.py:305
  126.8 5.0 %collective-permute-start.40 = (bf16[2,2,72,512]{3,2,1,0:T(8,128)(2,1)S(1)}, bf16[2,2,72,512]{3,2,1,0:T(8,128)(2,1)S(1)}, u32[]{:S(2)}, u32[]{:S(2)}) collective-permute-start(bf16[2,2,72,512]{3,2,1,0:T(8,128)(2,1)S(1)} %pad_maximum_fusion.1.refs_0_), channel_id=1, source_target_pairs={{0,1},{1,0},{2,3},{3,2},{4,5},{5,4},{6,7},{7,6},{8,9},{9,8},{10,11... | collective-permute-start | bytes 884744 | tf_op jit(solution)/shard_map/ppermute | solution.py:305
  126.8 8.3 %collective-permute-start.41 = (bf16[2,2,72,512]{3,2,1,0:T(8,128)(2,1)S(1)}, bf16[2,2,72,512]{3,2,1,0:T(8,128)(2,1)S(1)}, u32[]{:S(2)}, u32[]{:S(2)}) collective-permute-start(bf16[2,2,72,512]{3,2,1,0:T(8,128)(2,1)S(1)} %collective-permute-done.22.refs_1_), channel_id=1, source_target_pairs={{0,1},{1,0},{2,3},{3,2},{4,5},{5,4},{6,7},{7,6},{8,9},{9,8},{10,11... | collective-permute-start | bytes 884744 | tf_op jit(solution)/shard_map/ppermute | solution.py:305
  130.1 5.0 %collective-permute-start.37 = (bf16[2,1,64,512]{3,2,1,0:T(8,128)(2,1)S(1)}, bf16[2,1,64,512]{3,2,1,0:T(8,128)(2,1)S(1)}, u32[]{:S(2)}, u32[]{:S(2)}) collective-permute-start(bf16[2,1,64,512]{3,2,1,0:T(8,128)(2,1)S(1)} %pad_maximum_fusion.2.refs_2_.refs_0_), channel_id=1, source_target_pairs={{0,4},{1,3},{2,6},{3,1},{4,0},{5,7},{6,2},{7,5},{8,12},{9,11},{10,... | collective-permute-start | bytes 393224 | tf_op jit(solution)/shard_map/ppermute | solution.py:305
  131.9 3.2 %collective-permute-start.38 = (bf16[2,1,64,512]{3,2,1,0:T(8,128)(2,1)S(1)}, bf16[2,1,64,512]{3,2,1,0:T(8,128)(2,1)S(1)}, u32[]{:S(2)}, u32[]{:S(2)}) collective-permute-start(bf16[2,1,64,512]{3,2,1,0:T(8,128)(2,1)S(1)} %pad_maximum_fusion.2.refs_2_.refs_0_), channel_id=1, source_target_pairs={{0,1},{1,0},{2,3},{3,2},{4,5},{5,4},{6,7},{7,6},{8,9},{9,8},{10,11... | collective-permute-start | bytes 393224 | tf_op jit(solution)/shard_map/ppermute | solution.py:305
  135.1 2.3 %collective-permute-start.39 = (bf16[2,1,64,512]{3,2,1,0:T(8,128)(2,1)S(1)}, bf16[2,1,64,512]{3,2,1,0:T(8,128)(2,1)S(1)}, u32[]{:S(2)}, u32[]{:S(2)}) collective-permute-start(bf16[2,1,64,512]{3,2,1,0:T(8,128)(2,1)S(1)} %collective-permute-done.37.refs_3_.refs_1_), channel_id=1, source_target_pairs={{0,1},{1,0},{2,3},{3,2},{4,5},{5,4},{6,7},{7,6},{8,9},{9,8},{10,11... | collective-permute-start | bytes 393224 | tf_op jit(solution)/shard_map/ppermute | solution.py:305
  135.1 9.2 %collective-permute-start.45 = (bf16[72,512]{1,0:T(8,128)(2,1)S(1)}, bf16[72,512]{1,0:T(8,128)(2,1)S(1)}, u32[]{:S(2)}, u32[]{:S(2)}) collective-permute-start(bf16[72,512]{1,0:T(8,128)(2,1)S(1)} %get-tuple-element.57.refs_0_), channel_id=1, source_target_pairs={{0,8},{1,9},{2,10},{3,11},{4,12},{5,13},{6,14},{7,15},{8,0},{9,1},... | collective-permute-start | bytes 221192 | tf_op jit(solution)/shard_map/ppermute | solution.py:305
  135.1 12.4 %collective-permute-start.46 = (bf16[72,512]{1,0:T(8,128)(2,1)S(1)}, bf16[72,512]{1,0:T(8,128)(2,1)S(1)}, u32[]{:S(2)}, u32[]{:S(2)}) collective-permute-start(bf16[72,512]{1,0:T(8,128)(2,1)S(1)} %get-tuple-element.57.refs_0_), channel_id=1, source_target_pairs={{0,16},{1,17},{2,18},{3,19},{4,20},{5,21},{6,22},{7,23},{8,24},{9,... | collective-permute-start | bytes 221192 | tf_op jit(solution)/shard_map/ppermute | solution.py:305
  137.4 10.1 %collective-permute-start.47 = (bf16[72,512]{1,0:T(8,128)(2,1)S(1)}, bf16[72,512]{1,0:T(8,128)(2,1)S(1)}, u32[]{:S(2)}, u32[]{:S(2)}) collective-permute-start(bf16[72,512]{1,0:T(8,128)(2,1)S(1)} %get-tuple-element.57.refs_0_), channel_id=1, source_target_pairs={{0,24},{1,25},{2,26},{3,27},{4,28},{5,29},{6,30},{7,31},{8,16},{9,... | collective-permute-start | bytes 221192 | tf_op jit(solution)/shard_map/ppermute | solution.py:305
  142.0 10.1 %collective-permute-start.42 = (bf16[72,512]{1,0:T(8,128)(2,1)S(1)}, bf16[72,512]{1,0:T(8,128)(2,1)S(1)}, u32[]{:S(2)}, u32[]{:S(2)}) collective-permute-start(bf16[72,512]{1,0:T(8,128)(2,1)S(1)} %get-tuple-element.54), channel_id=1, source_target_pairs={{0,8},{1,9},{2,10},{3,11},{4,12},{5,13},{6,14},{7,15},{8,0},{9,1},... | collective-permute-start | bytes 221192 | tf_op jit(solution)/shard_map/ppermute | solution.py:305
  142.1 10.0 %collective-permute-start.43 = (bf16[72,512]{1,0:T(8,128)(2,1)S(1)}, bf16[72,512]{1,0:T(8,128)(2,1)S(1)}, u32[]{:S(2)}, u32[]{:S(2)}) collective-permute-start(bf16[72,512]{1,0:T(8,128)(2,1)S(1)} %get-tuple-element.55), channel_id=1, source_target_pairs={{0,16},{1,17},{2,18},{3,19},{4,20},{5,21},{6,22},{7,23},{8,24},{9,... | collective-permute-start | bytes 221192 | tf_op jit(solution)/shard_map/ppermute | solution.py:305
  144.3 7.7 %collective-permute-start.44 = (bf16[72,512]{1,0:T(8,128)(2,1)S(1)}, bf16[72,512]{1,0:T(8,128)(2,1)S(1)}, u32[]{:S(2)}, u32[]{:S(2)}) collective-permute-start(bf16[72,512]{1,0:T(8,128)(2,1)S(1)} %get-tuple-element.56), channel_id=1, source_target_pairs={{0,24},{1,25},{2,26},{3,27},{4,28},{5,29},{6,30},{7,31},{8,16},{9,... | collective-permute-start | bytes 221192 | tf_op jit(solution)/shard_map/ppermute | solution.py:305
  146.9 5.1 %copy-start.2 = (bf16[128,128]{1,0:T(8,128)(2,1)S(1)}, bf16[128,128]{1,0:T(8,128)(2,1)}, u32[]{:S(2)}) copy-start(bf16[128,128]{1,0:T(8,128)(2,1)} %refs_6_.1) | copy-start | bytes 98308
  147.0 5.1 %copy-start.3 = (f32[128]{0:T(128)S(1)}, f32[128]{0:T(128)}, u32[]{:S(2)}) copy-start(f32[128]{0:T(128)} %refs_7_.1) | copy-start | bytes 1540
  148.0 4.0 %collective-permute-start.52 = (f32[72,128]{1,0:T(8,128)S(1)}, f32[72,128]{1,0:T(8,128)S(1)}, u32[]{:S(2)}, u32[]{:S(2)}) collective-permute-start(f32[72,128]{1,0:T(8,128)S(1)} %get-tuple-element.59), channel_id=1, source_target_pairs={{0,4},{1,5},{2,6},{3,7},{4,0},{5,1},{6,2},{7,3},{8,12},{9,13},{10,... | collective-permute-start | bytes 110600 | tf_op jit(solution)/shard_map/ppermute | solution.py:305
